TPU v7x, 32 devices: a whole 2x2x4 slice. The times are simulated.
32 devices in a mesh: dp: 8 (over z, y), tensor: 4 (over x, core).
Axes of the slice: x: 2, y: 2, z: 4, core: 2. Of those that a mesh axis runs over, the one named last changes fastest.
Arguments:
- inputs: float32 [4096, 2048], P(('dp', 'tensor')), may hold values from -12 to 12
- grad_output: float32 [4096, 2048], P(('dp', 'tensor')), may hold values from -12 to 12
- seg_ids: int32 [4096], P('dp'), may hold values from 0 to 4, as said below
- positions: int32 [4096], P('dp'), may hold values from 0 to 319, as said below
- norm1_gain: float32 [2048], replicated, may hold values from 0.5 to 1.5
- norm1_bias: float32 [2048], replicated, may hold values from -1.75 to 1.75
- query_weight: float32 [2048, 2048], P('dp', 'tensor'), may hold values from -0.125 to 0.125
- query_bias: float32 [2048], P('tensor'), may hold values from -1.75 to 1.75
- key_weight: float32 [2048, 2048], P('dp', 'tensor'), may hold values from -0.125 to 0.125
- value_weight: float32 [2048, 2048], P('dp', 'tensor'), may hold values from -0.125 to 0.125
- value_bias: float32 [2048], P('tensor'), may hold values from -1.75 to 1.75
- out_weight: float32 [2048, 2048], P('tensor', 'dp'), may hold values from -0.5 to 0.5
- out_bias: float32 [2048], replicated, may hold values from -1.75 to 1.75
- norm2_gain: float32 [2048], replicated, may hold values from 0.5 to 1.5
- norm2_bias: float32 [2048], replicated, may hold values from -1.75 to 1.75
- up_weight: float32 [2048, 8192], P('dp', 'tensor'), may hold values from -0.125 to 0.125
- up_bias: float32 [8192], P('tensor'), may hold values from -1.75 to 1.75
- down_weight: float32 [8192, 2048], P('tensor', 'dp'), may hold values from -0.0625 to 0.0625
- down_bias: float32 [2048], replicated, may hold values from -1.75 to 1.75
Outputs:
- layer_output: float32 [4096, 2048], P(('dp', 'tensor'))
- grad_inputs: float32 [4096, 2048], P(('dp', 'tensor'))
- grad_norm1_gain: float32 [2048], replicated
- grad_norm1_bias: float32 [2048], replicated
- grad_query_weight: float32 [2048, 2048], P('dp', 'tensor')
- grad_query_bias: float32 [2048], P('tensor')
- grad_key_weight: float32 [2048, 2048], P('dp', 'tensor')
- grad_value_weight: float32 [2048, 2048], P('dp', 'tensor')
- grad_value_bias: float32 [2048], P('tensor')
- grad_out_weight: float32 [2048, 2048], P('tensor', 'dp')
- grad_out_bias: float32 [2048], replicated
- grad_norm2_gain: float32 [2048], replicated
- grad_norm2_bias: float32 [2048], replicated
- grad_up_weight: float32 [2048, 8192], P('dp', 'tensor')
- grad_up_bias: float32 [8192], P('tensor')
- grad_down_weight: float32 [8192, 2048], P('tensor', 'dp')
- grad_down_bias: float32 [2048], replicated
Inputs may be any that keep to these rules, and one draw needn't show every extreme that they name: `seg_ids`: each group of 512 consecutive tokens holds one prompt (segment 0, positions 0 to 255) and 4 continuations (segments 1 to 4, positions 256 to 319 each); the tokens stand in blocks of 64 consecutive positions of one segment, the blocks of a group in an order drawn from the seed. `positions`: positions as stated for seg_ids; within a block they rise by one from token to token.
All inputs are finite; a program needn't handle non-finite values.
Results may differ from a plain program's by a relative error of at most 0.012.
Values may be sent and summed in bfloat16 or wider, within the bound.
A program may use at most 192 MiB of HBM per device.

v0:
```python
import jax
import jax.numpy as jnp
from jax import lax
from jax.sharding import PartitionSpec as P

HEAD_DIM = 128
GROUP = 512


EPSILON = 1e-05
NEGATIVE = -1e30


def normalize(values, gain, shift):
    mean_row = jnp.mean(values, axis=1, keepdims=True)
    centred = values - mean_row
    inverse = lax.rsqrt(jnp.mean(centred * centred, axis=1, keepdims=True) + EPSILON)
    unit_rows = centred * inverse
    return (unit_rows * gain + shift, unit_rows, inverse)


def normalize_back(grad_rows, unit_rows, inverse, gain):
    scaled = grad_rows * gain
    grad_in = inverse * (
        scaled
        - jnp.mean(scaled, axis=1, keepdims=True)
        - unit_rows * jnp.mean(scaled * unit_rows, axis=1, keepdims=True)
    )
    return (grad_in, jnp.sum(grad_rows * unit_rows, axis=0), jnp.sum(grad_rows, axis=0))


def gelu_slope(pre_act):
    cumulative = 0.5 * (1.0 + lax.erf(pre_act * 0.7071067811865476))
    density = jnp.exp(-0.5 * pre_act * pre_act) * 0.3989422804014327
    return cumulative + pre_act * density


def allowed_mask(seg_rows, pos_rows, seg_cols, pos_cols):
    return (pos_cols[None, :] <= pos_rows[:, None]) & (
        (seg_cols[None, :] == seg_rows[:, None]) | (seg_cols[None, :] == 0)
    )


def span_scores(query_span, key_heads, seg_span, pos_span, segment, places):
    scale_factor = HEAD_DIM ** (-0.5)
    scores = (
        jnp.einsum("qhd,khd->hqk", query_span, key_heads, preferred_element_type=jnp.float32)
        * scale_factor
    )
    return jnp.where(allowed_mask(seg_span, pos_span, segment, places)[None], scores, NEGATIVE)


def attend_group(pieces):
    queries, keys, values, segment, places = pieces
    row_count = queries.shape[0]
    span = min(512, row_count)
    head_count = queries.shape[1] // HEAD_DIM
    query_heads = queries.reshape(row_count, head_count, HEAD_DIM)
    key_heads = keys.reshape(row_count, head_count, HEAD_DIM)
    value_heads = values.reshape(row_count, head_count, HEAD_DIM)

    def one_span(offset):
        scores = span_scores(query_heads, key_heads, segment, places, segment, places)
        row_max = jnp.max(scores, axis=2, keepdims=True)
        exp_terms = jnp.exp(scores - row_max)
        exp_total = jnp.sum(exp_terms, axis=2, keepdims=True)
        attn_probs = (exp_terms / exp_total).astype(jnp.bfloat16)
        mixed = jnp.einsum(
            "hqk,khd->qhd", attn_probs, value_heads, preferred_element_type=jnp.float32
        )
        return (
            mixed.astype(jnp.bfloat16).reshape(span, -1),
            (row_max + jnp.log(exp_total))[:, :, 0],
        )

    offsets = jnp.arange(row_count // span, dtype=jnp.int32) * span
    mixed_spans, log_totals = lax.map(one_span, offsets)
    return (mixed_spans.reshape(row_count, -1), log_totals)


def attend_back(pieces):
    queries, keys, values, grad_att, segment, places, log_totals = pieces
    row_count = queries.shape[0]
    span = min(512, row_count)
    head_count = queries.shape[1] // HEAD_DIM
    scale_factor = HEAD_DIM ** (-0.5)
    query_heads = queries.reshape(row_count, head_count, HEAD_DIM)
    key_heads = keys.reshape(row_count, head_count, HEAD_DIM)
    value_heads = values.reshape(row_count, head_count, HEAD_DIM)
    grad_heads = grad_att.reshape(row_count, head_count, HEAD_DIM)

    def one_span(carry, number):
        key_total, value_total = carry
        scores = span_scores(query_heads, key_heads, segment, places, segment, places)
        attn_probs = jnp.exp(scores - log_totals[number][:, :, None])
        grad_probs = jnp.einsum(
            "qhd,khd->hqk", grad_heads, value_heads, preferred_element_type=jnp.float32
        )
        row_delta = jnp.sum(attn_probs * grad_probs, axis=2, keepdims=True)
        grad_scores = (attn_probs * (grad_probs - row_delta)).astype(jnp.bfloat16)
        grad_query = (
            jnp.einsum("hqk,khd->qhd", grad_scores, key_heads, preferred_element_type=jnp.float32)
            * scale_factor
        )
        key_total = (
            key_total
            + jnp.einsum(
                "hqk,qhd->khd", grad_scores, query_heads, preferred_element_type=jnp.float32
            )
            * scale_factor
        )
        value_total = value_total + jnp.einsum(
            "hqk,qhd->khd",
            attn_probs.astype(jnp.bfloat16),
            grad_heads,
            preferred_element_type=jnp.float32,
        )
        return ((key_total, value_total), grad_query.astype(jnp.bfloat16).reshape(span, -1))

    empty = jnp.zeros((row_count, head_count, HEAD_DIM), jnp.float32)
    (key_total, value_total), grad_spans = lax.scan(
        one_span, (empty, empty), jnp.arange(row_count // span, dtype=jnp.int32)
    )
    return (
        grad_spans.reshape(row_count, -1),
        key_total.astype(jnp.bfloat16).reshape(row_count, -1),
        value_total.astype(jnp.bfloat16).reshape(row_count, -1),
    )


def local(
    inputs,
    grad_output,
    seg_ids,
    positions,
    norm1_gain,
    norm1_bias,
    query_weight,
    query_bias,
    key_weight,
    value_weight,
    value_bias,
    out_weight,
    out_bias,
    norm2_gain,
    norm2_bias,
    up_weight,
    up_bias,
    down_weight,
    down_bias,
):
    low_type = jnp.bfloat16
    group_total = seg_ids.shape[0] // GROUP
    q_full, k_full, v_full, o_full, up_full, down_full = (
        lax.all_gather(query_weight.astype(low_type), "dp", axis=0, tiled=True),
        lax.all_gather(key_weight.astype(low_type), "dp", axis=0, tiled=True),
        lax.all_gather(value_weight.astype(low_type), "dp", axis=0, tiled=True),
        lax.all_gather(out_weight.astype(low_type), "dp", axis=1, tiled=True),
        lax.all_gather(up_weight.astype(low_type), "dp", axis=0, tiled=True),
        lax.all_gather(down_weight.astype(low_type), "dp", axis=1, tiled=True),
    )
    normed1, unit1, inverse1 = normalize(inputs, norm1_gain, norm1_bias)
    whole1 = lax.all_gather(normed1.astype(low_type), "tensor", axis=0, tiled=True)
    queries = (jnp.dot(whole1, q_full, preferred_element_type=jnp.float32) + query_bias).astype(
        low_type
    )
    keys = jnp.dot(whole1, k_full, preferred_element_type=jnp.float32).astype(low_type)
    values = (jnp.dot(whole1, v_full, preferred_element_type=jnp.float32) + value_bias).astype(
        low_type
    )
    seg_groups = seg_ids.reshape(group_total, GROUP)
    pos_groups = positions.reshape(group_total, GROUP)
    attended, log_totals = lax.map(
        attend_group,
        (
            queries.reshape(group_total, GROUP, -1),
            keys.reshape(group_total, GROUP, -1),
            values.reshape(group_total, GROUP, -1),
            seg_groups,
            pos_groups,
        ),
    )
    attended = attended.reshape(whole1.shape[0], -1)
    projected = jnp.dot(attended, o_full, preferred_element_type=jnp.float32)
    resid = (
        inputs + lax.psum_scatter(projected, "tensor", scatter_dimension=0, tiled=True) + out_bias
    )
    normed2, unit2, inverse2 = normalize(resid, norm2_gain, norm2_bias)
    whole2 = lax.all_gather(normed2.astype(low_type), "tensor", axis=0, tiled=True)
    pre_act = jnp.dot(whole2, up_full, preferred_element_type=jnp.float32) + up_bias
    activated = jax.nn.gelu(pre_act, approximate=False).astype(low_type)
    lowered = jnp.dot(activated, down_full, preferred_element_type=jnp.float32)
    layer_output = (
        resid
        + lax.psum_scatter(
            lowered.astype(jnp.bfloat16), "tensor", scatter_dimension=0, tiled=True
        ).astype(jnp.float32)
        + down_bias
    )
    grad_whole = lax.all_gather(grad_output.astype(low_type), "tensor", axis=0, tiled=True)
    grad_down = jnp.einsum("tf,td->fd", activated, grad_whole, preferred_element_type=jnp.float32)
    grad_act = jnp.einsum("td,fd->tf", grad_whole, down_full, preferred_element_type=jnp.float32)
    grad_pre = (grad_act * gelu_slope(pre_act)).astype(low_type)
    grad_up = jnp.einsum("td,tf->df", whole2, grad_pre, preferred_element_type=jnp.float32)
    grad_up_part = jnp.sum(grad_pre.astype(jnp.float32), axis=0)
    grad_normed2 = lax.psum_scatter(
        jnp.einsum("tf,df->td", grad_pre, up_full, preferred_element_type=jnp.float32),
        "tensor",
        scatter_dimension=0,
        tiled=True,
    )
    back2, gain2_part, bias2_part = normalize_back(grad_normed2, unit2, inverse2, norm2_gain)
    grad_resid = grad_output + back2
    grad_mixed = lax.all_gather(grad_resid.astype(low_type), "tensor", axis=0, tiled=True)
    grad_out_w = jnp.einsum("te,td->ed", attended, grad_mixed, preferred_element_type=jnp.float32)
    grad_att = jnp.einsum(
        "td,ed->te", grad_mixed, o_full, preferred_element_type=jnp.float32
    ).astype(low_type)
    grad_queries, grad_keys, grad_values = lax.map(
        attend_back,
        (
            queries.reshape(group_total, GROUP, -1),
            keys.reshape(group_total, GROUP, -1),
            values.reshape(group_total, GROUP, -1),
            grad_att.reshape(group_total, GROUP, -1),
            seg_groups,
            pos_groups,
            log_totals,
        ),
    )
    grad_queries = grad_queries.reshape(whole1.shape[0], -1)
    grad_keys = grad_keys.reshape(whole1.shape[0], -1)
    grad_values = grad_values.reshape(whole1.shape[0], -1)
    grad_query_w = jnp.einsum("td,te->de", whole1, grad_queries, preferred_element_type=jnp.float32)
    grad_key_w = jnp.einsum("td,te->de", whole1, grad_keys, preferred_element_type=jnp.float32)
    grad_value_w = jnp.einsum("td,te->de", whole1, grad_values, preferred_element_type=jnp.float32)
    grad_whole1 = (
        jnp.einsum("te,de->td", grad_queries, q_full, preferred_element_type=jnp.float32)
        + jnp.einsum("te,de->td", grad_keys, k_full, preferred_element_type=jnp.float32)
        + jnp.einsum("te,de->td", grad_values, v_full, preferred_element_type=jnp.float32)
    )
    grad_normed1 = lax.psum_scatter(grad_whole1, "tensor", scatter_dimension=0, tiled=True)
    back1, gain1_part, bias1_part = normalize_back(grad_normed1, unit1, inverse1, norm1_gain)
    grad_inputs = grad_resid + back1
    tensor_index = lax.axis_index("tensor")
    model_width = inputs.shape[1]
    hidden_total = up_bias.shape[0] * lax.axis_size("tensor")
    head_width = query_bias.shape[0]
    hidden_width = up_bias.shape[0]
    query_part = jnp.sum(grad_queries.astype(jnp.float32), axis=0)
    value_part = jnp.sum(grad_values.astype(jnp.float32), axis=0)
    query_spread = lax.dynamic_update_slice(
        jnp.zeros((model_width,), jnp.float32), query_part, (tensor_index * head_width,)
    )
    value_spread = lax.dynamic_update_slice(
        jnp.zeros((model_width,), jnp.float32), value_part, (tensor_index * head_width,)
    )
    up_spread = lax.dynamic_update_slice(
        jnp.zeros((hidden_total,), jnp.float32), grad_up_part, (tensor_index * hidden_width,)
    )
    (
        sum_gain1,
        sum_bias1,
        sum_gain2,
        sum_bias2,
        sum_out_bias,
        sum_down_bias,
        sum_query,
        sum_value,
        sum_up,
    ) = lax.psum(
        (
            gain1_part,
            bias1_part,
            gain2_part,
            bias2_part,
            jnp.sum(grad_resid, axis=0),
            jnp.sum(grad_output, axis=0),
            query_spread,
            value_spread,
            up_spread,
        ),
        ("dp", "tensor"),
    )
    grad_query_b = lax.dynamic_slice_in_dim(sum_query, tensor_index * head_width, head_width, 0)
    grad_value_b = lax.dynamic_slice_in_dim(sum_value, tensor_index * head_width, head_width, 0)
    grad_up_b = lax.dynamic_slice_in_dim(sum_up, tensor_index * hidden_width, hidden_width, 0)
    query_done, key_done, value_done, out_done, up_done, down_done = (
        lax.psum_scatter(grad_query_w, "dp", scatter_dimension=0, tiled=True),
        lax.psum_scatter(grad_key_w, "dp", scatter_dimension=0, tiled=True),
        lax.psum_scatter(grad_value_w, "dp", scatter_dimension=0, tiled=True),
        lax.psum_scatter(grad_out_w, "dp", scatter_dimension=1, tiled=True),
        lax.psum_scatter(grad_up, "dp", scatter_dimension=0, tiled=True),
        lax.psum_scatter(grad_down, "dp", scatter_dimension=1, tiled=True),
    )
    return (
        layer_output,
        grad_inputs,
        sum_gain1,
        sum_bias1,
        query_done,
        grad_query_b,
        key_done,
        value_done,
        grad_value_b,
        out_done,
        sum_out_bias,
        sum_gain2,
        sum_bias2,
        up_done,
        grad_up_b,
        down_done,
        sum_down_bias,
    )


def solution(mesh):
    placed = (
        P(("dp", "tensor"), None),
        P(("dp", "tensor"), None),
        P("dp"),
        P("dp"),
        P(),
        P(),
        P("dp", "tensor"),
        P("tensor"),
        P("dp", "tensor"),
        P("dp", "tensor"),
        P("tensor"),
        P("tensor", "dp"),
        P(),
        P(),
        P(),
        P("dp", "tensor"),
        P("tensor"),
        P("tensor", "dp"),
        P(),
    )
    return jax.shard_map(
        local,
        mesh=mesh,
        in_specs=placed,
        out_specs=(
            P(("dp", "tensor"), None),
            P(("dp", "tensor"), None),
            P(),
            P(),
            P("dp", "tensor"),
            P("tensor"),
            P("dp", "tensor"),
            P("dp", "tensor"),
            P("tensor"),
            P("tensor", "dp"),
            P(),
            P(),
            P(),
            P("dp", "tensor"),
            P("tensor"),
            P("tensor", "dp"),
            P(),
        ),
        check_vma=False,
    )
```

profile of v0, /device:TPU:0, one launch (start us, length us, event | category | flops | bytes accessed | tf_op | source)
XLA Modules:
  0.0 1862.4 jit_solution(13621364097760568328)
XLA Ops:
  16.3 21.7 %all-gather.11.cloned.1.call-done = bf16[512,2048]{1,0:T(8,128)(2,1)} async-done(((bf16[128,2048]{1,0:T(8,128)(2,1)}), bf16[512,2048]{1,0:T(8,128)(2,1)}) %all-gather.11.cloned.1.call-update) | async-done | bytes 2097168 | tf_op jit(solution)/shard_map/all_gather | solution.py:163
  38.0 51.8 %all-gather.17.cloned.1.call-done = bf16[2048,512]{1,0:T(8,128)(2,1)} async-done(((bf16[256,512]{1,0:T(8,128)(2,1)}), bf16[2048,512]{1,0:T(8,128)(2,1)}) %all-gather.17.cloned.1.call-update) | async-done | bytes 2097168 | tf_op jit(solution)/shard_map/all_gather | solution.py:156
  93.4 46.8 %all-gather.15.cloned.1.call-done = bf16[2048,512]{1,0:T(8,128)(2,1)} async-done(((bf16[256,512]{1,0:T(8,128)(2,1)}), bf16[2048,512]{1,0:T(8,128)(2,1)}) %all-gather.15.cloned.1.call-update) | async-done | bytes 2097168 | tf_op jit(solution)/shard_map/all_gather | solution.py:155
  146.6 43.8 %all-gather.13.cloned.1.call-done = bf16[2048,512]{1,0:T(8,128)(2,1)} async-done(((bf16[256,512]{1,0:T(8,128)(2,1)}), bf16[2048,512]{1,0:T(8,128)(2,1)}) %all-gather.13.cloned.1.call-update) | async-done | bytes 2097168 | tf_op jit(solution)/shard_map/all_gather | solution.py:157
  194.5 47.3 %all-gather.19.cloned.1.call-done = bf16[512,2048]{1,0:T(8,128)(2,1)} async-done(((bf16[512,256]{1,0:T(8,128)(2,1)}), bf16[512,2048]{1,0:T(8,128)(2,1)}) %all-gather.19.cloned.1.call-update) | async-done | bytes 2097168 | tf_op jit(solution)/shard_map/all_gather | solution.py:158
  249.6 40.0 %reduce-scatter.11.cloned.1.call-done = f32[128,2048]{1,0:T(8,128)} async-done(((f32[512,2048]{1,0:T(8,128)}), f32[128,2048]{1,0:T(8,128)}) %reduce-scatter.11.cloned.1.call-update) | async-done | bytes 1048592 | tf_op jit(solution)/shard_map/reduce_scatter | solution.py:186
  299.3 117.5 %all-gather.23.cloned.1.call-done = bf16[2048,2048]{1,0:T(8,128)(2,1)} async-done(((bf16[256,2048]{1,0:T(8,128)(2,1)}), bf16[2048,2048]{1,0:T(8,128)(2,1)}) %all-gather.23.cloned.1.call-update) | async-done | bytes 8388624 | tf_op jit(solution)/shard_map/all_gather | solution.py:159
  416.8 22.9 %all-gather.21.cloned.1.call-done = bf16[512,2048]{1,0:T(8,128)(2,1)} async-done(((bf16[128,2048]{1,0:T(8,128)(2,1)}), bf16[512,2048]{1,0:T(8,128)(2,1)}) %all-gather.21.cloned.1.call-update) | async-done | bytes 2097168 | tf_op jit(solution)/shard_map/all_gather | solution.py:189
  439.7 17.7 fusion.2
  464.4 127.4 %all-gather.25.cloned.1.call-done = bf16[2048,2048]{1,0:T(8,128)(2,1)} async-done(((bf16[2048,256]{1,0:T(8,128)(2,1)}), bf16[2048,2048]{1,0:T(8,128)(2,1)}) %all-gather.25.cloned.1.call-update) | async-done | bytes 8388624 | tf_op jit(solution)/shard_map/all_gather | solution.py:160
  609.1 10.2 convolution_convert_fusion
  619.4 32.6 %reduce-scatter.15.cloned.1.call-done = f32[128,2048]{1,0:T(8,128)} async-done(((f32[512,2048]{1,0:T(8,128)}), f32[128,2048]{1,0:T(8,128)}) %reduce-scatter.15.cloned.1.call-update) | async-done | bytes 1048592 | tf_op jit(solution)/shard_map/reduce_scatter | solution.py:206
  654.6 31.6 %reduce-scatter.13.cloned.1.call-done = bf16[128,2048]{1,0:T(8,128)(2,1)} async-done(((bf16[512,2048]{1,0:T(8,128)(2,1)}), bf16[128,2048]{1,0:T(8,128)(2,1)}) %reduce-scatter.13.cloned.1.call-update) | async-done | bytes 524304 | tf_op jit(solution)/shard_map/reduce_scatter | solution.py:195
  700.3 14.5 all-gather.29.cloned.1.call-done
  730.5 44.1 %reduce-scatter.17.cloned.1.call-done = f32[128,2048]{1,0:T(8,128)} async-done(((f32[512,2048]{1,0:T(8,128)}), f32[128,2048]{1,0:T(8,128)}) %reduce-scatter.17.cloned.1.call-update) | async-done | bytes 1048592 | tf_op jit(solution)/shard_map/reduce_scatter | solution.py:242
  797.8 9.8 fusion.42
  809.2 9.8 fusion.43
  822.0 87.8 %all-reduce.3.cloned.1.call-done = (f32[2048]{0:T(1024)}, f32[2048]{0:T(1024)}, f32[2048]{0:T(1024)}, f32[2048]{0:T(1024)}, f32[2048]{0:T(1024)}, /*index=5*/f32...) async-done(((f32[2048]{0:T(1024)}, f32[2048]{0:T(1024)}, f32[2048]{0:T(1024)}, f32[2048]{0:T(1024)}, f32[2048]{0:T(1024)}, /*index=5*/f32[2048]{0:T(1024)}, ...) | async-done | bytes 98320 | tf_op jit(solution)/shard_map/psum | solution.py:271
  913.7 89.5 %reduce-scatter.23.cloned.1.call-done = f32[256,512]{1,0:T(8,128)} async-done(((f32[2048,512]{1,0:T(8,128)}), f32[256,512]{1,0:T(8,128)}) %reduce-scatter.23.cloned.1.call-update) | async-done | bytes 524304 | tf_op jit(solution)/shard_map/reduce_scatter | solution.py:291
  1003.2 92.0 %reduce-scatter.21.cloned.1.call-done = f32[256,512]{1,0:T(8,128)} async-done(((f32[2048,512]{1,0:T(8,128)}), f32[256,512]{1,0:T(8,128)}) %reduce-scatter.21.cloned.1.call-update) | async-done | bytes 524304 | tf_op jit(solution)/shard_map/reduce_scatter | solution.py:290
  1095.2 92.0 %reduce-scatter.19.cloned.1.call-done = f32[256,512]{1,0:T(8,128)} async-done(((f32[2048,512]{1,0:T(8,128)}), f32[256,512]{1,0:T(8,128)}) %reduce-scatter.19.cloned.1.call-update) | async-done | bytes 524304 | tf_op jit(solution)/shard_map/reduce_scatter | solution.py:289
  1187.2 92.6 %reduce-scatter.25.cloned.1.call-done = f32[512,256]{1,0:T(8,128)} async-done(((f32[512,2048]{1,0:T(8,128)}), f32[512,256]{1,0:T(8,128)}) %reduce-scatter.25.cloned.1.call-update) | async-done | bytes 524304 | tf_op jit(solution)/shard_map/reduce_scatter | solution.py:292
  1279.8 284.1 %reduce-scatter.27.cloned.1.call-done = f32[256,2048]{1,0:T(8,128)} async-done(((f32[2048,2048]{1,0:T(8,128)}), f32[256,2048]{1,0:T(8,128)}) %reduce-scatter.27.cloned.1.call-update) | async-done | bytes 2097168 | tf_op jit(solution)/shard_map/reduce_scatter | solution.py:293
  1563.9 283.7 %reduce-scatter.29.cloned.1.call-done = f32[2048,256]{1,0:T(8,128)} async-done(((f32[2048,2048]{1,0:T(8,128)}), f32[2048,256]{1,0:T(8,128)}) %reduce-scatter.29.cloned.1.call-update) | async-done | bytes 2097168 | tf_op jit(solution)/shard_map/reduce_scatter | solution.py:294
  (196 shorter events, 136.1 us)
Async XLA Ops:
  7.3 30.8 %all-gather.11.cloned.1.call-start = ((), (), s32[]{:S(2)}) async-start(), calls=%async_computation.10 | async-start | bytes 2621440 | tf_op jit(solution)/shard_map/all_gather | solution.py:163
  12.6 77.3 %all-gather.17.cloned.1.call-start = ((), (), s32[]{:S(2)}) async-start(), calls=%async_computation.13 | async-start | bytes 2359296 | tf_op jit(solution)/shard_map/all_gather | solution.py:156
  13.4 126.8 %all-gather.15.cloned.1.call-start = ((), (), s32[]{:S(2)}) async-start(), calls=%async_computation.12 | async-start | bytes 2359296 | tf_op jit(solution)/shard_map/all_gather | solution.py:155
  14.2 176.2 %all-gather.13.cloned.1.call-start = ((), (), s32[]{:S(2)}) async-start(), calls=%async_computation.11 | async-start | bytes 2359296 | tf_op jit(solution)/shard_map/all_gather | solution.py:157
  15.1 226.7 %all-gather.19.cloned.1.call-start = ((), (), s32[]{:S(2)}) async-start(), calls=%async_computation.14 | async-start | bytes 2359296 | tf_op jit(solution)/shard_map/all_gather | solution.py:158
  15.9 273.7 %reduce-scatter.11.cloned.1.call-start = ((), (), s32[]{:S(2)}) async-start(), calls=%async_computation.15 | async-start | bytes 5242880 | tf_op jit(solution)/shard_map/reduce_scatter | solution.py:186
  16.3 123.9 %copy-start.41 = (f32[512]{0:T(512)S(1)}, f32[512]{0:T(512)}, u32[]{:S(2)}) copy-start(f32[512]{0:T(512)} %param.26) | copy-start | bytes 6148
  38.0 102.2 %copy-start.4 = (bf16[512,2048]{1,0:T(8,128)(2,1)S(1)}, bf16[512,2048]{1,0:T(8,128)(2,1)}, u32[]{:S(2)}) copy-start(bf16[512,2048]{1,0:T(8,128)(2,1)} %all-gather.11.cloned.1.call-done) | copy-start | bytes 6291460
  246.7 170.1 %all-gather.23.cloned.1.call-start = ((), (), s32[]{:S(2)}) async-start(), calls=%async_computation.17 | async-start | bytes 9437184 | tf_op jit(solution)/shard_map/all_gather | solution.py:159
  249.6 190.1 %all-gather.21.cloned.1.call-start = ((), (), s32[]{:S(2)}) async-start(), calls=%async_computation.16 | async-start | bytes 2621440 | tf_op jit(solution)/shard_map/all_gather | solution.py:189
  292.0 147.7 %copy-start.40 = (f32[2048]{0:T(1024)S(1)}, f32[2048]{0:T(1024)}, u32[]{:S(2)}) copy-start(f32[2048]{0:T(1024)} %param.35) | copy-start | bytes 24580
  293.1 171.3 %all-gather.27.cloned.1.call-start = ((), (), s32[]{:S(2)}) async-start(), calls=%async_computation.20 | async-start | bytes 2621440 | tf_op jit(solution)/shard_map/all_gather | solution.py:200
  296.2 295.7 %all-gather.25.cloned.1.call-start = ((), (), s32[]{:S(2)}) async-start(), calls=%async_computation.18 | async-start | bytes 9437184 | tf_op jit(solution)/shard_map/all_gather | solution.py:160
  298.9 353.0 %reduce-scatter.15.cloned.1.call-start = ((), (), s32[]{:S(2)}) async-start(), calls=%async_computation.21 | async-start | bytes 5242880 | tf_op jit(solution)/shard_map/reduce_scatter | solution.py:206
  609.1 77.1 %reduce-scatter.13.cloned.1.call-start = ((), (), s32[]{:S(2)}) async-start(), calls=%async_computation.19 | async-start | bytes 2621440 | tf_op jit(solution)/shard_map/reduce_scatter | solution.py:195
  619.4 95.4 %all-gather.29.cloned.1.call-start = ((), (), s32[]{:S(2)}) async-start(), calls=%async_computation.22 | async-start | bytes 2621440 | tf_op jit(solution)/shard_map/all_gather | solution.py:214
  692.1 82.5 %reduce-scatter.17.cloned.1.call-start = ((), (), s32[]{:S(2)}) async-start(), calls=%async_computation.23 | async-start | bytes 5242880 | tf_op jit(solution)/shard_map/reduce_scatter | solution.py:242
  729.8 179.9 %all-reduce.3.cloned.1.call-start = ((), (), s32[]{:S(2)}) async-start(), calls=%async_computation.30 | async-start | bytes 196608 | tf_op jit(solution)/shard_map/psum | solution.py:271
  776.9 226.4 %reduce-scatter.23.cloned.1.call-start = ((), (), s32[]{:S(2)}) async-start(), calls=%async_computation.26 | async-start | bytes 4718592 | tf_op jit(solution)/shard_map/reduce_scatter | solution.py:291
  781.2 314.0 %reduce-scatter.21.cloned.1.call-start = ((), (), s32[]{:S(2)}) async-start(), calls=%async_computation.25 | async-start | bytes 4718592 | tf_op jit(solution)/shard_map/reduce_scatter | solution.py:290
  785.9 401.4 %reduce-scatter.19.cloned.1.call-start = ((), (), s32[]{:S(2)}) async-start(), calls=%async_computation.24 | async-start | bytes 4718592 | tf_op jit(solution)/shard_map/reduce_scatter | solution.py:289
  790.4 489.4 %reduce-scatter.25.cloned.1.call-start = ((), (), s32[]{:S(2)}) async-start(), calls=%async_computation.27 | async-start | bytes 4718592 | tf_op jit(solution)/shard_map/reduce_scatter | solution.py:292
  796.2 767.7 %reduce-scatter.27.cloned.1.call-start = ((), (), s32[]{:S(2)}) async-start(), calls=%async_computation.28 | async-start | bytes 18874368 | tf_op jit(solution)/shard_map/reduce_scatter | solution.py:293
  807.6 1040.0 %reduce-scatter.29.cloned.1.call-start = ((), (), s32[]{:S(2)}) async-start(), calls=%async_computation.29 | async-start | bytes 18874368 | tf_op jit(solution)/shard_map/reduce_scatter | solution.py:294
  (41 other events, 676.4 us)
Sparse Core Ops, SparseCore 0:
  12.7 25.2 all-gather.10
  40.7 49.0 all-gather.16
  92.6 47.6 all-gather.14
  142.8 47.6 all-gather.12
  192.9 48.8 all-gather.18
  246.8 42.7 reduce-scatter.10
  292.3 124.4 all-gather.22
  418.9 20.7 all-gather.20
  441.8 22.5 all-gather.26
  466.9 124.9 all-gather.24
  609.2 42.7 reduce-scatter.14
  654.9 31.1 reduce-scatter.12
  692.2 22.5 all-gather.28
  729.9 44.5 reduce-scatter.16
  782.6 127.1 all-reduce.2
  913.8 89.3 reduce-scatter.22
  1007.3 87.9 reduce-scatter.20
  1099.3 87.8 reduce-scatter.18
  1191.4 88.3 reduce-scatter.24
  1284.0 279.8 reduce-scatter.26
  1568.3 279.2 reduce-scatter.28
where the time goes:
time: 1870 us; the launch traced here: 1860 us
  waiting for transfers between devices  1670 us (89%)
  matrix products  110 us (6%)
  other arithmetic  32.7 us (2%)
  local copies, waits for them, and re-layouts  24.3 us (1%)
    reduce_scatter x1, waiting for transfers between devices, local(): lax.psum_scatter(grad_up, 'dp', scatter_dimension=0, tiled=True)  284 us
    reduce_scatter x1, waiting for transfers between devices, local(): lax.psum_scatter(grad_down, 'dp', scatter_dimension=1, tiled=True)  284 us
    all_gather x1, waiting for transfers between devices, local(): lax.all_gather(down_weight.astype(low_type), 'dp', axis=1, tiled=True)  127 us
    all_gather x1, waiting for transfers between devices, local(): lax.all_gather(up_weight.astype(low_type), 'dp', axis=0, tiled=True)  118 us
    reduce_scatter x1, waiting for transfers between devices, local(): lax.psum_scatter(grad_out_w, 'dp', scatter_dimension=1, tiled=True)  92.6 us
    reduce_scatter x1, waiting for transfers between devices, local(): lax.psum_scatter(grad_key_w, 'dp', scatter_dimension=0, tiled=True)  92 us
    reduce_scatter x1, waiting for transfers between devices, local(): lax.psum_scatter(grad_query_w, 'dp', scatter_dimension=0, tiled=True)  92 us
    reduce_scatter x1, waiting for transfers between devices, local(): lax.psum_scatter(grad_value_w, 'dp', scatter_dimension=0, tiled=True)  89.5 us
  transfers between devices with their start and end apart: 21, of which 21 were waited for; matrix products, arithmetic and copies ran while one was open for 5% of the time, Pallas kernels for 0%

commit v1 on v0

v1 whole, which is shorter than its diff:
```python
import jax
import jax.numpy as jnp
from jax import lax
from jax.sharding import PartitionSpec as P

HEAD_DIM = 128
GROUP = 512
EPSILON = 1e-05
NEGATIVE = -1e30
LOW = jnp.bfloat16
F32 = jnp.float32


def normalize(values, gain, shift):
    mean_row = jnp.mean(values, axis=1, keepdims=True)
    centred = values - mean_row
    inverse = lax.rsqrt(jnp.mean(centred * centred, axis=1, keepdims=True) + EPSILON)
    unit_rows = centred * inverse
    return (unit_rows * gain + shift, unit_rows, inverse)


def normalize_back(grad_rows, unit_rows, inverse, gain):
    scaled = grad_rows * gain
    grad_in = inverse * (
        scaled
        - jnp.mean(scaled, axis=1, keepdims=True)
        - unit_rows * jnp.mean(scaled * unit_rows, axis=1, keepdims=True)
    )
    return (grad_in, jnp.sum(grad_rows * unit_rows, axis=0), jnp.sum(grad_rows, axis=0))


def gelu_parts(pre_act):
    cumulative = 0.5 * (1.0 + lax.erf(pre_act * 0.7071067811865476))
    density = jnp.exp(-0.5 * pre_act * pre_act) * 0.3989422804014327
    return cumulative, cumulative + pre_act * density


def heads_of(rows):
    return rows.reshape(-1, GROUP, rows.shape[1] // HEAD_DIM, HEAD_DIM)


def scores_of(query_heads, key_heads, segment, places):
    scores = jnp.einsum(
        "gqhd,gkhd->ghqk", query_heads, key_heads, preferred_element_type=F32
    ) * (HEAD_DIM**-0.5)
    allowed = (places[:, None, :] <= places[:, :, None]) & (
        (segment[:, None, :] == segment[:, :, None]) | (segment[:, None, :] == 0)
    )
    return jnp.where(allowed[:, None], scores, NEGATIVE)


def attend(queries, keys, values, segment, places):
    scores = scores_of(heads_of(queries), heads_of(keys), segment, places)
    row_max = jnp.max(scores, axis=3, keepdims=True)
    exp_terms = jnp.exp(scores - row_max)
    exp_total = jnp.sum(exp_terms, axis=3, keepdims=True)
    probs = (exp_terms / exp_total).astype(LOW)
    mixed = jnp.einsum("ghqk,gkhd->gqhd", probs, heads_of(values), preferred_element_type=F32)
    return mixed.astype(LOW).reshape(queries.shape), row_max + jnp.log(exp_total)


def attend_back(queries, keys, values, grad_att, segment, places, log_totals):
    scale_factor = HEAD_DIM**-0.5
    query_heads, key_heads, value_heads, grad_heads = map(heads_of, (queries, keys, values, grad_att))
    probs = jnp.exp(scores_of(query_heads, key_heads, segment, places) - log_totals)
    grad_probs = jnp.einsum("gqhd,gkhd->ghqk", grad_heads, value_heads, preferred_element_type=F32)
    row_delta = jnp.sum(probs * grad_probs, axis=3, keepdims=True)
    grad_scores = (probs * (grad_probs - row_delta)).astype(LOW)
    grad_query = jnp.einsum("ghqk,gkhd->gqhd", grad_scores, key_heads, preferred_element_type=F32)
    grad_key = jnp.einsum("ghqk,gqhd->gkhd", grad_scores, query_heads, preferred_element_type=F32)
    grad_value = jnp.einsum(
        "ghqk,gqhd->gkhd", probs.astype(LOW), grad_heads, preferred_element_type=F32
    )
    return (
        (grad_query * scale_factor).astype(LOW).reshape(queries.shape),
        (grad_key * scale_factor).astype(LOW).reshape(queries.shape),
        grad_value.astype(LOW).reshape(queries.shape),
    )


def local(
    inputs,
    grad_output,
    seg_ids,
    positions,
    norm1_gain,
    norm1_bias,
    query_weight,
    query_bias,
    key_weight,
    value_weight,
    value_bias,
    out_weight,
    out_bias,
    norm2_gain,
    norm2_bias,
    up_weight,
    up_bias,
    down_weight,
    down_bias,
):
    dp_total = lax.axis_size("dp")
    half_total = dp_total // 2
    tensor_total = lax.axis_size("tensor")
    place = lax.axis_index("dp")
    lane, line = place & 1, place >> 1
    side = line & 1

    def hop(rows, mask):
        return lax.ppermute(rows, "dp", [(i, i ^ mask) for i in range(dp_total)])

    def hop_tensor(rows, mask):
        return lax.ppermute(rows, "tensor", [(i, i ^ mask) for i in range(tensor_total)])

    def own_half(array, axis):
        size = array.shape[axis] // 2
        return lax.dynamic_slice_in_dim(array, side * size, size, axis)

    def gather_weight(weight, axis):
        size = weight.shape[1 - axis] // 2
        low = weight.astype(LOW)
        mine = lax.dynamic_slice_in_dim(low, side * size, size, 1 - axis)
        other = lax.dynamic_slice_in_dim(low, (1 - side) * size, size, 1 - axis)
        along = [mine] + [hop(other if k & 1 else mine, 2 * k) for k in range(1, half_total)]
        across = [hop(mine, 1)] + [hop(block, 1) for block in along[1:]]
        shape = list(mine.shape)
        width = shape[axis]
        shape[axis] *= dp_total
        whole = jnp.zeros(tuple(shape), LOW)
        for k in range(half_total):
            for step, block in ((0, along[k]), (1, across[k])):
                start = [0, 0]
                start[axis] = (place ^ (2 * k + step)) * width
                whole = lax.dynamic_update_slice(whole, block, tuple(start))
        return whole

    def block_at(array, axis, index, width):
        return lax.dynamic_slice_in_dim(array, index * width, width, axis)

    def scatter_grad(partial, axis):
        width = partial.shape[axis] // dp_total
        send = jnp.concatenate(
            [block_at(partial, axis, 2 * k + 1 - lane, width) for k in range(half_total)], axis
        )
        got = hop(send, 1)

        def summed(index):
            return block_at(partial, axis, 2 * index + lane, width).astype(F32) + block_at(
                got, axis, index, width
            ).astype(F32)

        sums = [summed(line), None]
        for k in range(1, half_total):
            came = hop(summed(line ^ k).astype(LOW), 2 * k).astype(F32)
            sums[k & 1] = came if sums[k & 1] is None else sums[k & 1] + came
        first = jnp.where(side == 0, sums[0], sums[1])
        second = jnp.where(side == 0, sums[1], sums[0])
        return jnp.concatenate([first, second], 1 - axis)

    def gather_tokens(rows):
        pair = jnp.stack([rows, hop(rows, 2)])
        whole = lax.all_gather(pair, "tensor", axis=1, tiled=True)
        return whole.reshape(-1, rows.shape[1])

    def scatter_tokens(partial):
        pair = partial.astype(LOW).reshape(2, -1, partial.shape[1])
        mine = lax.psum_scatter(pair, "tensor", scatter_dimension=1, tiled=True)
        return mine[0].astype(F32) + hop(mine[1], 2).astype(F32)

    def mm(left, right):
        return jnp.dot(left, right, preferred_element_type=F32)

    def mm_nt(left, right):
        return jnp.einsum("td,fd->tf", left, right, preferred_element_type=F32)

    def mm_tn(left, right):
        return jnp.einsum("ta,tb->ab", left, right, preferred_element_type=F32)

    segment = jnp.stack([seg_ids, hop(seg_ids, 2)]).reshape(-1, GROUP)
    places = jnp.stack([positions, hop(positions, 2)]).reshape(-1, GROUP)

    normed1, unit1, inverse1 = normalize(inputs, norm1_gain, norm1_bias)
    whole1 = gather_tokens(normed1.astype(LOW))
    q_full = gather_weight(query_weight, 0)
    k_full = gather_weight(key_weight, 0)
    v_full = gather_weight(value_weight, 0)
    queries = (mm(whole1, q_full) + own_half(query_bias, 0)).astype(LOW)
    keys = mm(whole1, k_full).astype(LOW)
    values = (mm(whole1, v_full) + own_half(value_bias, 0)).astype(LOW)
    attended, log_totals = attend(queries, keys, values, segment, places)
    o_full = gather_weight(out_weight, 1)
    resid = inputs + scatter_tokens(mm(attended, o_full)) + out_bias
    normed2, unit2, inverse2 = normalize(resid, norm2_gain, norm2_bias)
    whole2 = gather_tokens(normed2.astype(LOW))
    up_full = gather_weight(up_weight, 0)
    pre_act = mm(whole2, up_full) + own_half(up_bias, 0)
    cumulative, slope = gelu_parts(pre_act)
    activated = (pre_act * cumulative).astype(LOW)
    grad_whole = gather_tokens(grad_output.astype(LOW))
    down_full = gather_weight(down_weight, 1)
    grad_down = scatter_grad(mm_tn(activated, grad_whole).astype(LOW), 1)
    layer_output = resid + scatter_tokens(mm(activated, down_full)) + down_bias
    grad_pre = (mm_nt(grad_whole, down_full) * slope).astype(LOW)
    grad_up_part = jnp.sum(grad_pre.astype(F32), axis=0)
    grad_up = scatter_grad(mm_tn(whole2, grad_pre).astype(LOW), 0)
    grad_normed2 = scatter_tokens(mm_nt(grad_pre, up_full))
    back2, gain2_part, bias2_part = normalize_back(grad_normed2, unit2, inverse2, norm2_gain)
    grad_resid = grad_output + back2
    grad_mixed = gather_tokens(grad_resid.astype(LOW))
    grad_out_w = scatter_grad(mm_tn(attended, grad_mixed).astype(LOW), 1)
    grad_att = mm_nt(grad_mixed, o_full).astype(LOW)
    grad_queries, grad_keys, grad_values = attend_back(
        queries, keys, values, grad_att, segment, places, log_totals
    )
    grad_value_w = scatter_grad(mm_tn(whole1, grad_values).astype(LOW), 0)
    grad_key_w = scatter_grad(mm_tn(whole1, grad_keys).astype(LOW), 0)
    grad_query_w = scatter_grad(mm_tn(whole1, grad_queries).astype(LOW), 0)
    grad_normed1 = scatter_tokens(
        mm_nt(grad_queries, q_full) + mm_nt(grad_keys, k_full) + mm_nt(grad_values, v_full)
    )
    back1, gain1_part, bias1_part = normalize_back(grad_normed1, unit1, inverse1, norm1_gain)
    grad_inputs = grad_resid + back1

    def sum_dp(vector):
        mask = 1
        while mask < dp_total:
            vector = vector + hop(vector, mask)
            mask *= 2
        return vector

    def sum_all(vector):
        vector = sum_dp(vector)
        mask = 1
        while mask < tensor_total:
            vector = vector + hop_tensor(vector, mask)
            mask *= 2
        return vector

    def spread(half):
        empty = jnp.zeros_like(half)
        return jnp.where(
            side == 0, jnp.concatenate([half, empty]), jnp.concatenate([empty, half])
        )

    width = inputs.shape[1]
    early = sum_all(
        jnp.stack(
            [
                jnp.sum(grad_output, axis=0),
                gain2_part,
                bias2_part,
                jnp.sum(grad_resid, axis=0),
            ]
        )
    )
    late = sum_all(jnp.stack([gain1_part, bias1_part]))
    up_sum = sum_dp(spread(grad_up_part))
    query_sum = sum_dp(spread(jnp.sum(grad_queries.astype(F32), axis=0)))
    value_sum = sum_dp(spread(jnp.sum(grad_values.astype(F32), axis=0)))
    return (
        layer_output,
        grad_inputs,
        late[0],
        late[1],
        grad_query_w,
        query_sum,
        grad_key_w,
        grad_value_w,
        value_sum,
        grad_out_w,
        early[3],
        early[1],
        early[2],
        grad_up,
        up_sum,
        grad_down,
        early[0],
    )


def solution(mesh):
    tokens, weight, weight_t = P(("dp", "tensor"), None), P("dp", "tensor"), P("tensor", "dp")
    whole, part = P(), P("tensor")
    return jax.shard_map(
        local,
        mesh=mesh,
        in_specs=(
            tokens, tokens, P("dp"), P("dp"), whole, whole, weight, part, weight, weight, part,
            weight_t, whole, whole, whole, weight, part, weight_t, whole,
        ),
        out_specs=(
            tokens, tokens, whole, whole, weight, part, weight, weight, part, weight_t, whole,
            whole, whole, weight, part, weight_t, whole,
        ),
        check_vma=False,
    )
```

time: 1870 us -> 840 us (0.45)
  waiting for transfers between devices: 1670 us -> 445 us
  starting transfers between devices: 9.52 us -> 155 us
  local copies, waits for them, and re-layouts: 24.3 us -> 65.2 us
  other arithmetic: 32.7 us -> 53.2 us
    reduce_scatter x10 -> x4, waiting for transfers between devices: 1080 us -> 127 us  [scatter_tokens(): mine = lax.psum_scatter(pair, 'tensor', scatter_dimension=1, tiled=True)]
    all_gather x10 -> x4, waiting for transfers between devices: 501 us -> 12.7 us  [gather_tokens(): whole = lax.all_gather(pair, 'tensor', axis=1, tiled=True)]
    ppermute x0 -> x95, waiting for transfers between devices: none -> 305 us  [the longest x91 301 us: hop(): return lax.ppermute(rows, 'dp', [(i, i ^ mask) for i in range(dp_total)])]
    ppermute x0 -> x95, starting transfers between devices: none -> 154 us  [the longest x91 152 us: hop(): return lax.ppermute(rows, 'dp', [(i, i ^ mask) for i in range(dp_total)])]
    psum x1 -> x0, waiting for transfers between devices: 87.8 us -> none  [local(): lax.psum((gain1_part, bias1_part, gain2_part, bias2_part, jnp.sum(grad_re...]
    dynamic_update_slice x3 -> x48, local copies, waits for them, and re-layouts: 0.57 us -> 29.3 us  [gather_weight(): whole = lax.dynamic_update_slice(whole, block, tuple(start))]
  transfers between devices with their start and end apart: 21 -> 103, of which waited for: 21 -> 47; matrix products, arithmetic and copies ran while one was open for 5% -> 18% of each run, Pallas kernels for 0% -> 0%
where the time goes in v1:
time: 840 us; the launch traced here: 830 us
  waiting for transfers between devices  445 us (53%)
  starting transfers between devices  155 us (18%)
  matrix products  95.9 us (11%)
  local copies, waits for them, and re-layouts  65.2 us (8%)
  other arithmetic  53.2 us (6%)
  between operations  15.9 us (2%)
    ppermute x91, waiting for transfers between devices, hop(): return lax.ppermute(rows, 'dp', [(i, i ^ mask) for i in range(dp_total)])  301 us
    ppermute x91, starting transfers between devices, hop(): return lax.ppermute(rows, 'dp', [(i, i ^ mask) for i in range(dp_total)])  152 us
    reduce_scatter x4, waiting for transfers between devices, scatter_tokens(): mine = lax.psum_scatter(pair, 'tensor', scatter_dimension=1, tiled=True)  127 us
    dot_general x6, matrix products, mm(): return jnp.dot(left, right, preferred_element_type=F32)  36.6 us
    dot_general x6, matrix products, mm_nt(): return jnp.einsum('td,fd->tf', left, right, preferred_element_type=F32)  30.1 us
    dynamic_update_slice x48, local copies, waits for them, and re-layouts, gather_weight(): whole = lax.dynamic_update_slice(whole, block, tuple(start))  29.3 us
    dot_general x6, matrix products, mm_tn(): return jnp.einsum('ta,tb->ab', left, right, preferred_element_type=F32)  18.2 us
  transfers between devices with their start and end apart: 103, of which 47 were waited for; matrix products, arithmetic and copies ran while one was open for 18% of the time, Pallas kernels for 0%

profile of v1, /device:TPU:0, one launch (start us, length us, event | category | flops | bytes accessed | tf_op | source)
XLA Modules:
  0.0 829.7 jit_solution(6120658701385712714)
XLA Ops:
  15.9 11.0 %collective-permute-done = bf16[128,2048]{1,0:T(8,128)(2,1)S(1)} collective-permute-done((bf16[128,2048]{1,0:T(8,128)(2,1)S(1)}, bf16[128,2048]{1,0:T(8,128)(2,1)S(1)}, u32[]{:S(2)}, u32[]{:S(2)}) %collective-permute-start) | collective-permute-done | bytes 524320 | tf_op jit(solution)/shard_map/ppermute | solution.py:110
  135.8 44.6 %reduce-scatter.5.cloned.1.call-done = bf16[2,128,2048]{2,1,0:T(8,128)(2,1)} async-done(((bf16[2,512,2048]{2,1,0:T(8,128)(2,1)}), bf16[2,128,2048]{2,1,0:T(8,128)(2,1)}) %reduce-scatter.5.cloned.1.call-update) | async-done | bytes 1048592 | tf_op jit(solution)/shard_map/reduce_scatter | solution.py:167
  183.1 12.0 %collective-permute-done.31 = bf16[128,2048]{1,0:T(8,128)(2,1)S(1)} collective-permute-done((bf16[128,2048]{1,0:T(8,128)(2,1)S(1)}, bf16[128,2048]{1,0:T(8,128)(2,1)S(1)}, u32[]{:S(2)}, u32[]{:S(2)}) %collective-permute-start.31) | collective-permute-done | bytes 524320 | tf_op jit(solution)/shard_map/ppermute | solution.py:110
  199.5 10.9 %collective-permute-done.32 = bf16[128,2048]{1,0:T(8,128)(2,1)S(1)} collective-permute-done((bf16[128,2048]{1,0:T(8,128)(2,1)S(1)}, bf16[128,2048]{1,0:T(8,128)(2,1)S(1)}, u32[]{:S(2)}, u32[]{:S(2)}) %collective-permute-start.32) | collective-permute-done | bytes 524320 | tf_op jit(solution)/shard_map/ppermute | solution.py:110
  213.1 10.3 %collective-permute-done.48 = bf16[128,2048]{1,0:T(8,128)(2,1)S(1)} collective-permute-done((bf16[128,2048]{1,0:T(8,128)(2,1)S(1)}, bf16[128,2048]{1,0:T(8,128)(2,1)S(1)}, u32[]{:S(2)}, u32[]{:S(2)}) %collective-permute-start.48) | collective-permute-done | bytes 524320 | tf_op jit(solution)/shard_map/ppermute | solution.py:110
  245.1 21.4 %collective-permute-done.43 = bf16[1024,256]{1,0:T(8,128)(2,1)S(1)} collective-permute-done((bf16[1024,256]{1,0:T(8,128)(2,1)S(1)}, bf16[1024,256]{1,0:T(8,128)(2,1)S(1)}, u32[]{:S(2)}, u32[]{:S(2)}) %collective-permute-start.43) | collective-permute-done | bytes 524320 | tf_op jit(solution)/shard_map/ppermute | solution.py:110
  281.2 30.3 %collective-permute-done.36 = bf16[256,1024]{1,0:T(8,128)(2,1)S(1)} collective-permute-done((bf16[256,1024]{1,0:T(8,128)(2,1)S(1)}, bf16[256,1024]{1,0:T(8,128)(2,1)S(1)}, u32[]{:S(2)}, u32[]{:S(2)}) %collective-permute-start.36) | collective-permute-done | bytes 524320 | tf_op jit(solution)/shard_map/ppermute | solution.py:110
  319.2 18.3 %collective-permute-done.37 = bf16[256,1024]{1,0:T(8,128)(2,1)S(1)} collective-permute-done((bf16[256,1024]{1,0:T(8,128)(2,1)S(1)}, bf16[256,1024]{1,0:T(8,128)(2,1)S(1)}, u32[]{:S(2)}, u32[]{:S(2)}) %collective-permute-start.37) | collective-permute-done | bytes 524320 | tf_op jit(solution)/shard_map/ppermute | solution.py:110
  346.4 10.9 %multiply_convert_fusion.1 = (bf16[1024,1024]{1,0:T(8,128)(2,1)}, f32[1024,1024]{1,0:T(8,128)}) fusion(f32[1024]{0:T(1024)S(1)} %dynamic_slice.273, bf16[1024,2048]{1,0:T(8,128)(2,1)} %bitcast.216, bf16[2048,1024]{1,0:T(8,128)(2,1)} %constant_dynamic-update-slice_fusion.8), kind=kOutput, calls=%fused_computation.12 | convolution fusion | flops 4301258752 | bytes 14684160 | tf_op jit(solution)/shard_map/dot_general | solution.py:171
  357.3 9.6 %convert_reduce_fusion = (f32[1024]{0:T(1024)S(1)}, bf16[1024,1024]{1,0:T(8,128)(2,1)S(1)}) fusion(f32[1024,1024]{1,0:T(8,128)} %get-tuple-element.113, f32[1024]{0:T(1024)S(1)} %dynamic_slice.273, bf16[1024,2048]{1,0:T(8,128)(2,1)} %bitcast.218, bf16[1024,2048]{1,0:T(8,128)(2,1)} %constant_dynamic-update-slice_fusion), kind=kOutput, calls=%fused_computation.8 | convolution fusion | flops 4308597760 | bytes 14688256 | tf_op jit(solution)/shard_map/td,fd->tf/dot_general | solution.py:174
  366.8 9.1 %convolution_convert_fusion.3 = bf16[1024,2048]{1,0:T(8,128)(2,1)} fusion(bf16[1024,1024]{1,0:T(8,128)(2,1)S(1)} %get-tuple-element.121, bf16[2048,1024]{1,0:T(8,128)(2,1)} %constant_dynamic-update-slice_fusion.8), kind=kOutput, calls=%fused_computation.20 | convolution fusion | flops 4297064448 | bytes 10485760 | tf_op jit(solution)/shard_map/td,fd->tf/dot_general | solution.py:174
  376.5 9.4 %convolution_convert_fusion.4 = bf16[1024,2048]{1,0:T(8,128)(2,1)} fusion(bf16[1024,1024]{1,0:T(8,128)(2,1)} %get-tuple-element.112, bf16[1024,2048]{1,0:T(8,128)(2,1)} %constant_dynamic-update-slice_fusion), kind=kOutput, calls=%fused_computation.21 | convolution fusion | flops 4297064448 | bytes 10485760 | tf_op jit(solution)/shard_map/dot_general | solution.py:171
  386.0 38.4 %reduce-scatter.9.cloned.1.call-done = bf16[2,128,2048]{2,1,0:T(8,128)(2,1)} async-done(((bf16[2,512,2048]{2,1,0:T(8,128)(2,1)}), bf16[2,128,2048]{2,1,0:T(8,128)(2,1)}) %reduce-scatter.9.cloned.1.call-update) | async-done | bytes 1048592 | tf_op jit(solution)/shard_map/reduce_scatter | solution.py:167
  427.8 43.6 %reduce-scatter.7.cloned.1.call-done = bf16[2,128,2048]{2,1,0:T(8,128)(2,1)} async-done(((bf16[2,512,2048]{2,1,0:T(8,128)(2,1)}), bf16[2,128,2048]{2,1,0:T(8,128)(2,1)}) %reduce-scatter.7.cloned.1.call-update) | async-done | bytes 1048592 | tf_op jit(solution)/shard_map/reduce_scatter | solution.py:167
  475.8 10.2 %collective-permute-done.47 = bf16[128,2048]{1,0:T(8,128)(2,1)S(1)} collective-permute-done((bf16[128,2048]{1,0:T(8,128)(2,1)S(1)}, bf16[128,2048]{1,0:T(8,128)(2,1)S(1)}, u32[]{:S(2)}, u32[]{:S(2)}) %collective-permute-start.47) | collective-permute-done | bytes 524320 | tf_op jit(solution)/shard_map/ppermute | solution.py:110
  491.0 11.1 %collective-permute-done.50 = bf16[128,2048]{1,0:T(8,128)(2,1)S(1)} collective-permute-done((bf16[128,2048]{1,0:T(8,128)(2,1)S(1)}, bf16[128,2048]{1,0:T(8,128)(2,1)S(1)}, u32[]{:S(2)}, u32[]{:S(2)}) %collective-permute-start.50) | collective-permute-done | bytes 524320 | tf_op jit(solution)/shard_map/ppermute | solution.py:110
  525.2 12.6 %all-gather.11.cloned.1.call-done = bf16[2,512,2048]{2,1,0:T(8,128)(2,1)} async-done(((bf16[2,128,2048]{2,1,0:T(8,128)(2,1)}), bf16[2,512,2048]{2,1,0:T(8,128)(2,1)}) %all-gather.11.cloned.1.call-update) | async-done | bytes 4194320 | tf_op jit(solution)/shard_map/all_gather | solution.py:162
  569.6 35.2 %collective-permute-done.88 = f32[2048]{0:T(1024)S(1)} collective-permute-done((f32[2048]{0:T(1024)S(1)}, f32[2048]{0:T(1024)S(1)}, u32[]{:S(2)}, u32[]{:S(2)}) %collective-permute-start.88) | collective-permute-done | bytes 8224 | tf_op jit(solution)/shard_map/ppermute | solution.py:110
  628.0 38.5 %collective-permute-done.92 = bf16[1024,256]{1,0:T(8,128)(2,1)S(1)} collective-permute-done((bf16[1024,256]{1,0:T(8,128)(2,1)S(1)}, bf16[1024,256]{1,0:T(8,128)(2,1)S(1)}, u32[]{:S(2)}, u32[]{:S(2)}) %collective-permute-start.92) | collective-permute-done | bytes 524320 | tf_op jit(solution)/shard_map/ppermute | solution.py:110
  666.5 17.3 %collective-permute-start.80 = (f32[4,2048]{1,0:T(4,128)S(1)}, f32[4,2048]{1,0:T(4,128)S(1)}, u32[]{:S(2)}, u32[]{:S(2)}) collective-permute-start(f32[4,2048]{1,0:T(4,128)S(1)} %fusion.76), channel_id=1, source_target_pairs={{0,8},{4,12},{8,0},{12,4},{16,24},{20,28},{24,16},{28,20},{1,9},{5... | collective-permute-start | bytes 98312 | tf_op jit(solution)/shard_map/ppermute | solution.py:110
  685.5 8.3 %collective-permute-done.80 = f32[4,2048]{1,0:T(4,128)S(1)} collective-permute-done((f32[4,2048]{1,0:T(4,128)S(1)}, f32[4,2048]{1,0:T(4,128)S(1)}, u32[]{:S(2)}, u32[]{:S(2)}) %collective-permute-start.80) | collective-permute-done | bytes 32800 | tf_op jit(solution)/shard_map/ppermute | solution.py:110
  697.3 8.8 %collective-permute-done.81 = f32[4,2048]{1,0:T(4,128)S(1)} collective-permute-done((f32[4,2048]{1,0:T(4,128)S(1)}, f32[4,2048]{1,0:T(4,128)S(1)}, u32[]{:S(2)}, u32[]{:S(2)}) %collective-permute-start.81) | collective-permute-done | bytes 32800 | tf_op jit(solution)/shard_map/ppermute | solution.py:110
  725.7 15.2 %collective-permute-done.61 = f32[512]{0:T(512)S(1)} collective-permute-done((f32[512]{0:T(512)S(1)}, f32[512]{0:T(512)S(1)}, u32[]{:S(2)}, u32[]{:S(2)}) %collective-permute-start.61) | collective-permute-done | bytes 2080 | tf_op jit(solution)/shard_map/ppermute | solution.py:110
  766.3 8.1 collective-permute-start.58
  (499 shorter events, 368.4 us)
Async XLA Ops:
  7.2 99.6 %all-gather.5.cloned.1.call-start = ((), (), s32[]{:S(2)}) async-start(), calls=%async_computation.4 | async-start | bytes 5242880 | tf_op jit(solution)/shard_map/all_gather | solution.py:162
  27.9 152.5 %reduce-scatter.5.cloned.1.call-start = ((), (), s32[]{:S(2)}) async-start(), calls=%async_computation.5 | async-start | bytes 5242880 | tf_op jit(solution)/shard_map/reduce_scatter | solution.py:167
  30.6 41.5 %collective-permute-start.20 = (bf16[256,256]{1,0:T(8,128)(2,1)}, bf16[256,256]{1,0:T(8,128)(2,1)}, u32[]{:S(2)}, u32[]{:S(2)}) collective-permute-start(bf16[256,256]{1,0:T(8,128)(2,1)} %get-tuple-element.36), channel_id=1, source_target_pairs={{0,16},{4,20},{8,24},{12,28},{16,0},{20,4},{24,8},{28,12},{1,17},{... | collective-permute-start | bytes 393224 | tf_op jit(solution)/shard_map/ppermute | solution.py:110
  33.2 55.9 %collective-permute-start.22 = (bf16[256,256]{1,0:T(8,128)(2,1)}, bf16[256,256]{1,0:T(8,128)(2,1)S(1)}, u32[]{:S(2)}, u32[]{:S(2)}) collective-permute-start(bf16[256,256]{1,0:T(8,128)(2,1)} %get-tuple-element.101), channel_id=1, source_target_pairs={{0,24},{4,28},{8,16},{12,20},{16,8},{20,12},{24,0},{28,4},{1,25},{... | collective-permute-start | bytes 393224 | tf_op jit(solution)/shard_map/ppermute | solution.py:110
  135.5 210.8 %all-gather.7.cloned.1.call-start = ((), (), s32[]{:S(2)}) async-start(), calls=%async_computation.6 | async-start | bytes 5242880 | tf_op jit(solution)/shard_map/all_gather | solution.py:162
  211.6 145.7 %all-gather.9.cloned.1.call-start = ((), (), s32[]{:S(2)}) async-start(), calls=%async_computation.8 | async-start | bytes 5242880 | tf_op jit(solution)/shard_map/all_gather | solution.py:162
  224.6 199.8 %reduce-scatter.9.cloned.1.call-start = ((), (), s32[]{:S(2)}) async-start(), calls=%async_computation.9 | async-start | bytes 5242880 | tf_op jit(solution)/shard_map/reduce_scatter | solution.py:167
  266.5 44.9 %collective-permute-start.36 = (bf16[256,1024]{1,0:T(8,128)(2,1)S(1)}, bf16[256,1024]{1,0:T(8,128)(2,1)S(1)}, u32[]{:S(2)}, u32[]{:S(2)}) collective-permute-start(bf16[256,1024]{1,0:T(8,128)(2,1)S(1)} %get-tuple-element.30), channel_id=1, source_target_pairs={{0,16},{4,20},{8,24},{12,28},{16,0},{20,4},{24,8},{28,12},{1,17},{... | collective-permute-start | bytes 1572872 | tf_op jit(solution)/shard_map/ppermute | solution.py:110
  266.5 45.4 %collective-permute-start.38 = (bf16[256,1024]{1,0:T(8,128)(2,1)S(1)}, bf16[256,1024]{1,0:T(8,128)(2,1)S(1)}, u32[]{:S(2)}, u32[]{:S(2)}) collective-permute-start(bf16[256,1024]{1,0:T(8,128)(2,1)S(1)} %get-tuple-element.99), channel_id=1, source_target_pairs={{0,24},{4,28},{8,16},{12,20},{16,8},{20,12},{24,0},{28,4},{1,25},{... | collective-permute-start | bytes 1572872 | tf_op jit(solution)/shard_map/ppermute | solution.py:110
  271.3 42.1 %collective-permute-start.42 = (bf16[1024,256]{1,0:T(8,128)(2,1)S(1)}, bf16[1024,256]{1,0:T(8,128)(2,1)S(1)}, u32[]{:S(2)}, u32[]{:S(2)}) collective-permute-start(bf16[1024,256]{1,0:T(8,128)(2,1)S(1)} %collective-permute-done.41), channel_id=1, source_target_pairs={{0,4},{4,0},{8,12},{12,8},{16,20},{20,16},{24,28},{28,24},{1,5},{5... | collective-permute-start | bytes 1572872 | tf_op jit(solution)/shard_map/ppermute | solution.py:110
  272.8 42.9 %collective-permute-start.44 = (bf16[1024,256]{1,0:T(8,128)(2,1)S(1)}, bf16[1024,256]{1,0:T(8,128)(2,1)S(1)}, u32[]{:S(2)}, u32[]{:S(2)}) collective-permute-start(bf16[1024,256]{1,0:T(8,128)(2,1)S(1)} %collective-permute-done.43), channel_id=1, source_target_pairs={{0,4},{4,0},{8,12},{12,8},{16,20},{20,16},{24,28},{28,24},{1,5},{5... | collective-permute-start | bytes 1572872 | tf_op jit(solution)/shard_map/ppermute | solution.py:110
  376.0 95.4 %reduce-scatter.7.cloned.1.call-start = ((), (), s32[]{:S(2)}) async-start(), calls=%async_computation.7 | async-start | bytes 5242880 | tf_op jit(solution)/shard_map/reduce_scatter | solution.py:167
  385.9 151.9 %all-gather.11.cloned.1.call-start = ((), (), s32[]{:S(2)}) async-start(), calls=%async_computation.10 | async-start | bytes 5242880 | tf_op jit(solution)/shard_map/all_gather | solution.py:162
  426.3 47.8 %collective-permute-start.49 = (bf16[128,2048]{1,0:T(8,128)(2,1)}, bf16[128,2048]{1,0:T(8,128)(2,1)S(1)}, u32[]{:S(2)}, u32[]{:S(2)}) collective-permute-start(bf16[128,2048]{1,0:T(8,128)(2,1)} %slice_bitcast_fusion.2), channel_id=1, source_target_pairs={{0,8},{4,12},{8,0},{12,4},{16,24},{20,28},{24,16},{28,20},{1,9},{5... | collective-permute-start | bytes 1572872 | tf_op jit(solution)/shard_map/ppermute | solution.py:110
  503.2 284.2 %reduce-scatter.11.cloned.1.call-start = ((), (), s32[]{:S(2)}) async-start(), calls=%async_computation.11 | async-start | bytes 5242880 | tf_op jit(solution)/shard_map/reduce_scatter | solution.py:167
  514.0 99.7 %collective-permute-start.91 = (bf16[1024,1024]{1,0:T(8,128)(2,1)}, bf16[1024,1024]{1,0:T(8,128)(2,1)}, u32[]{:S(2)}, u32[]{:S(2)}) collective-permute-start(bf16[1024,1024]{1,0:T(8,128)(2,1)} %pad_maximum_fusion.2), channel_id=1, source_target_pairs={{0,4},{4,0},{8,12},{12,8},{16,20},{20,16},{24,28},{28,24},{1,5},{5... | collective-permute-start | bytes 6291464 | tf_op jit(solution)/shard_map/ppermute | solution.py:110
  523.7 97.8 %collective-permute-start.84 = (bf16[1024,1024]{1,0:T(8,128)(2,1)}, bf16[1024,1024]{1,0:T(8,128)(2,1)}, u32[]{:S(2)}, u32[]{:S(2)}) collective-permute-start(bf16[1024,1024]{1,0:T(8,128)(2,1)} %pad_maximum_fusion), channel_id=1, source_target_pairs={{0,4},{4,0},{8,12},{12,8},{16,20},{20,16},{24,28},{28,24},{1,5},{5... | collective-permute-start | bytes 6291464 | tf_op jit(solution)/shard_map/ppermute | solution.py:110
  615.9 50.7 %collective-permute-start.92 = (bf16[1024,256]{1,0:T(8,128)(2,1)S(1)}, bf16[1024,256]{1,0:T(8,128)(2,1)S(1)}, u32[]{:S(2)}, u32[]{:S(2)}) collective-permute-start(bf16[1024,256]{1,0:T(8,128)(2,1)S(1)} %get-tuple-element.45), channel_id=1, source_target_pairs={{0,16},{4,20},{8,24},{12,28},{16,0},{20,4},{24,8},{28,12},{1,17},{... | collective-permute-start | bytes 1572872 | tf_op jit(solution)/shard_map/ppermute | solution.py:110
  618.4 48.2 %collective-permute-start.94 = (bf16[1024,256]{1,0:T(8,128)(2,1)S(1)}, bf16[1024,256]{1,0:T(8,128)(2,1)S(1)}, u32[]{:S(2)}, u32[]{:S(2)}) collective-permute-start(bf16[1024,256]{1,0:T(8,128)(2,1)S(1)} %get-tuple-element.46), channel_id=1, source_target_pairs={{0,24},{4,28},{8,16},{12,20},{16,8},{20,12},{24,0},{28,4},{1,25},{... | collective-permute-start | bytes 1572872 | tf_op jit(solution)/shard_map/ppermute | solution.py:110
  619.8 64.0 %collective-permute-start.93 = (bf16[1024,256]{1,0:T(8,128)(2,1)S(1)}, bf16[1024,256]{1,0:T(8,128)(2,1)S(1)}, u32[]{:S(2)}, u32[]{:S(2)}) collective-permute-start(bf16[1024,256]{1,0:T(8,128)(2,1)S(1)} %get-tuple-element.47), channel_id=1, source_target_pairs={{0,8},{4,12},{8,0},{12,4},{16,24},{20,28},{24,16},{28,20},{1,9},{5... | collective-permute-start | bytes 1572872 | tf_op jit(solution)/shard_map/ppermute | solution.py:110
  623.5 72.2 %collective-permute-start.85 = (bf16[256,1024]{1,0:T(8,128)(2,1)S(1)}, bf16[256,1024]{1,0:T(8,128)(2,1)S(1)}, u32[]{:S(2)}, u32[]{:S(2)}) collective-permute-start(bf16[256,1024]{1,0:T(8,128)(2,1)S(1)} %get-tuple-element.48), channel_id=1, source_target_pairs={{0,16},{4,20},{8,24},{12,28},{16,0},{20,4},{24,8},{28,12},{1,17},{... | collective-permute-start | bytes 1572872 | tf_op jit(solution)/shard_map/ppermute | solution.py:110
  626.4 69.3 %collective-permute-start.87 = (bf16[256,1024]{1,0:T(8,128)(2,1)S(1)}, bf16[256,1024]{1,0:T(8,128)(2,1)S(1)}, u32[]{:S(2)}, u32[]{:S(2)}) collective-permute-start(bf16[256,1024]{1,0:T(8,128)(2,1)S(1)} %get-tuple-element.49), channel_id=1, source_target_pairs={{0,24},{4,28},{8,16},{12,20},{16,8},{20,12},{24,0},{28,4},{1,25},{... | collective-permute-start | bytes 1572872 | tf_op jit(solution)/shard_map/ppermute | solution.py:110
  714.8 37.9 %collective-permute-start.75 = (bf16[256,1024]{1,0:T(8,128)(2,1)S(1)}, bf16[256,1024]{1,0:T(8,128)(2,1)S(1)}, u32[]{:S(2)}, u32[]{:S(2)}) collective-permute-start(bf16[256,1024]{1,0:T(8,128)(2,1)S(1)} %pad_maximum_fusion.14), channel_id=1, source_target_pairs={{0,4},{4,0},{8,12},{12,8},{16,20},{20,16},{24,28},{28,24},{1,5},{5... | collective-permute-start | bytes 1572872 | tf_op jit(solution)/shard_map/ppermute | solution.py:110
  716.9 39.9 %collective-permute-start.68 = (bf16[1024,256]{1,0:T(8,128)(2,1)S(1)}, bf16[1024,256]{1,0:T(8,128)(2,1)S(1)}, u32[]{:S(2)}, u32[]{:S(2)}) collective-permute-start(bf16[1024,256]{1,0:T(8,128)(2,1)S(1)} %pad_maximum_fusion.12), channel_id=1, source_target_pairs={{0,4},{4,0},{8,12},{12,8},{16,20},{20,16},{24,28},{28,24},{1,5},{5... | collective-permute-start | bytes 1572872 | tf_op jit(solution)/shard_map/ppermute | solution.py:110
  (138 other events, 2165.2 us)
Sparse Core Ops, SparseCore 0:
  28.1 35.8 all-gather.4
  135.6 44.7 reduce-scatter.4
  211.7 34.4 all-gather.6
  248.2 34.4 all-gather.8
  376.1 48.1 reduce-scatter.8
  426.8 44.5 reduce-scatter.6
  503.4 34.4 all-gather.10
  568.2 44.5 reduce-scatter.10

commit v2 on v1

--- a/solution.py
+++ b/solution.py
@@ -1,6 +1,8 @@
 import jax
 import jax.numpy as jnp
 from jax import lax
+from jax.experimental import pallas as pl
+from jax.experimental.pallas import tpu as pltpu
 from jax.sharding import PartitionSpec as P
 
 HEAD_DIM = 128
@@ -9,24 +11,6 @@
 NEGATIVE = -1e30
 LOW = jnp.bfloat16
 F32 = jnp.float32
-
-
-def normalize(values, gain, shift):
-    mean_row = jnp.mean(values, axis=1, keepdims=True)
-    centred = values - mean_row
-    inverse = lax.rsqrt(jnp.mean(centred * centred, axis=1, keepdims=True) + EPSILON)
-    unit_rows = centred * inverse
-    return (unit_rows * gain + shift, unit_rows, inverse)
-
-
-def normalize_back(grad_rows, unit_rows, inverse, gain):
-    scaled = grad_rows * gain
-    grad_in = inverse * (
-        scaled
-        - jnp.mean(scaled, axis=1, keepdims=True)
-        - unit_rows * jnp.mean(scaled * unit_rows, axis=1, keepdims=True)
-    )
-    return (grad_in, jnp.sum(grad_rows * unit_rows, axis=0), jnp.sum(grad_rows, axis=0))
 
 
 def gelu_parts(pre_act):
@@ -76,6 +60,358 @@
         (grad_key * scale_factor).astype(LOW).reshape(queries.shape),
         grad_value.astype(LOW).reshape(queries.shape),
     )
+
+
+NC = 4
+MESH = pl.DeviceIdType.MESH
+
+
+class Place:
+    def __init__(self):
+        self.d = lax.axis_index("dp")
+        self.t = lax.axis_index("tensor")
+        self.c = lax.rem(self.t, 2)
+        self.t_core = self.t + 1 - 2 * self.c
+        self.t_x = lax.rem(self.t + 2, 4)
+        self.t_far = lax.rem(self.t_core + 2, 4)
+        self.d_y = self.d + 1 - 2 * lax.rem(self.d, 2)
+        self.d_z = self.d + 2 - 4 * lax.rem(lax.div(self.d, 2), 2)
+        c = self.c
+        self.first = (self.d + c * (self.d_z - self.d), self.t_x + c * (self.t - self.t_x))
+        self.second = (self.d_z + c * (self.d - self.d_z), self.t + c * (self.t_x - self.t))
+        self.core = (self.d, self.t_core)
+        self.x = (self.d, self.t_x)
+        self.z = (self.d_z, self.t)
+
+
+def greet(peers):
+    barrier = pltpu.get_barrier_semaphore()
+    for peer in peers:
+        pl.semaphore_signal(barrier, inc=1, device_id=peer, device_id_type=MESH)
+    pl.semaphore_wait(barrier, len(peers))
+
+
+def remote(src, dst, send, recv, peer):
+    return pltpu.make_async_remote_copy(
+        src_ref=src, dst_ref=dst, send_sem=send, recv_sem=recv, device_id=peer, device_id_type=MESH
+    )
+
+
+class Gather:
+    SEMS = [pltpu.SemaphoreType.DMA((7, NC)), pltpu.SemaphoreType.DMA((7, NC)), pltpu.SemaphoreType.DMA((NC,))]
+
+    def __init__(self, me, own, whole, send, recv, keep):
+        self.me, self.own, self.whole = me, own, whole
+        self.send, self.recv, self.keep = send, recv, keep
+        self.rows = own.shape[0] // NC
+
+    def at(self, side, t, j):
+        return self.whole.at[side, t, pl.ds(j * self.rows, self.rows)]
+
+    def piece(self, j):
+        return self.own.at[pl.ds(j * self.rows, self.rows)]
+
+    def copy(self, kind, j, src, dst, peer):
+        return remote(src, dst, self.send.at[kind, j], self.recv.at[kind, j], peer)
+
+    def own_copies(self, j):
+        me = self.me
+        return [
+            self.copy(2, j, self.piece(j), self.at(1, me.t, j), me.z),
+            self.copy(1, j, self.piece(j), self.at(0, me.t, j), me.x),
+            self.copy(0, j, self.piece(j), self.at(0, me.t, j), me.core),
+            pltpu.make_async_copy(self.piece(j), self.at(0, me.t, j), self.keep.at[j]),
+        ]
+
+    def start(self, j):
+        for copy in self.own_copies(j):
+            copy.start()
+
+    def wait_recv(self, kind, j, side, t):
+        slot = self.at(side, t, j)
+        self.copy(kind, j, slot, slot, self.me.core).wait_recv()
+
+    def relay(self, kind, j, side, t):
+        slot = self.at(side, t, j)
+        self.copy(kind + 3, j, slot, slot, self.me.core).start()
+
+    def finish(self):
+        me, c = self.me, self.me.c
+
+        @pl.loop(0, NC)
+        def _(j):
+            side, t = 1 - c, me.t + c * (me.t_x - me.t)
+            self.wait_recv(2 - c, j, side, t)
+            slot = self.at(side, t, j)
+            self.copy(3, j, slot, self.at(1, t, j), me.first).start()
+            self.relay(2 - c, j, side, t)
+            side, t = c, me.t_x + c * (me.t - me.t_x)
+            self.wait_recv(1 + c, j, side, t)
+            self.relay(1 + c, j, side, t)
+
+        @pl.loop(0, NC)
+        def _(j):
+            self.wait_recv(3, j, 1, me.t_x)
+            self.relay(3, j, 1, me.t_x)
+
+        @pl.loop(0, NC)
+        def _(j):
+            self.wait_recv(0, j, 0, me.t_core)
+            self.wait_recv(4, j, 0, me.t_far)
+            self.wait_recv(5, j, 1, me.t_core)
+            self.wait_recv(6, j, 1, me.t_far)
+            for copy in self.own_copies(j)[:3]:
+                copy.wait_send()
+            self.own_copies(j)[3].wait()
+            for kind in (3, 4, 5, 6):
+                slot = self.at(0, me.t, j)
+                self.copy(kind, j, slot, slot, me.core).wait_send()
+
+
+class Scatter:
+    SEMS = [
+        pltpu.SemaphoreType.DMA((4, NC)),
+        pltpu.SemaphoreType.DMA((4, NC)),
+        pltpu.SemaphoreType.DMA((4, NC)),
+        pltpu.SemaphoreType.DMA((3, NC)),
+        pltpu.SemaphoreType.DMA((3, NC)),
+    ]
+
+    @staticmethod
+    def buffers(rows, width):
+        return [
+            pltpu.VMEM((4, rows, width), LOW),
+            pltpu.VMEM((4, rows, width), LOW),
+            pltpu.VMEM((3, rows, width), LOW),
+        ]
+
+    def __init__(self, me, parts, held, came, hops, load, send, recv, hop_send, hop_recv):
+        self.me, self.parts = me, parts
+        self.held, self.came, self.hops = held, came, hops
+        self.load, self.send, self.recv = load, send, recv
+        self.hop_send, self.hop_recv = hop_send, hop_recv
+        self.rows = held.shape[1] // NC
+
+    def span(self, j):
+        return pl.ds(j * self.rows, self.rows)
+
+    def pairs(self):
+        me = self.me
+        return [(0, me.t, me.t_core), (0, me.t_x, me.t_far), (1, me.t, me.t_core), (1, me.t_x, me.t_far)]
+
+    def core_copy(self, i, j):
+        side, _, theirs = self.pairs()[i]
+        return remote(
+            self.parts.at[side, theirs, self.span(j)],
+            self.came.at[i, self.span(j)],
+            self.send.at[i, j],
+            self.recv.at[i, j],
+            self.me.core,
+        )
+
+    def load_copy(self, i, j):
+        side, mine, _ = self.pairs()[i]
+        return pltpu.make_async_copy(
+            self.parts.at[side, mine, self.span(j)], self.held.at[i, self.span(j)], self.load.at[i, j]
+        )
+
+    def hop(self, kind, j, src, peer):
+        return remote(
+            src, self.hops.at[kind, self.span(j)], self.hop_send.at[kind, j], self.hop_recv.at[kind, j], peer
+        )
+
+    def start(self):
+        for i in (3, 1, 2, 0):
+
+            @pl.loop(0, NC)
+            def _(j):
+                self.core_copy(i, j).start()
+                self.load_copy(i, j).start()
+
+    def joined(self, i, j):
+        held, came = self.held.at[i, self.span(j)], self.came.at[i, self.span(j)]
+        pltpu.make_async_copy(held, held, self.load.at[i, j]).wait()
+        remote(came, came, self.send.at[i, j], self.recv.at[i, j], self.me.core).wait_recv()
+        return held[...].astype(F32) + came[...].astype(F32)
+
+    def spread(self):
+        me, c = self.me, self.me.c
+        straight, turn = 1 + c, 2 - c
+
+        @pl.loop(0, NC)
+        def _(j):
+            self.held[3, self.span(j)] = self.joined(3, j).astype(LOW)
+            self.hop(0, j, self.held.at[3, self.span(j)], me.first).start()
+
+        @pl.loop(0, NC)
+        def _(j):
+            self.held[straight, self.span(j)] = self.joined(straight, j).astype(LOW)
+            self.hop(1, j, self.held.at[straight, self.span(j)], me.first).start()
+
+        @pl.loop(0, NC)
+        def _(j):
+            total = self.joined(turn, j)
+            arrived = self.hops.at[0, self.span(j)]
+            self.hop(0, j, arrived, me.first).wait_recv()
+            self.held[turn, self.span(j)] = (total + arrived[...].astype(F32)).astype(LOW)
+            self.hop(2, j, self.held.at[turn, self.span(j)], me.second).start()
+
+    def result(self, j):
+        total = self.joined(0, j)
+        for kind in (1, 2):
+            arrived = self.hops.at[kind, self.span(j)]
+            self.hop(kind, j, arrived, self.me.first).wait_recv()
+            total = total + arrived[...].astype(F32)
+        return total
+
+    def finish(self):
+        @pl.loop(0, NC)
+        def _(j):
+            for i in range(4):
+                self.core_copy(i, j).wait_send()
+            for kind in range(3):
+                self.hop(kind, j, self.hops.at[kind, self.span(j)], self.me.first).wait_send()
+
+
+def unit_of(rows):
+    centred = rows - jnp.mean(rows, axis=1, keepdims=True)
+    inverse = lax.rsqrt(jnp.mean(centred * centred, axis=1, keepdims=True) + EPSILON)
+    return centred * inverse, inverse
+
+
+def back_of(grad_rows, unit_rows, inverse, gain):
+    scaled = grad_rows * gain
+    return inverse * (
+        scaled
+        - jnp.mean(scaled, axis=1, keepdims=True)
+        - unit_rows * jnp.mean(scaled * unit_rows, axis=1, keepdims=True)
+    )
+
+
+def pieces(rows):
+    size = rows // NC
+    return lambda j: pl.ds(j * size, size)
+
+
+def head_kernel(x, gain, shift, grad, whole, whole_grad, own, own_grad, *sems):
+    me = Place()
+    at = pieces(x.shape[0])
+    gather = Gather(me, own, whole, *sems[:3])
+    gather_grad = Gather(me, own_grad, whole_grad, *sems[3:])
+    greet([me.core, me.x, me.z])
+
+    @pl.loop(0, NC)
+    def _(j):
+        unit_rows, _ = unit_of(x[at(j)])
+        own[at(j)] = (unit_rows * gain[...] + shift[...]).astype(LOW)
+        gather.start(j)
+
+    gather.finish()
+
+    @pl.loop(0, NC)
+    def _(j):
+        own_grad[at(j)] = grad[at(j)].astype(LOW)
+        gather_grad.start(j)
+
+    gather_grad.finish()
+
+
+def middle_kernel(parts, base, gain, shift, resid, whole, own, *scratch):
+    me = Place()
+    at = pieces(base.shape[0])
+    scatter = Scatter(me, parts, *scratch[:8])
+    gather = Gather(me, own, whole, *scratch[8:])
+    greet([me.core, me.x, me.z])
+    scatter.start()
+    scatter.spread()
+
+    @pl.loop(0, NC)
+    def _(j):
+        rows = base[at(j)] + scatter.result(j)
+        resid[at(j)] = rows
+        unit_rows, _ = unit_of(rows)
+        own[at(j)] = (unit_rows * gain[...] + shift[...]).astype(LOW)
+        gather.start(j)
+
+    gather.finish()
+    scatter.finish()
+
+
+def turn_kernel(parts, resid, grad, gain, grad_resid, whole, sums, own, *scratch):
+    me = Place()
+    at = pieces(resid.shape[0])
+    scatter = Scatter(me, parts, *scratch[:8])
+    gather = Gather(me, own, whole, *scratch[8:])
+    greet([me.core, me.x, me.z])
+    scatter.start()
+    scatter.spread()
+    sums[...] = jnp.zeros_like(sums)
+
+    @pl.loop(0, NC)
+    def _(j):
+        unit_rows, inverse = unit_of(resid[at(j)])
+        e = scatter.result(j)
+        rows = grad[at(j)] + back_of(e, unit_rows, inverse, gain[...])
+        grad_resid[at(j)] = rows
+        own[at(j)] = rows.astype(LOW)
+        gather.start(j)
+        sums[0:1] += jnp.sum(e * unit_rows, axis=0, keepdims=True)
+        sums[1:2] += jnp.sum(e, axis=0, keepdims=True)
+        sums[2:3] += jnp.sum(rows, axis=0, keepdims=True)
+
+    gather.finish()
+    scatter.finish()
+
+
+def tail_kernel(parts, lowered, x, gain, grad_resid, base, grad_inputs, output, sums, *scratch):
+    me = Place()
+    at = pieces(x.shape[0])
+    scatter = Scatter(me, parts, *scratch[:8])
+    other = Scatter(me, lowered, *scratch[8:])
+    greet([me.core, me.x, me.z])
+    scatter.start()
+    scatter.spread()
+    other.start()
+    sums[...] = jnp.zeros_like(sums)
+
+    @pl.loop(0, NC)
+    def _(j):
+        unit_rows, inverse = unit_of(x[at(j)])
+        e = scatter.result(j)
+        grad_inputs[at(j)] = grad_resid[at(j)] + back_of(e, unit_rows, inverse, gain[...])
+        sums[0:1] += jnp.sum(e * unit_rows, axis=0, keepdims=True)
+        sums[1:2] += jnp.sum(e, axis=0, keepdims=True)
+
+    scatter.finish()
+    other.spread()
+
+    @pl.loop(0, NC)
+    def _(j):
+        output[at(j)] = base[at(j)] + other.result(j)
+
+    other.finish()
+
+
+VMEM = pl.BlockSpec(memory_space=pltpu.VMEM)
+ANY = pl.BlockSpec(memory_space=pl.ANY)
+
+
+def call(kernel, number, ins, in_specs, outs, out_specs, scratch):
+    return pl.pallas_call(
+        kernel,
+        out_shape=outs,
+        in_specs=in_specs,
+        out_specs=out_specs,
+        scratch_shapes=scratch,
+        compiler_params=pltpu.CompilerParams(
+            collective_id=number, has_side_effects=True, vmem_limit_bytes=40 << 20
+        ),
+        cost_estimate=pl.CostEstimate(flops=0, bytes_accessed=100_000_000, transcendentals=0),
+    )(*ins)
+
+
+def like(*shape, dtype=F32):
+    return jax.ShapeDtypeStruct(shape, dtype)
 
 
 def local(
@@ -157,16 +493,6 @@
         second = jnp.where(side == 0, sums[1], sums[0])
         return jnp.concatenate([first, second], 1 - axis)
 
-    def gather_tokens(rows):
-        pair = jnp.stack([rows, hop(rows, 2)])
-        whole = lax.all_gather(pair, "tensor", axis=1, tiled=True)
-        return whole.reshape(-1, rows.shape[1])
-
-    def scatter_tokens(partial):
-        pair = partial.astype(LOW).reshape(2, -1, partial.shape[1])
-        mine = lax.psum_scatter(pair, "tensor", scatter_dimension=1, tiled=True)
-        return mine[0].astype(F32) + hop(mine[1], 2).astype(F32)
-
     def mm(left, right):
         return jnp.dot(left, right, preferred_element_type=F32)
 
@@ -176,50 +502,75 @@
     def mm_tn(left, right):
         return jnp.einsum("ta,tb->ab", left, right, preferred_element_type=F32)
 
+    rows, width = inputs.shape
+    row = lambda vector: vector.reshape(1, -1)
+    group = like(2, tensor_total, rows, width, dtype=LOW)
+    own = pltpu.VMEM((rows, width), LOW)
+    spread_scratch = Scatter.buffers(rows, width) + Scatter.SEMS
+
     segment = jnp.stack([seg_ids, hop(seg_ids, 2)]).reshape(-1, GROUP)
     places = jnp.stack([positions, hop(positions, 2)]).reshape(-1, GROUP)
 
-    normed1, unit1, inverse1 = normalize(inputs, norm1_gain, norm1_bias)
-    whole1 = gather_tokens(normed1.astype(LOW))
-    q_full = gather_weight(query_weight, 0)
-    k_full = gather_weight(key_weight, 0)
-    v_full = gather_weight(value_weight, 0)
-    queries = (mm(whole1, q_full) + own_half(query_bias, 0)).astype(LOW)
-    keys = mm(whole1, k_full).astype(LOW)
-    values = (mm(whole1, v_full) + own_half(value_bias, 0)).astype(LOW)
+    whole1, grad_whole = call(
+        head_kernel, 1,
+        (inputs, row(norm1_gain), row(norm1_bias), grad_output), [VMEM] * 4,
+        (group, group), (ANY, ANY),
+        [own, own] + Gather.SEMS * 2,
+    )
+    whole1, grad_whole = whole1.reshape(-1, width), grad_whole.reshape(-1, width)
+    halves = query_bias.shape[0] // 2
+    qkv_weight = jnp.stack([query_weight, key_weight, value_weight], 1).astype(LOW)
+    qkv_full = gather_weight(
+        jnp.concatenate([qkv_weight[..., :halves].reshape(-1, 3 * halves), qkv_weight[..., halves:].reshape(-1, 3 * halves)], 1), 0
+    )
+    qkv = mm(whole1, qkv_full)
+    queries = (qkv[:, :halves] + own_half(query_bias, 0)).astype(LOW)
+    keys = qkv[:, halves : 2 * halves].astype(LOW)
+    values = (qkv[:, 2 * halves :] + own_half(value_bias, 0)).astype(LOW)
     attended, log_totals = attend(queries, keys, values, segment, places)
     o_full = gather_weight(out_weight, 1)
-    resid = inputs + scatter_tokens(mm(attended, o_full)) + out_bias
-    normed2, unit2, inverse2 = normalize(resid, norm2_gain, norm2_bias)
-    whole2 = gather_tokens(normed2.astype(LOW))
+
+    def as_group(partial):
+        return partial.astype(LOW).reshape(group.shape)
+
+    resid, whole2 = call(
+        middle_kernel, 2,
+        (as_group(mm(attended, o_full)), inputs + out_bias, row(norm2_gain), row(norm2_bias)), [ANY] + [VMEM] * 3,
+        (like(rows, width), group), (VMEM, ANY),
+        [own] + spread_scratch + Gather.SEMS,
+    )
+    whole2 = whole2.reshape(-1, width)
     up_full = gather_weight(up_weight, 0)
     pre_act = mm(whole2, up_full) + own_half(up_bias, 0)
     cumulative, slope = gelu_parts(pre_act)
     activated = (pre_act * cumulative).astype(LOW)
-    grad_whole = gather_tokens(grad_output.astype(LOW))
     down_full = gather_weight(down_weight, 1)
     grad_down = scatter_grad(mm_tn(activated, grad_whole).astype(LOW), 1)
-    layer_output = resid + scatter_tokens(mm(activated, down_full)) + down_bias
+    lowered = as_group(mm(activated, down_full))
     grad_pre = (mm_nt(grad_whole, down_full) * slope).astype(LOW)
     grad_up_part = jnp.sum(grad_pre.astype(F32), axis=0)
     grad_up = scatter_grad(mm_tn(whole2, grad_pre).astype(LOW), 0)
-    grad_normed2 = scatter_tokens(mm_nt(grad_pre, up_full))
-    back2, gain2_part, bias2_part = normalize_back(grad_normed2, unit2, inverse2, norm2_gain)
-    grad_resid = grad_output + back2
-    grad_mixed = gather_tokens(grad_resid.astype(LOW))
+    grad_resid, grad_mixed, sums2 = call(
+        turn_kernel, 3,
+        (as_group(mm_nt(grad_pre, up_full)), resid, grad_output, row(norm2_gain)), [ANY] + [VMEM] * 3,
+        (like(rows, width), group, like(8, width)), (VMEM, ANY, VMEM),
+        [own] + spread_scratch + Gather.SEMS,
+    )
+    grad_mixed = grad_mixed.reshape(-1, width)
     grad_out_w = scatter_grad(mm_tn(attended, grad_mixed).astype(LOW), 1)
     grad_att = mm_nt(grad_mixed, o_full).astype(LOW)
     grad_queries, grad_keys, grad_values = attend_back(
         queries, keys, values, grad_att, segment, places, log_totals
     )
-    grad_value_w = scatter_grad(mm_tn(whole1, grad_values).astype(LOW), 0)
-    grad_key_w = scatter_grad(mm_tn(whole1, grad_keys).astype(LOW), 0)
-    grad_query_w = scatter_grad(mm_tn(whole1, grad_queries).astype(LOW), 0)
-    grad_normed1 = scatter_tokens(
-        mm_nt(grad_queries, q_full) + mm_nt(grad_keys, k_full) + mm_nt(grad_values, v_full)
-    )
-    back1, gain1_part, bias1_part = normalize_back(grad_normed1, unit1, inverse1, norm1_gain)
-    grad_inputs = grad_resid + back1
+    grad_qkv = jnp.concatenate([grad_queries, grad_keys, grad_values], 1)
+    grad_qkv_w = scatter_grad(mm_tn(whole1, grad_qkv).astype(LOW), 0)
+    grad_qkv_w = grad_qkv_w.reshape(-1, 2, 3, halves).transpose(2, 0, 1, 3).reshape(3, -1, 2 * halves)
+    grad_inputs, layer_output, sums1 = call(
+        tail_kernel, 4,
+        (as_group(mm_nt(grad_qkv, qkv_full)), lowered, inputs, row(norm1_gain), grad_resid, resid + down_bias), [ANY] * 2 + [VMEM] * 4,
+        (like(rows, width), like(rows, width), like(8, width)), (VMEM,) * 3,
+        spread_scratch * 2,
+    )
 
     def sum_dp(vector):
         mask = 1
@@ -242,18 +593,17 @@
             side == 0, jnp.concatenate([half, empty]), jnp.concatenate([empty, half])
         )
 
-    width = inputs.shape[1]
     early = sum_all(
         jnp.stack(
             [
                 jnp.sum(grad_output, axis=0),
-                gain2_part,
-                bias2_part,
-                jnp.sum(grad_resid, axis=0),
+                sums2[0],
+                sums2[1],
+                sums2[2],
             ]
         )
     )
-    late = sum_all(jnp.stack([gain1_part, bias1_part]))
+    late = sum_all(sums1[:2])
     up_sum = sum_dp(spread(grad_up_part))
     query_sum = sum_dp(spread(jnp.sum(grad_queries.astype(F32), axis=0)))
     value_sum = sum_dp(spread(jnp.sum(grad_values.astype(F32), axis=0)))
@@ -262,10 +612,10 @@
         grad_inputs,
         late[0],
         late[1],
-        grad_query_w,
+        grad_qkv_w[0],
         query_sum,
-        grad_key_w,
-        grad_value_w,
+        grad_qkv_w[1],
+        grad_qkv_w[2],
         value_sum,
         grad_out_w,
         early[3],

time: 840 us -> 728 us (0.87)
  waiting for transfers between devices: 445 us -> 219 us
  Pallas kernels: 0 us -> 181 us
  starting transfers between devices: 155 us -> 115 us
  local copies, waits for them, and re-layouts: 65.2 us -> 87.1 us
  other arithmetic: 53.2 us -> 33.8 us
  matrix products: 95.9 us -> 77.8 us
  between operations: 15.9 us -> 1.82 us
    pallas_call x0 -> x4, Pallas kernels: none -> 181 us  [call(): pl.pallas_call(kernel, out_shape=outs, in_specs=in_specs, out_specs=out_s...]
    reduce_scatter x4 -> x0, waiting for transfers between devices: 127 us -> none  [scatter_tokens(): mine = lax.psum_scatter(pair, 'tensor', scatter_dimension=1, tiled=True)]
    ppermute x91 -> x61, waiting for transfers between devices: 301 us -> 217 us  [hop(): return lax.ppermute(rows, 'dp', [(i, i ^ mask) for i in range(dp_total)])]
    ppermute x91 -> x61, starting transfers between devices: 152 us -> 112 us  [hop(): return lax.ppermute(rows, 'dp', [(i, i ^ mask) for i in range(dp_total)])]
    dot_general x6 -> x4, matrix products: 36.6 us -> 21 us  [mm(): return jnp.dot(left, right, preferred_element_type=F32)]
    all_gather x4 -> x0, waiting for transfers between devices: 12.7 us -> none  [gather_tokens(): whole = lax.all_gather(pair, 'tensor', axis=1, tiled=True)]
    reduce_sum x7 -> x1, other arithmetic: 10.9 us -> 0.66 us  [local(): jnp.sum(grad_output, axis=0)]
    dot_general x6 -> x4, matrix products: 30.1 us -> 22.6 us  [mm_nt(): return jnp.einsum('td,fd->tf', left, right, preferred_element_type=F32)]
  transfers between devices with their start and end apart: 103 -> 65, of which waited for: 47 -> 20; matrix products, arithmetic and copies ran while one was open for 18% -> 17% of each run, Pallas kernels for 0% -> 19%
where the time goes in v2:
time: 728 us; the launch traced here: 716 us
  waiting for transfers between devices  219 us (30%)
  Pallas kernels  181 us (25%)
  starting transfers between devices  115 us (16%)
  local copies, waits for them, and re-layouts  87.1 us (12%)
  matrix products  77.8 us (11%)
  other arithmetic  33.8 us (5%)
    ppermute x61, waiting for transfers between devices, hop(): return lax.ppermute(rows, 'dp', [(i, i ^ mask) for i in range(dp_total)])  217 us
    pallas_call x4, Pallas kernels, call(): pl.pallas_call(kernel, out_shape=outs, in_specs=in_specs, out_specs=out_s...  181 us
    ppermute x61, starting transfers between devices, hop(): return lax.ppermute(rows, 'dp', [(i, i ^ mask) for i in range(dp_total)])  112 us
    dynamic_update_slice x31, local copies, waits for them, and re-layouts, gather_weight(): whole = lax.dynamic_update_slice(whole, block, tuple(start))  33.4 us
    dot_general x4, matrix products, mm_nt(): return jnp.einsum('td,fd->tf', left, right, preferred_element_type=F32)  22.6 us
    dot_general x4, matrix products, mm_tn(): return jnp.einsum('ta,tb->ab', left, right, preferred_element_type=F32)  22.3 us
    dot_general x4, matrix products, mm(): return jnp.dot(left, right, preferred_element_type=F32)  21 us
  transfers between devices with their start and end apart: 65, of which 20 were waited for; matrix products, arithmetic and copies ran while one was open for 17% of the time, Pallas kernels for 19%

profile of v2, /device:TPU:0, one launch (start us, length us, event | category | flops | bytes accessed | tf_op | source)
XLA Modules:
  0.0 715.9 jit_solution(12331299172340881342)
XLA Ops:
  36.8 42.1 %shard_map.314 = (bf16[2,4,128,2048]{3,2,1,0:T(8,128)(2,1)S(1)}, bf16[2,4,128,2048]{3,2,1,0:T(8,128)(2,1)S(1)}) custom-call(f32[128,2048]{1,0:T(8,128)S(1)} %copy-done, f32[1,2048]{1,0:T(1,128)S(1)} %bitcast.105, f32[1,2048]{1,0:T(1,128)S(1)} %bitcast.107, f32[128,2048]{1,0:T(8,128)S(1)} %copy-done.1), custom_call_target="tpu_custom_call" | custom-call | bytes 100000000 | tf_op jit(solution)/shard_map/pallas_call | solution.py:400
  91.8 6.1 collective-permute-done.18
  101.8 8.4 %collective-permute-done.20 = bf16[256,256]{1,0:T(8,128)(2,1)S(1)} collective-permute-done((bf16[256,256]{1,0:T(8,128)(2,1)}, bf16[256,256]{1,0:T(8,128)(2,1)S(1)}, u32[]{:S(2)}, u32[]{:S(2)}) %collective-permute-start.20) | collective-permute-done | bytes 131104 | tf_op jit(solution)/shard_map/ppermute | solution.py:446
  126.8 9.0 %collective-permute-done.3 = bf16[256,768]{0,1:T(8,128)(2,1)S(1)} collective-permute-done((bf16[256,768]{0,1:T(8,128)(2,1)S(1)}, bf16[256,768]{0,1:T(8,128)(2,1)S(1)}, u32[]{:S(2)}, u32[]{:S(2)}) %collective-permute-start.3) | collective-permute-done | bytes 393248 | tf_op jit(solution)/shard_map/ppermute | solution.py:446
  143.4 6.3 collective-permute-done.5
  149.7 25.6 %collective-permute-start.12 = (bf16[1024,256]{1,0:T(8,128)(2,1)}, bf16[1024,256]{1,0:T(8,128)(2,1)}, u32[]{:S(2)}, u32[]{:S(2)}) collective-permute-start(bf16[1024,256]{1,0:T(8,128)(2,1)} %get-tuple-element.55), channel_id=1, source_target_pairs={{0,16},{4,20},{8,24},{12,28},{16,0},{20,4},{24,8},{28,12},{1,17},{... | collective-permute-start | bytes 1572872 | tf_op jit(solution)/shard_map/ppermute | solution.py:446
  181.4 26.2 %collective-permute-done.26 = bf16[256,1024]{1,0:T(8,128)(2,1)} collective-permute-done((bf16[256,1024]{1,0:T(8,128)(2,1)S(1)}, bf16[256,1024]{1,0:T(8,128)(2,1)}, u32[]{:S(2)}, u32[]{:S(2)}) %collective-permute-start.26) | collective-permute-done | bytes 524320 | tf_op jit(solution)/shard_map/ppermute | solution.py:446
  240.1 52.5 %shard_map.315 = (f32[128,2048]{1,0:T(8,128)S(1)}, bf16[2,4,128,2048]{3,2,1,0:T(8,128)(2,1)S(1)}) custom-call(bf16[2,4,128,2048]{3,2,1,0:T(8,128)(2,1)S(1)} %bitcast.99, f32[128,2048]{1,0:T(8,128)S(1)} %broadcast_add_fusion.1.base, f32[1,2048]{1,0:T(1,128)S(1)} %bitcast.103, f32[1,2048]{1,0:T(1,128)S(1)} %bitcast.108), custom_call_target="tpu_custom_call" | custom-call | bytes 100000000 | tf_op jit(solution)/shard_map/pallas_call | solution.py:400
  305.9 6.8 multiply_convert_fusion
  312.8 6.3 convolution_convert_fusion.2
  321.5 8.0 %collective-permute-done.15 = bf16[1024,256]{1,0:T(8,128)(2,1)S(1)} collective-permute-done((bf16[1024,256]{1,0:T(8,128)(2,1)}, bf16[1024,256]{1,0:T(8,128)(2,1)S(1)}, u32[]{:S(2)}, u32[]{:S(2)}) %collective-permute-start.15) | collective-permute-done | bytes 524320 | tf_op jit(solution)/shard_map/ppermute | solution.py:446
  329.6 6.2 convolution_convert_fusion.4
  335.8 6.1 convert_reduce_fusion
  341.9 6.2 convolution_convert_fusion.3
  348.1 7.2 convolution_convert_fusion.5
  355.3 42.4 %shard_map.316 = (f32[128,2048]{1,0:T(8,128)S(1)}, bf16[2,4,128,2048]{3,2,1,0:T(8,128)(2,1)S(1)}, f32[8,2048]{1,0:T(8,128)S(1)}) custom-call(bf16[2,4,128,2048]{3,2,1,0:T(8,128)(2,1)S(1)} %bitcast.100, f32[128,2048]{1,0:T(8,128)S(1)} %get-tuple-element.30.resid, f32[128,2048]{1,0:T(8,128)S(1)} %copy-done.1, f32[1,2048]{1,0:T(1,128)S(1)} %bitcast.104), custom_call_target="tpu_custom_call" | custom-call | bytes 100000000 | tf_op jit(solution)/shard_map/pallas_call | solution.py:400
  422.3 7.5 %convolution_convert_fusion.6 = bf16[2048,768]{1,0:T(8,128)(2,1)} fusion(bf16[1024,2048]{1,0:T(8,128)(2,1)} %bitcast.110, bf16[1024,768]{1,0:T(8,128)(2,1)S(1)} %bitcast_dynamic-update-slice_fusion), kind=kOutput, calls=%fused_computation.23 | convolution fusion | flops 3222798336 | bytes 8912896 | tf_op jit(solution)/shard_map/ta,tb->ab/dot_general | solution.py:503
  442.4 43.9 %shard_map.317 = (f32[128,2048]{1,0:T(8,128)S(1)}, f32[128,2048]{1,0:T(8,128)S(1)}, f32[8,2048]{1,0:T(8,128)S(1)}) custom-call(bf16[2,4,128,2048]{3,2,1,0:T(8,128)(2,1)S(1)} %bitcast.102, bf16[2,4,128,2048]{3,2,1,0:T(8,128)(2,1)S(1)} %bitcast.101, f32[128,2048]{1,0:T(8,128)S(1)} %copy-done, f32[1,2048]{1,0:T(1,128)S(1)} %bitcast.106, ...), custom_call_target="tpu_custom_call" | custom-call | bytes 100000000 | tf_op jit(solution)/shard_map/pallas_call | solution.py:400
  523.2 60.5 %collective-permute-done.45 = bf16[256,1024]{1,0:T(8,128)(2,1)S(1)} collective-permute-done((bf16[256,1024]{1,0:T(8,128)(2,1)S(1)}, bf16[256,1024]{1,0:T(8,128)(2,1)S(1)}, u32[]{:S(2)}, u32[]{:S(2)}) %collective-permute-start.45) | collective-permute-done | bytes 524320 | tf_op jit(solution)/shard_map/ppermute | solution.py:446
  588.3 9.5 %collective-permute-done.46 = bf16[256,256]{1,0:T(8,128)(2,1)S(1)} collective-permute-done((bf16[256,256]{1,0:T(8,128)(2,1)S(1)}, bf16[256,256]{1,0:T(8,128)(2,1)S(1)}, u32[]{:S(2)}, u32[]{:S(2)}) %collective-permute-start.46) | collective-permute-done | bytes 131104 | tf_op jit(solution)/shard_map/ppermute | solution.py:446
  597.8 8.3 %collective-permute-start.38 = (bf16[256,768]{1,0:T(8,128)(2,1)S(1)}, bf16[256,768]{1,0:T(8,128)(2,1)S(1)}, u32[]{:S(2)}, u32[]{:S(2)}) collective-permute-start(bf16[256,768]{1,0:T(8,128)(2,1)S(1)} %get-tuple-element.75), channel_id=1, source_target_pairs={{0,24},{4,28},{8,16},{12,20},{16,8},{20,12},{24,0},{28,4},{1,25},{... | collective-permute-start | bytes 1179656 | tf_op jit(solution)/shard_map/ppermute | solution.py:446
  612.9 8.4 %collective-permute-done.36 = bf16[256,768]{1,0:T(8,128)(2,1)S(1)} collective-permute-done((bf16[256,768]{1,0:T(8,128)(2,1)S(1)}, bf16[256,768]{1,0:T(8,128)(2,1)S(1)}, u32[]{:S(2)}, u32[]{:S(2)}) %collective-permute-start.36) | collective-permute-done | bytes 393248 | tf_op jit(solution)/shard_map/ppermute | solution.py:446
  648.7 19.8 %collective-permute-done.62 = bf16[1024,256]{1,0:T(8,128)(2,1)} collective-permute-done((bf16[1024,256]{1,0:T(8,128)(2,1)}, bf16[1024,256]{1,0:T(8,128)(2,1)}, u32[]{:S(2)}, u32[]{:S(2)}) %collective-permute-start.62) | collective-permute-done | bytes 524320 | tf_op jit(solution)/shard_map/ppermute | solution.py:446
  672.0 38.6 %collective-permute-done.55 = bf16[256,1024]{1,0:T(8,128)(2,1)S(1)} collective-permute-done((bf16[256,1024]{1,0:T(8,128)(2,1)S(1)}, bf16[256,1024]{1,0:T(8,128)(2,1)S(1)}, u32[]{:S(2)}, u32[]{:S(2)}) %collective-permute-start.55) | collective-permute-done | bytes 524320 | tf_op jit(solution)/shard_map/ppermute | solution.py:446
  (349 shorter events, 252.3 us)
Async XLA Ops:
  3.6 81.8 %collective-permute-start.16 = (bf16[256,256]{1,0:T(8,128)(2,1)}, bf16[256,256]{1,0:T(8,128)(2,1)}, u32[]{:S(2)}, u32[]{:S(2)}) collective-permute-start(bf16[256,256]{1,0:T(8,128)(2,1)} %get-tuple-element.59), channel_id=1, source_target_pairs={{0,4},{4,0},{8,12},{12,8},{16,20},{20,16},{24,28},{28,24},{1,5},{5... | collective-permute-start | bytes 393224 | tf_op jit(solution)/shard_map/ppermute | solution.py:446
  6.6 84.7 %collective-permute-start.19 = (bf16[256,256]{1,0:T(8,128)(2,1)}, bf16[256,256]{1,0:T(8,128)(2,1)}, u32[]{:S(2)}, u32[]{:S(2)}) collective-permute-start(bf16[256,256]{1,0:T(8,128)(2,1)} %get-tuple-element.59), channel_id=1, source_target_pairs={{0,16},{4,20},{8,24},{12,28},{16,0},{20,4},{24,8},{28,12},{1,17},{... | collective-permute-start | bytes 393224 | tf_op jit(solution)/shard_map/ppermute | solution.py:446
  9.2 91.4 %collective-permute-start.21 = (bf16[256,256]{1,0:T(8,128)(2,1)}, bf16[256,256]{1,0:T(8,128)(2,1)}, u32[]{:S(2)}, u32[]{:S(2)}) collective-permute-start(bf16[256,256]{1,0:T(8,128)(2,1)} %get-tuple-element.108), channel_id=1, source_target_pairs={{0,24},{4,28},{8,16},{12,20},{16,8},{20,12},{24,0},{28,4},{1,25},{... | collective-permute-start | bytes 393224 | tf_op jit(solution)/shard_map/ppermute | solution.py:446
  10.6 76.1 %collective-permute-start.17 = (bf16[256,256]{1,0:T(8,128)(2,1)}, bf16[256,256]{1,0:T(8,128)(2,1)}, u32[]{:S(2)}, u32[]{:S(2)}) collective-permute-start(bf16[256,256]{1,0:T(8,128)(2,1)} %get-tuple-element.108), channel_id=1, source_target_pairs={{0,8},{4,12},{8,0},{12,4},{16,24},{20,28},{24,16},{28,20},{1,9},{5... | collective-permute-start | bytes 393224 | tf_op jit(solution)/shard_map/ppermute | solution.py:446
  10.8 68.2 %collective-permute-start.8 = (s32[512]{0:T(512)}, s32[512]{0:T(512)}, u32[]{:S(2)}, u32[]{:S(2)}) collective-permute-start(s32[512]{0:T(512)} %param.21), channel_id=1, source_target_pairs={{0,8},{4,12},{8,0},{12,4},{16,24},{20,28},{24,16},{28,20},{1,9},{5... | collective-permute-start | bytes 6152 | tf_op jit(solution)/shard_map/ppermute | solution.py:446
  122.6 52.7 %collective-permute-start.2 = (bf16[256,768]{0,1:T(8,128)(2,1)S(1)}, bf16[256,768]{0,1:T(8,128)(2,1)S(1)}, u32[]{:S(2)}, u32[]{:S(2)}) collective-permute-start(bf16[256,768]{0,1:T(8,128)(2,1)S(1)} %collective-permute-done.1), channel_id=1, source_target_pairs={{0,4},{4,0},{8,12},{12,8},{16,20},{20,16},{24,28},{28,24},{1,5},{5... | collective-permute-start | bytes 1179656 | tf_op jit(solution)/shard_map/ppermute | solution.py:446
  135.7 71.8 %collective-permute-start.26 = (bf16[256,1024]{1,0:T(8,128)(2,1)S(1)}, bf16[256,1024]{1,0:T(8,128)(2,1)}, u32[]{:S(2)}, u32[]{:S(2)}) collective-permute-start(bf16[256,1024]{1,0:T(8,128)(2,1)S(1)} %copy-done.38), channel_id=1, source_target_pairs={{0,16},{4,20},{8,24},{12,28},{16,0},{20,4},{24,8},{28,12},{1,17},{... | collective-permute-start | bytes 1572872 | tf_op jit(solution)/shard_map/ppermute | solution.py:446
  141.7 67.4 %collective-permute-start.28 = (bf16[256,1024]{1,0:T(8,128)(2,1)S(1)}, bf16[256,1024]{1,0:T(8,128)(2,1)}, u32[]{:S(2)}, u32[]{:S(2)}) collective-permute-start(bf16[256,1024]{1,0:T(8,128)(2,1)S(1)} %copy-done.37), channel_id=1, source_target_pairs={{0,24},{4,28},{8,16},{12,20},{16,8},{20,12},{24,0},{28,4},{1,25},{... | collective-permute-start | bytes 1572872 | tf_op jit(solution)/shard_map/ppermute | solution.py:446
  149.7 143.1 %collective-permute-start.12 = (bf16[1024,256]{1,0:T(8,128)(2,1)}, bf16[1024,256]{1,0:T(8,128)(2,1)}, u32[]{:S(2)}, u32[]{:S(2)}) collective-permute-start(bf16[1024,256]{1,0:T(8,128)(2,1)} %get-tuple-element.55), channel_id=1, source_target_pairs={{0,16},{4,20},{8,24},{12,28},{16,0},{20,4},{24,8},{28,12},{1,17},{... | collective-permute-start | bytes 1572872 | tf_op jit(solution)/shard_map/ppermute | solution.py:446
  178.4 115.9 %collective-permute-start.14 = (bf16[1024,256]{1,0:T(8,128)(2,1)}, bf16[1024,256]{1,0:T(8,128)(2,1)}, u32[]{:S(2)}, u32[]{:S(2)}) collective-permute-start(bf16[1024,256]{1,0:T(8,128)(2,1)} %get-tuple-element.103), channel_id=1, source_target_pairs={{0,24},{4,28},{8,16},{12,20},{16,8},{20,12},{24,0},{28,4},{1,25},{... | collective-permute-start | bytes 1572872 | tf_op jit(solution)/shard_map/ppermute | solution.py:446
  207.5 87.3 %collective-permute-start.25 = (bf16[256,1024]{1,0:T(8,128)(2,1)}, bf16[256,1024]{1,0:T(8,128)(2,1)}, u32[]{:S(2)}, u32[]{:S(2)}) collective-permute-start(bf16[256,1024]{1,0:T(8,128)(2,1)} %collective-permute-done.24), channel_id=1, source_target_pairs={{0,4},{4,0},{8,12},{12,8},{16,20},{20,16},{24,28},{28,24},{1,5},{5... | collective-permute-start | bytes 1572872 | tf_op jit(solution)/shard_map/ppermute | solution.py:446
  209.0 91.2 %collective-permute-start.27 = (bf16[256,1024]{1,0:T(8,128)(2,1)}, bf16[256,1024]{1,0:T(8,128)(2,1)}, u32[]{:S(2)}, u32[]{:S(2)}) collective-permute-start(bf16[256,1024]{1,0:T(8,128)(2,1)} %collective-permute-done.26), channel_id=1, source_target_pairs={{0,4},{4,0},{8,12},{12,8},{16,20},{20,16},{24,28},{28,24},{1,5},{5... | collective-permute-start | bytes 1572872 | tf_op jit(solution)/shard_map/ppermute | solution.py:446
  209.6 94.5 %collective-permute-start.29 = (bf16[256,1024]{1,0:T(8,128)(2,1)}, bf16[256,1024]{1,0:T(8,128)(2,1)}, u32[]{:S(2)}, u32[]{:S(2)}) collective-permute-start(bf16[256,1024]{1,0:T(8,128)(2,1)} %collective-permute-done.28), channel_id=1, source_target_pairs={{0,4},{4,0},{8,12},{12,8},{16,20},{20,16},{24,28},{28,24},{1,5},{5... | collective-permute-start | bytes 1572872 | tf_op jit(solution)/shard_map/ppermute | solution.py:446
  435.5 63.1 %collective-permute-start.58 = (f32[2048]{0:T(1024)S(1)}, f32[2048]{0:T(1024)S(1)}, u32[]{:S(2)}, u32[]{:S(2)}) collective-permute-start(f32[2048]{0:T(1024)S(1)} %pad_select_fusion), channel_id=1, source_target_pairs={{0,4},{4,0},{8,12},{12,8},{16,20},{20,16},{24,28},{28,24},{1,5},{5... | collective-permute-start | bytes 24584 | tf_op jit(solution)/shard_map/ppermute | solution.py:446
  437.1 55.8 %collective-permute-start.49 = (f32[4,2048]{1,0:T(4,128)S(1)}, f32[4,2048]{1,0:T(4,128)S(1)}, u32[]{:S(2)}, u32[]{:S(2)}) collective-permute-start(f32[4,2048]{1,0:T(4,128)S(1)} %pad_maximum_fusion.9), channel_id=1, source_target_pairs={{0,4},{4,0},{8,12},{12,8},{16,20},{20,16},{24,28},{28,24},{1,5},{5... | collective-permute-start | bytes 98312 | tf_op jit(solution)/shard_map/ppermute | solution.py:446
  437.7 52.5 %collective-permute-start.42 = (f32[512]{0:T(512)S(1)}, f32[512]{0:T(512)S(1)}, u32[]{:S(2)}, u32[]{:S(2)}) collective-permute-start(f32[512]{0:T(512)S(1)} %pad_select_fusion.1), channel_id=1, source_target_pairs={{0,4},{4,0},{8,12},{12,8},{16,20},{20,16},{24,28},{28,24},{1,5},{5... | collective-permute-start | bytes 6152 | tf_op jit(solution)/shard_map/ppermute | solution.py:446
  441.9 48.8 %collective-permute-start.39 = (f32[512]{0:T(512)S(1)}, f32[512]{0:T(512)S(1)}, u32[]{:S(2)}, u32[]{:S(2)}) collective-permute-start(f32[512]{0:T(512)S(1)} %pad_select_fusion.2), channel_id=1, source_target_pairs={{0,4},{4,0},{8,12},{12,8},{16,20},{20,16},{24,28},{28,24},{1,5},{5... | collective-permute-start | bytes 6152 | tf_op jit(solution)/shard_map/ppermute | solution.py:446
  490.1 97.9 %collective-permute-start.35 = (bf16[1024,768]{1,0:T(8,128)(2,1)S(1)}, bf16[1024,768]{1,0:T(8,128)(2,1)S(1)}, u32[]{:S(2)}, u32[]{:S(2)}) collective-permute-start(bf16[1024,768]{1,0:T(8,128)(2,1)S(1)} %pad_maximum_fusion.4), channel_id=1, source_target_pairs={{0,4},{4,0},{8,12},{12,8},{16,20},{20,16},{24,28},{28,24},{1,5},{5... | collective-permute-start | bytes 4718600 | tf_op jit(solution)/shard_map/ppermute | solution.py:446
  506.1 117.6 %collective-permute-start.61 = (bf16[1024,1024]{1,0:T(8,128)(2,1)S(1)}, bf16[1024,1024]{1,0:T(8,128)(2,1)S(1)}, u32[]{:S(2)}, u32[]{:S(2)}) collective-permute-start(bf16[1024,1024]{1,0:T(8,128)(2,1)S(1)} %pad_maximum_fusion.2), channel_id=1, source_target_pairs={{0,4},{4,0},{8,12},{12,8},{16,20},{20,16},{24,28},{28,24},{1,5},{5... | collective-permute-start | bytes 6291464 | tf_op jit(solution)/shard_map/ppermute | solution.py:446
  512.2 71.5 %collective-permute-start.45 = (bf16[256,1024]{1,0:T(8,128)(2,1)S(1)}, bf16[256,1024]{1,0:T(8,128)(2,1)S(1)}, u32[]{:S(2)}, u32[]{:S(2)}) collective-permute-start(bf16[256,1024]{1,0:T(8,128)(2,1)S(1)} %pad_maximum_fusion.7), channel_id=1, source_target_pairs={{0,4},{4,0},{8,12},{12,8},{16,20},{20,16},{24,28},{28,24},{1,5},{5... | collective-permute-start | bytes 1572872 | tf_op jit(solution)/shard_map/ppermute | solution.py:446
  518.5 123.3 %collective-permute-start.54 = (bf16[1024,1024]{1,0:T(8,128)(2,1)}, bf16[1024,1024]{1,0:T(8,128)(2,1)}, u32[]{:S(2)}, u32[]{:S(2)}) collective-permute-start(bf16[1024,1024]{1,0:T(8,128)(2,1)} %pad_maximum_fusion), channel_id=1, source_target_pairs={{0,4},{4,0},{8,12},{12,8},{16,20},{20,16},{24,28},{28,24},{1,5},{5... | collective-permute-start | bytes 6291464 | tf_op jit(solution)/shard_map/ppermute | solution.py:446
  625.7 42.8 %collective-permute-start.62 = (bf16[1024,256]{1,0:T(8,128)(2,1)}, bf16[1024,256]{1,0:T(8,128)(2,1)}, u32[]{:S(2)}, u32[]{:S(2)}) collective-permute-start(bf16[1024,256]{1,0:T(8,128)(2,1)} %get-tuple-element.66), channel_id=1, source_target_pairs={{0,16},{4,20},{8,24},{12,28},{16,0},{20,4},{24,8},{28,12},{1,17},{... | collective-permute-start | bytes 1572872 | tf_op jit(solution)/shard_map/ppermute | solution.py:446
  644.2 66.4 %collective-permute-start.55 = (bf16[256,1024]{1,0:T(8,128)(2,1)S(1)}, bf16[256,1024]{1,0:T(8,128)(2,1)S(1)}, u32[]{:S(2)}, u32[]{:S(2)}) collective-permute-start(bf16[256,1024]{1,0:T(8,128)(2,1)S(1)} %get-tuple-element.69), channel_id=1, source_target_pairs={{0,16},{4,20},{8,24},{12,28},{16,0},{20,4},{24,8},{28,12},{1,17},{... | collective-permute-start | bytes 1572872 | tf_op jit(solution)/shard_map/ppermute | solution.py:446
  647.1 63.5 %collective-permute-start.57 = (bf16[256,1024]{1,0:T(8,128)(2,1)S(1)}, bf16[256,1024]{1,0:T(8,128)(2,1)S(1)}, u32[]{:S(2)}, u32[]{:S(2)}) collective-permute-start(bf16[256,1024]{1,0:T(8,128)(2,1)S(1)} %get-tuple-element.70), channel_id=1, source_target_pairs={{0,24},{4,28},{8,16},{12,20},{16,8},{20,12},{24,0},{28,4},{1,25},{... | collective-permute-start | bytes 1572872 | tf_op jit(solution)/shard_map/ppermute | solution.py:446
  (88 other events, 1880.6 us)

commit v3 on v2

v3 whole, which is shorter than its diff:
```python
import functools

import jax
import jax.numpy as jnp
from jax import lax
from jax.experimental import pallas as pl
from jax.experimental.pallas import tpu as pltpu
from jax.sharding import PartitionSpec as P

HEAD_DIM = 128
GROUP = 512
EPSILON = 1e-05
NEGATIVE = -1e30
LOW = jnp.bfloat16
F32 = jnp.float32


def gelu_parts(pre_act):
    cumulative = 0.5 * (1.0 + lax.erf(pre_act * 0.7071067811865476))
    density = jnp.exp(-0.5 * pre_act * pre_act) * 0.3989422804014327
    return cumulative, cumulative + pre_act * density


def heads_of(rows):
    return rows.reshape(-1, GROUP, rows.shape[1] // HEAD_DIM, HEAD_DIM)


def scores_of(query_heads, key_heads, segment, places):
    scores = jnp.einsum(
        "gqhd,gkhd->ghqk", query_heads, key_heads, preferred_element_type=F32
    ) * (HEAD_DIM**-0.5)
    allowed = (places[:, None, :] <= places[:, :, None]) & (
        (segment[:, None, :] == segment[:, :, None]) | (segment[:, None, :] == 0)
    )
    return jnp.where(allowed[:, None], scores, NEGATIVE)


def attend(queries, keys, values, segment, places):
    scores = scores_of(heads_of(queries), heads_of(keys), segment, places)
    row_max = jnp.max(scores, axis=3, keepdims=True)
    exp_terms = jnp.exp(scores - row_max)
    exp_total = jnp.sum(exp_terms, axis=3, keepdims=True)
    probs = (exp_terms / exp_total).astype(LOW)
    mixed = jnp.einsum("ghqk,gkhd->gqhd", probs, heads_of(values), preferred_element_type=F32)
    return mixed.astype(LOW).reshape(queries.shape), row_max + jnp.log(exp_total)


def attend_back(queries, keys, values, grad_att, segment, places, log_totals):
    scale_factor = HEAD_DIM**-0.5
    query_heads, key_heads, value_heads, grad_heads = map(heads_of, (queries, keys, values, grad_att))
    probs = jnp.exp(scores_of(query_heads, key_heads, segment, places) - log_totals)
    grad_probs = jnp.einsum("gqhd,gkhd->ghqk", grad_heads, value_heads, preferred_element_type=F32)
    row_delta = jnp.sum(probs * grad_probs, axis=3, keepdims=True)
    grad_scores = (probs * (grad_probs - row_delta)).astype(LOW)
    grad_query = jnp.einsum("ghqk,gkhd->gqhd", grad_scores, key_heads, preferred_element_type=F32)
    grad_key = jnp.einsum("ghqk,gqhd->gkhd", grad_scores, query_heads, preferred_element_type=F32)
    grad_value = jnp.einsum(
        "ghqk,gqhd->gkhd", probs.astype(LOW), grad_heads, preferred_element_type=F32
    )
    return (
        (grad_query * scale_factor).astype(LOW).reshape(queries.shape),
        (grad_key * scale_factor).astype(LOW).reshape(queries.shape),
        grad_value.astype(LOW).reshape(queries.shape),
    )


NC = 4
NW = 2
MESH = pl.DeviceIdType.MESH


def remote(src, dst, send, recv, peer):
    return pltpu.make_async_remote_copy(
        src_ref=src, dst_ref=dst, send_sem=send, recv_sem=recv, device_id=peer, device_id_type=MESH
    )


def grid_of(*shape):
    return pltpu.SemaphoreType.DMA(shape)


class Place:
    def __init__(self, dp_total):
        self.lines = dp_total // 2
        self.d = lax.axis_index("dp")
        self.t = lax.axis_index("tensor")
        self.lane, self.line = lax.rem(self.d, 2), lax.div(self.d, 2)
        self.side = lax.rem(self.line, 2)
        self.t_core = self.t + 1 - 2 * lax.rem(self.t, 2)
        self.t_x = lax.rem(self.t + 2, 4)
        self.t_far = lax.rem(self.t_core + 2, 4)
        self.core = (self.d, self.t_core)
        self.x = (self.d, self.t_x)
        self.y = (self.d + 1 - 2 * self.lane, self.t)
        self.z = (self.d + 2 - 4 * self.side, self.t)

    def ahead(self, k):
        return lax.rem(self.line + k, self.lines)

    def behind(self, k):
        return lax.rem(self.line + self.lines - k, self.lines)

    def mate(self, line):
        return (2 * line + self.lane, self.t)

    def greet(self):
        barrier = pltpu.get_barrier_semaphore()
        for peer in (self.core, self.x, self.y):
            pl.semaphore_signal(barrier, inc=1, device_id=peer, device_id_type=MESH)

        @pl.loop(1, self.lines)
        def _(k):
            pl.semaphore_signal(barrier, inc=1, device_id=self.mate(self.ahead(k)), device_id_type=MESH)

        pl.semaphore_wait(barrier, 2 + self.lines)


class Gather:
    SEMS = [grid_of(7, NC), grid_of(7, NC), grid_of(NC)]

    def __init__(self, me, own, whole, send, recv, keep):
        self.me, self.own, self.whole = me, own, whole
        self.send, self.recv, self.keep = send, recv, keep
        self.rows = own.shape[0] // NC

    def at(self, side, t, j):
        return self.whole.at[side, t, pl.ds(j * self.rows, self.rows)]

    def piece(self, j):
        return self.own.at[pl.ds(j * self.rows, self.rows)]

    def copy(self, kind, j, src, dst, peer):
        return remote(src, dst, self.send.at[kind, j], self.recv.at[kind, j], peer)

    def local(self, j):
        return pltpu.make_async_copy(self.piece(j), self.at(0, self.me.t, j), self.keep.at[j])

    def start(self, j):
        me = self.me
        self.copy(2, j, self.piece(j), self.at(1, me.t, j), me.z).start()
        self.copy(1, j, self.piece(j), self.at(0, me.t, j), me.x).start()
        self.copy(0, j, self.piece(j), self.at(0, me.t, j), me.core).start()
        self.local(j).start()

    def wait_recv(self, kind, j, side, t):
        slot = self.at(side, t, j)
        self.copy(kind, j, slot, slot, self.me.core).wait_recv()

    def share(self, kind, j, side, t):
        self.wait_recv(kind, j, side, t)
        slot = self.at(side, t, j)
        self.copy(kind + 3, j, slot, slot, self.me.core).start()

    def relay(self):
        me = self.me

        @pl.loop(0, NC)
        def _(j):
            self.share(2, j, 1, me.t)
            slot = self.at(1, me.t, j)
            self.copy(3, j, slot, slot, me.x).start()
            self.share(1, j, 0, me.t_x)

    def finish(self):
        me = self.me

        @pl.loop(0, NC)
        def _(j):
            self.share(3, j, 1, me.t_x)

        @pl.loop(0, NC)
        def _(j):
            self.wait_recv(0, j, 0, me.t_core)
            self.wait_recv(4, j, 0, me.t_far)
            self.wait_recv(5, j, 1, me.t_core)
            self.wait_recv(6, j, 1, me.t_far)
            self.local(j).wait()
            for kind in range(7):
                self.copy(kind, j, self.piece(j), self.piece(j), me.core).wait_send()


class Scatter:
    SEMS = [grid_of(4, NC), grid_of(4, NC), grid_of(4, NC), grid_of(3, NC), grid_of(3, NC)]

    @staticmethod
    def scratch(rows, width):
        return [pltpu.VMEM((n, rows, width), LOW) for n in (4, 4, 3)] + Scatter.SEMS

    def __init__(self, me, parts, held, came, hops, load, send, recv, hop_send, hop_recv):
        self.me, self.parts = me, parts
        self.held, self.came, self.hops = held, came, hops
        self.load, self.send, self.recv = load, send, recv
        self.hop_send, self.hop_recv = hop_send, hop_recv
        self.rows = held.shape[1] // NC
        self.pairs = [
            (0, me.t, me.t_core),
            (0, me.t_x, me.t_far),
            (1, me.t, me.t_core),
            (1, me.t_x, me.t_far),
        ]

    def span(self, j):
        return pl.ds(j * self.rows, self.rows)

    def core_copy(self, i, j):
        side, _, theirs = self.pairs[i]
        return remote(
            self.parts.at[side, theirs, self.span(j)],
            self.came.at[i, self.span(j)],
            self.send.at[i, j],
            self.recv.at[i, j],
            self.me.core,
        )

    def load_copy(self, i, j):
        side, mine, _ = self.pairs[i]
        return pltpu.make_async_copy(
            self.parts.at[side, mine, self.span(j)], self.held.at[i, self.span(j)], self.load.at[i, j]
        )

    def hop(self, kind, j, src, peer):
        return remote(
            src, self.hops.at[kind, self.span(j)], self.hop_send.at[kind, j], self.hop_recv.at[kind, j], peer
        )

    def start(self):
        for i in (3, 1, 2, 0):

            @pl.loop(0, NC)
            def _(j):
                self.core_copy(i, j).start()
                self.load_copy(i, j).start()

    def joined(self, i, j):
        self.load_copy(i, j).wait()
        self.core_copy(i, j).wait_recv()
        return self.held[i, self.span(j)].astype(F32) + self.came[i, self.span(j)].astype(F32)

    def arrived(self, kind, j):
        self.hop(kind, j, self.hops.at[kind, self.span(j)], self.me.x).wait_recv()
        return self.hops[kind, self.span(j)].astype(F32)

    def spread(self):
        for kind, i in ((0, 3), (1, 1)):

            @pl.loop(0, NC)
            def _(j):
                self.held[i, self.span(j)] = self.joined(i, j).astype(LOW)
                self.hop(kind, j, self.held.at[i, self.span(j)], self.me.x).start()

    def turn(self):
        @pl.loop(0, NC)
        def _(j):
            total = self.joined(2, j) + self.arrived(0, j)
            self.held[2, self.span(j)] = total.astype(LOW)
            self.hop(2, j, self.held.at[2, self.span(j)], self.me.z).start()

    def result(self, j):
        return self.joined(0, j) + self.arrived(1, j) + self.arrived(2, j)

    def finish(self):
        @pl.loop(0, NC)
        def _(j):
            for i in range(4):
                self.core_copy(i, j).wait_send()
            for kind in range(3):
                self.hop(kind, j, self.hops.at[kind, self.span(j)], self.me.x).wait_send()


def block_at(ref, owner, rows, width, first=0, count=None):
    count = rows if count is None else count
    if len(ref.shape) == 3:
        return ref.at[owner, pl.ds(first, count)]
    if ref.shape[0] == rows:
        return ref.at[pl.ds(first, count), pl.ds(pl.multiple_of(owner * width, width), width)]
    return ref.at[pl.ds(pl.multiple_of(owner * rows + first, count), count)]


class WeightGather:
    @staticmethod
    def sems(lines):
        return [grid_of(lines, NW), grid_of(lines, NW), grid_of(lines, NW), grid_of(lines, NW), grid_of(NW)]

    def __init__(self, me, halves, whole, z_send, z_recv, y_send, y_recv, keep):
        self.me, self.halves, self.whole = me, halves, whole
        self.z_send, self.z_recv, self.y_send, self.y_recv, self.keep = z_send, z_recv, y_send, y_recv, keep
        _, self.rows, self.width = halves.shape
        self.count = self.rows // NW

    def at(self, owner, p):
        return block_at(self.whole, owner, self.rows, self.width, p * self.count, self.count)

    def piece(self, half, p):
        return self.halves.at[half, pl.ds(p * self.count, self.count)]

    def z_copy(self, k, p, src, dst, peer):
        return remote(src, dst, self.z_send.at[k, p], self.z_recv.at[k, p], peer)

    def y_copy(self, k, p, src, dst):
        return remote(src, dst, self.y_send.at[k, p], self.y_recv.at[k, p], self.me.y)

    def local(self, p):
        return pltpu.make_async_copy(self.piece(self.me.side, p), self.at(self.me.d, p), self.keep.at[p])

    def start(self, p):
        me = self.me

        @pl.loop(1, me.lines)
        def _(k):
            line = me.ahead(k)
            self.z_copy(k, p, self.piece(lax.rem(line, 2), p), self.at(me.d, p), me.mate(line)).start()

        self.y_copy(0, p, self.piece(me.side, p), self.at(me.d, p)).start()
        self.local(p).start()

    def forward(self, p):
        me = self.me

        @pl.loop(1, me.lines)
        def _(k):
            slot = self.at(2 * me.behind(k) + me.lane, p)
            self.z_copy(k, p, slot, slot, me.y).wait_recv()
            self.y_copy(k, p, slot, slot).start()

    def finish(self):
        me = self.me
        for p in range(NW):

            @pl.loop(0, me.lines)
            def _(k):
                slot = self.at(2 * me.behind(k) + 1 - me.lane, p)
                self.y_copy(k, p, slot, slot).wait()

            @pl.loop(1, me.lines)
            def _(k):
                slot = self.at(me.d, p)
                self.z_copy(k, p, slot, slot, me.y).wait_send()

            self.local(p).wait()


class WeightScatter:
    @staticmethod
    def scratch(lines, rows, width):
        return [pltpu.VMEM((lines, rows, width), LOW)] * 3 + [grid_of(lines)] * 5

    def __init__(self, me, parts, held, came, hops, load, y_send, y_recv, z_send, z_recv):
        self.me, self.parts, self.held, self.came, self.hops = me, parts, held, came, hops
        self.load, self.y_send, self.y_recv, self.z_send, self.z_recv = load, y_send, y_recv, z_send, z_recv
        _, self.rows, self.width = held.shape
        self.step = 32

    def y_copy(self, k):
        src = block_at(self.parts, 2 * self.me.ahead(k) + 1 - self.me.lane, self.rows, self.width)
        return remote(src, self.came.at[k], self.y_send.at[k], self.y_recv.at[k], self.me.y)

    def load_copy(self, k):
        src = block_at(self.parts, 2 * self.me.ahead(k) + self.me.lane, self.rows, self.width)
        return pltpu.make_async_copy(src, self.held.at[k], self.load.at[k])

    def z_copy(self, k, peer):
        return remote(self.held.at[k], self.hops.at[k], self.z_send.at[k], self.z_recv.at[k], peer)

    def start(self):
        @pl.loop(1, self.me.lines + 1)
        def _(n):
            k = lax.rem(n, self.me.lines)
            self.y_copy(k).start()
            self.load_copy(k).start()

    def joined(self, k, at):
        return self.held[k, at].astype(F32) + self.came[k, at].astype(F32)

    def spread(self, first, last):
        @pl.loop(first, last)
        def _(k):
            self.load_copy(k).wait()
            self.y_copy(k).wait_recv()

            @pl.loop(0, self.rows, step=self.step)
            def _(row):
                at = pl.ds(row, self.step)
                self.held[k, at] = self.joined(k, at).astype(LOW)

            self.z_copy(k, self.me.mate(self.me.ahead(k))).start()

    def finish(self, store):
        me = self.me
        self.load_copy(0).wait()
        self.y_copy(0).wait_recv()

        @pl.loop(1, me.lines)
        def _(k):
            self.z_copy(k, me.y).wait_recv()

        @pl.loop(0, self.rows, step=self.step)
        def _(row):
            at = pl.ds(row, self.step)
            same, other = self.joined(0, at), self.hops[1, at].astype(F32)
            for k in range(2, me.lines):
                if k % 2:
                    other = other + self.hops[k, at].astype(F32)
                else:
                    same = same + self.hops[k, at].astype(F32)
            store(me.side, at, same)
            store(1 - me.side, at, other)

        @pl.loop(0, me.lines)
        def _(k):
            self.y_copy(k).wait_send()

        @pl.loop(1, me.lines)
        def _(k):
            self.z_copy(k, me.y).wait_send()


def store_columns(*outs):
    def store(half, at, value):
        width = outs[0].shape[1] // 2
        for n, out in enumerate(outs):
            out[at, pl.ds(pl.multiple_of(half * width, width), width)] = value[:, n * width : (n + 1) * width]

    return store


def store_rows(out):
    def store(half, at, value):
        out[pl.ds(pl.multiple_of(half * (out.shape[0] // 2) + at.start, at.size), at.size)] = value

    return store


class SumAll:
    @staticmethod
    def scratch(dp_total, width):
        steps = dp_total.bit_length() + 1
        return [pltpu.VMEM((steps + 1, 8, width), F32), pltpu.VMEM((steps, 8, width), F32), grid_of(steps), grid_of(steps)]

    def __init__(self, me, held, came, send, recv):
        self.me, self.held, self.came, self.send, self.recv = me, held, came, send, recv

    def run(self, shared):
        me, peers, mask = self.me, [], 1
        while mask < 2 * me.lines:
            peers.append((me.d + mask - 2 * mask * lax.rem(lax.div(me.d, mask), 2), me.t))
            mask *= 2
        dp_steps = len(peers)
        for n, peer in enumerate(peers + [me.core, me.x]):
            copy = remote(self.held.at[n], self.came.at[n], self.send.at[n], self.recv.at[n], peer)
            copy.start()
            copy.wait()
            total = self.held[n] + self.came[n]
            if n >= dp_steps:
                row = lax.broadcasted_iota(jnp.int32, total.shape, 0)
                total = jnp.where(row < shared, total, self.held[n])
            self.held[n + 1] = total
        return self.held[dp_steps + 2]


def unit_of(rows):
    centred = rows - jnp.mean(rows, axis=1, keepdims=True)
    inverse = lax.rsqrt(jnp.mean(centred * centred, axis=1, keepdims=True) + EPSILON)
    return centred * inverse, inverse


def back_of(grad_rows, unit_rows, inverse, gain):
    scaled = grad_rows * gain
    return inverse * (
        scaled
        - jnp.mean(scaled, axis=1, keepdims=True)
        - unit_rows * jnp.mean(scaled * unit_rows, axis=1, keepdims=True)
    )


def pieces(rows):
    size = rows // NC
    return lambda j: pl.ds(j * size, size)


class Cut:
    def __init__(self, refs):
        self.refs = list(refs)

    def take(self, count):
        taken, self.refs = self.refs[:count], self.refs[count:]
        return taken


def head_kernel(dp_total, x, gain, shift, grad, qkv, out, whole, whole_grad, qkv_whole, out_whole, own, own_grad, *scratch):
    me = Place(dp_total)
    at, cut = pieces(x.shape[0]), Cut(scratch)
    gather, gather_grad = Gather(me, own, whole, *cut.take(3)), Gather(me, own_grad, whole_grad, *cut.take(3))
    first, second = WeightGather(me, qkv, qkv_whole, *cut.take(5)), WeightGather(me, out, out_whole, *cut.take(5))
    me.greet()

    @pl.loop(0, NC)
    def _(j):
        unit_rows, _ = unit_of(x[at(j)])
        own[at(j)] = (unit_rows * gain[...] + shift[...]).astype(LOW)
        gather.start(j)

    for p in range(NW):
        first.start(p)

    @pl.loop(0, NC)
    def _(j):
        own_grad[at(j)] = grad[at(j)].astype(LOW)

    gather.relay()
    for p in range(NW):
        second.start(p)
    first.forward(0)
    gather.finish()

    @pl.loop(0, NC)
    def _(j):
        gather_grad.start(j)

    for p in range(1, NW):
        first.forward(p)
    for p in range(NW):
        second.forward(p)
    gather_grad.relay()
    gather_grad.finish()
    first.finish()
    second.finish()


def middle_kernel(dp_total, parts, base, gain, shift, up, down, resid, whole, up_whole, down_whole, own, *scratch):
    me = Place(dp_total)
    at, cut = pieces(base.shape[0]), Cut(scratch)
    scatter, gather = Scatter(me, parts, *cut.take(8)), Gather(me, own, whole, *cut.take(3))
    first, second = WeightGather(me, up, up_whole, *cut.take(5)), WeightGather(me, down, down_whole, *cut.take(5))
    me.greet()
    scatter.start()
    first.start(0)
    scatter.spread()
    scatter.turn()
    first.forward(0)

    @pl.loop(0, NC)
    def _(j):
        rows = base[at(j)] + scatter.result(j)
        resid[at(j)] = rows
        unit_rows, _ = unit_of(rows)
        own[at(j)] = (unit_rows * gain[...] + shift[...]).astype(LOW)
        gather.start(j)

    for p in range(1, NW):
        first.start(p)
    for p in range(NW):
        second.start(p)
    gather.relay()
    for p in range(1, NW):
        first.forward(p)
    gather.finish()
    for p in range(NW):
        second.forward(p)
    scatter.finish()
    first.finish()
    second.finish()


def turn_kernel(
    dp_total, parts, resid, grad, gain, down, up, grad_resid, whole, sums, down_done, up_done, own, *scratch
):
    me = Place(dp_total)
    at, cut = pieces(resid.shape[0]), Cut(scratch)
    scatter, gather = Scatter(me, parts, *cut.take(8)), Gather(me, own, whole, *cut.take(3))
    first, second = WeightScatter(me, down, *cut.take(8)), WeightScatter(me, up, *cut.take(8))
    lines = me.lines
    me.greet()
    scatter.start()
    first.start()
    second.start()
    scatter.spread()
    scatter.turn()
    first.spread(1, lines // 2)
    sums[...] = jnp.zeros_like(sums)

    @pl.loop(0, NC)
    def _(j):
        unit_rows, inverse = unit_of(resid[at(j)])
        e = scatter.result(j)
        rows = grad[at(j)] + back_of(e, unit_rows, inverse, gain[...])
        grad_resid[at(j)] = rows
        own[at(j)] = rows.astype(LOW)
        gather.start(j)
        sums[0:1] += jnp.sum(e * unit_rows, axis=0, keepdims=True)
        sums[1:2] += jnp.sum(e, axis=0, keepdims=True)
        sums[2:3] += jnp.sum(rows, axis=0, keepdims=True)
        sums[3:4] += jnp.sum(grad[at(j)], axis=0, keepdims=True)

    first.spread(lines // 2, lines)
    gather.relay()
    gather.finish()
    scatter.finish()
    second.spread(1, lines)
    first.finish(store_rows(down_done))
    second.finish(store_columns(up_done))


def tail_kernel(
    dp_total, parts, lowered, x, gain, grad_resid, base, early, out, qkv,
    grad_inputs, output, sums, out_done, query_done, key_done, value_done, *scratch,
):
    me = Place(dp_total)
    at, cut = pieces(x.shape[0]), Cut(scratch)
    scatter, other = Scatter(me, parts, *cut.take(8)), Scatter(me, lowered, *cut.take(8))
    first, second = WeightScatter(me, out, *cut.take(8)), WeightScatter(me, qkv, *cut.take(8))
    vectors = SumAll(me, *cut.take(4))
    me.greet()
    scatter.start()
    second.start()
    first.start()
    scatter.spread()
    scatter.turn()
    vectors.held[0] = early[...]
    other.start()
    second.spread(1, me.lines)

    @pl.loop(0, NC)
    def _(j):
        unit_rows, inverse = unit_of(x[at(j)])
        e = scatter.result(j)
        grad_inputs[at(j)] = grad_resid[at(j)] + back_of(e, unit_rows, inverse, gain[...])
        vectors.held[0, 0:1] += jnp.sum(e * unit_rows, axis=0, keepdims=True)
        vectors.held[0, 1:2] += jnp.sum(e, axis=0, keepdims=True)

    sums[...] = vectors.run(6)
    scatter.finish()
    other.spread()
    other.turn()
    first.spread(1, me.lines)

    @pl.loop(0, NC)
    def _(j):
        output[at(j)] = base[at(j)] + other.result(j)

    other.finish()
    second.finish(store_columns(query_done, key_done, value_done))
    first.finish(store_rows(out_done))


VMEM = pl.BlockSpec(memory_space=pltpu.VMEM)
ANY = pl.BlockSpec(memory_space=pl.ANY)


def call(kernel, number, ins, in_specs, outs, out_specs, scratch):
    return pl.pallas_call(
        functools.partial(kernel, lax.axis_size("dp")),
        out_shape=outs,
        in_specs=in_specs,
        out_specs=out_specs,
        scratch_shapes=scratch,
        compiler_params=pltpu.CompilerParams(
            collective_id=number, has_side_effects=True, vmem_limit_bytes=48 << 20
        ),
        cost_estimate=pl.CostEstimate(flops=0, bytes_accessed=100_000_000, transcendentals=0),
    )(*ins)


def like(*shape, dtype=F32):
    return jax.ShapeDtypeStruct(shape, dtype)


def local(
    inputs,
    grad_output,
    seg_ids,
    positions,
    norm1_gain,
    norm1_bias,
    query_weight,
    query_bias,
    key_weight,
    value_weight,
    value_bias,
    out_weight,
    out_bias,
    norm2_gain,
    norm2_bias,
    up_weight,
    up_bias,
    down_weight,
    down_bias,
):
    dp_total = lax.axis_size("dp")
    tensor_total = lax.axis_size("tensor")
    lines = dp_total // 2
    place = lax.axis_index("dp")
    side = (place >> 1) & 1

    def hop(rows, mask):
        return lax.ppermute(rows, "dp", [(i, i ^ mask) for i in range(dp_total)])

    def own_half(vector):
        return lax.dynamic_slice_in_dim(vector, side * (vector.shape[0] // 2), vector.shape[0] // 2, 0)

    def column_halves(*weights):
        cut = [w.astype(LOW).reshape(w.shape[0], 2, -1) for w in weights]
        return jnp.concatenate(cut, 2).transpose(1, 0, 2)

    def row_halves(weight):
        return weight.astype(LOW).reshape(2, -1, weight.shape[1])

    def mm(left, right):
        return jnp.dot(left, right, preferred_element_type=F32)

    def mm_nt(left, right):
        return jnp.einsum("td,fd->tf", left, right, preferred_element_type=F32)

    def mm_tn(left, right):
        return jnp.einsum("ta,tb->ab", left, right, preferred_element_type=F32)

    rows, width = inputs.shape
    row = lambda vector: vector.reshape(1, -1)
    group = like(2, tensor_total, rows, width, dtype=LOW)
    own = pltpu.VMEM((rows, width), LOW)
    token_scratch = Scatter.scratch(rows, width)

    def whole_rows(halves):
        return like(dp_total * halves.shape[1], halves.shape[2], dtype=LOW)

    def whole_columns(halves):
        _, high, wide = halves.shape
        return like(*((dp_total, high, wide) if wide % 128 else (high, dp_total * wide)), dtype=LOW)

    def side_by_side(whole):
        return whole if whole.ndim == 2 else whole.transpose(1, 0, 2).reshape(whole.shape[1], -1)

    def column_blocks(partial):
        wide = partial.shape[1] // dp_total
        return partial.reshape(-1, dp_total, wide).transpose(1, 0, 2) if wide % 128 else partial

    segment = jnp.stack([seg_ids, hop(seg_ids, 2)]).reshape(-1, GROUP)
    places = jnp.stack([positions, hop(positions, 2)]).reshape(-1, GROUP)
    qkv_halves = column_halves(query_weight, key_weight, value_weight)
    out_halves, up_halves, down_halves = row_halves(out_weight), column_halves(up_weight), row_halves(down_weight)

    whole1, grad_whole, qkv_full, o_full = call(
        head_kernel, 1,
        (inputs, row(norm1_gain), row(norm1_bias), grad_output, qkv_halves, out_halves), [VMEM] * 6,
        (group, group, whole_rows(qkv_halves), whole_columns(out_halves)), (ANY,) * 4,
        [own, own] + Gather.SEMS * 2 + WeightGather.sems(lines) * 2,
    )
    whole1, grad_whole, o_full = whole1.reshape(-1, width), grad_whole.reshape(-1, width), side_by_side(o_full)
    halves = query_bias.shape[0] // 2
    qkv = mm(whole1, qkv_full)
    queries = (qkv[:, :halves] + own_half(query_bias)).astype(LOW)
    keys = qkv[:, halves : 2 * halves].astype(LOW)
    values = (qkv[:, 2 * halves :] + own_half(value_bias)).astype(LOW)
    attended, log_totals = attend(queries, keys, values, segment, places)

    def as_group(partial):
        return partial.astype(LOW).reshape(group.shape)

    resid, whole2, up_full, down_full = call(
        middle_kernel, 2,
        (as_group(mm(attended, o_full)), inputs + out_bias, row(norm2_gain), row(norm2_bias), up_halves, down_halves),
        [ANY] + [VMEM] * 5,
        (like(rows, width), group, whole_rows(up_halves), whole_columns(down_halves)), (VMEM, ANY, ANY, ANY),
        [own] + token_scratch + Gather.SEMS + WeightGather.sems(lines) * 2,
    )
    whole2, down_full = whole2.reshape(-1, width), side_by_side(down_full)
    pre_act = mm(whole2, up_full) + own_half(up_bias)
    cumulative, slope = gelu_parts(pre_act)
    activated = (pre_act * cumulative).astype(LOW)
    grad_down = column_blocks(mm_tn(activated, grad_whole).astype(LOW))
    lowered = as_group(mm(activated, down_full))
    grad_pre = (mm_nt(grad_whole, down_full) * slope).astype(LOW)
    grad_up = mm_tn(whole2, grad_pre).astype(LOW)

    grad_resid, grad_mixed, sums2, down_done, up_done = call(
        turn_kernel, 3,
        (as_group(mm_nt(grad_pre, up_full)), resid, grad_output, row(norm2_gain), grad_down, grad_up),
        [ANY] + [VMEM] * 3 + [ANY] * 2,
        (like(rows, width), group, like(8, width), like(*down_weight.shape), like(*up_weight.shape)),
        (VMEM, ANY, VMEM, VMEM, VMEM),
        [own] + token_scratch + Gather.SEMS
        + WeightScatter.scratch(lines, *down_halves.shape[1:]) + WeightScatter.scratch(lines, *up_halves.shape[1:]),
    )
    grad_mixed = grad_mixed.reshape(-1, width)
    grad_out = column_blocks(mm_tn(attended, grad_mixed).astype(LOW))
    grad_att = mm_nt(grad_mixed, o_full).astype(LOW)
    grad_queries, grad_keys, grad_values = attend_back(
        queries, keys, values, grad_att, segment, places, log_totals
    )
    grad_qkv = jnp.concatenate([grad_queries, grad_keys, grad_values], 1)
    grad_qkv_w = mm_tn(whole1, grad_qkv).astype(LOW)

    def column_sums(values):
        half = jnp.sum(values.astype(F32), axis=0)
        return jnp.where(side == jnp.arange(2)[:, None], half, 0.0).reshape(-1)

    heads = jnp.concatenate([column_sums(grad_queries), column_sums(grad_values)])
    early = jnp.concatenate(
        [
            jnp.zeros((2, width), F32),
            sums2[:4],
            row(jnp.pad(column_sums(grad_pre), (0, width - 2 * grad_pre.shape[1]))),
            row(jnp.pad(heads, (0, width - heads.shape[0]))),
        ]
    )
    grad_inputs, layer_output, sums, out_done, query_done, key_done, value_done = call(
        tail_kernel, 4,
        (
            as_group(mm_nt(grad_qkv, qkv_full)), lowered, inputs, row(norm1_gain), grad_resid, resid + down_bias, early,
            grad_out, grad_qkv_w,
        ),
        [ANY] * 2 + [VMEM] * 5 + [ANY] * 2,
        (
            like(rows, width), like(rows, width), like(8, width), like(*out_weight.shape),
            *[like(*query_weight.shape)] * 3,
        ),
        (VMEM,) * 7,
        token_scratch * 2
        + WeightScatter.scratch(lines, *out_halves.shape[1:]) + WeightScatter.scratch(lines, *qkv_halves.shape[1:])
        + SumAll.scratch(dp_total, width),
    )
    return (
        layer_output,
        grad_inputs,
        sums[0],
        sums[1],
        query_done,
        sums[7, : 2 * halves],
        key_done,
        value_done,
        sums[7, 2 * halves : 4 * halves],
        out_done,
        sums[4],
        sums[2],
        sums[3],
        up_done,
        sums[6, : up_bias.shape[0]],
        down_done,
        sums[5],
    )


def solution(mesh):
    tokens, weight, weight_t = P(("dp", "tensor"), None), P("dp", "tensor"), P("tensor", "dp")
    whole, part = P(), P("tensor")
    return jax.shard_map(
        local,
        mesh=mesh,
        in_specs=(
            tokens, tokens, P("dp"), P("dp"), whole, whole, weight, part, weight, weight, part,
            weight_t, whole, whole, whole, weight, part, weight_t, whole,
        ),
        out_specs=(
            tokens, tokens, whole, whole, weight, part, weight, weight, part, weight_t, whole,
            whole, whole, weight, part, weight_t, whole,
        ),
        check_vma=False,
    )
```

time: 728 us -> 537 us (0.74); the launches traced: 716 us -> 533 us
  Pallas kernels: 181 us -> 404 us
  waiting for transfers between devices: 219 us -> 0.01 us
  starting transfers between devices: 115 us -> 3.2 us
  local copies, waits for them, and re-layouts: 87.1 us -> 35 us
  other arithmetic: 33.8 us -> 8.98 us
    pallas_call x4, Pallas kernels: 181 us -> 404 us  [call(): pl.pallas_call(functools.partial(kernel, lax.axis_size('dp')), out_shape=...]
    ppermute x61 -> x2, waiting for transfers between devices: 217 us -> 0.01 us  [hop(): return lax.ppermute(rows, 'dp', [(i, i ^ mask) for i in range(dp_total)])]
    ppermute x61 -> x2, starting transfers between devices: 112 us -> 3.2 us  [hop(): return lax.ppermute(rows, 'dp', [(i, i ^ mask) for i in range(dp_total)])]
    dynamic_update_slice x31 -> x0, local copies, waits for them, and re-layouts: 33.4 us -> none  [gather_weight(): whole = lax.dynamic_update_slice(whole, block, tuple(start))]
    concatenate x8 -> x2, other arithmetic: 8.74 us -> 0.09 us  [the longest x1 0.08 us: local(): jnp.concatenate([jnp.zeros((2, width), F32), sums2[:4], row(jnp.pad(colum...]
    unnamed x104 -> x85, local copies, waits for them, and re-layouts: 13 us -> 15 us
  transfers between devices with their start and end apart: 65 -> 2, of which waited for: 20 -> 0; matrix products, arithmetic and copies ran while one was open for 17% -> 6% of each run, Pallas kernels for 19% -> 13%
where the time goes in v3:
time: 537 us; the launch traced here: 533 us
  Pallas kernels  404 us (75%)
  matrix products  80.5 us (15%)
  local copies, waits for them, and re-layouts  35 us (7%)
  other arithmetic  8.98 us (2%)
    pallas_call x4, Pallas kernels, call(): pl.pallas_call(functools.partial(kernel, lax.axis_size('dp')), out_shape=...  404 us
    dot_general x4, matrix products, mm(): return jnp.dot(left, right, preferred_element_type=F32)  25.7 us
    dot_general x4, matrix products, mm_tn(): return jnp.einsum('ta,tb->ab', left, right, preferred_element_type=F32)  22.4 us
    dot_general x4, matrix products, mm_nt(): return jnp.einsum('td,fd->tf', left, right, preferred_element_type=F32)  22.2 us
    unnamed x85, local copies, waits for them, and re-layouts  15 us
  transfers between devices with their start and end apart: 2, of which 0 were waited for; matrix products, arithmetic and copies ran while one was open for 6% of the time, Pallas kernels for 13%

profile of v3, /device:TPU:0, one launch (start us, length us, event | category | flops | bytes accessed | tf_op | source)
XLA Modules:
  0.0 532.7 jit_solution(6499620537050081991)
XLA Ops:
  0.7 3.1 collective-permute-start.1
  11.7 69.8 %shard_map.314 = (bf16[2,4,128,2048]{3,2,1,0:T(8,128)(2,1)}, bf16[2,4,128,2048]{3,2,1,0:T(8,128)(2,1)}, bf16[2048,768]{1,0:T(8,128)(2,1)}, bf16[256,2048]{1,0:T(8,128)(2,1)S(1)}) custom-call(f32[128,2048]{1,0:T(8,128)S(1)} %copy-done, f32[1,2048]{1,0:T(1,128)S(1)} %bitcast.107, f32[1,2048]{1,0:T(1,128)S(1)} %bitcast.111, f32[128,2048]{1,0:T(8,128)S(1)} %copy-done.1, ...), custom_call_target="tpu_custom_call" | custom-call | bytes 100000000 | tf_op jit(solution)/shard_map/pallas_call | solution.py:650
  81.5 6.5 %fusion.36 = f32[1024,768]{1,0:T(8,128)S(1)} fusion(bf16[1024,2048]{1,0:T(8,128)(2,1)} %bitcast.147, bf16[2048,768]{1,0:T(8,128)(2,1)} %get-tuple-element.38), kind=kOutput, calls=%fused_computation.75 | convolution fusion | flops 3221225472 | bytes 10485760 | tf_op jit(solution)/shard_map/dot_general | solution.py:708
  94.8 2.0 reshape.215
  96.8 2.0 reshape.212
  98.7 2.0 copy.63
  102.7 2.0 copy.66
  105.5 2.3 fusion.35
  111.6 2.0 copy.58
  113.6 4.8 convolution_convert_fusion
  118.4 112.6 %shard_map.315 = (f32[128,2048]{1,0:T(8,128)S(1)}, bf16[2,4,128,2048]{3,2,1,0:T(8,128)(2,1)}, bf16[2048,1024]{1,0:T(8,128)(2,1)}, bf16[1024,2048]{1,0:T(8,128)(2,1)}) custom-call(bf16[2,4,128,2048]{3,2,1,0:T(8,128)(2,1)} %bitcast.113, f32[128,2048]{1,0:T(8,128)S(1)} %copy-done.2, f32[1,2048]{1,0:T(1,128)S(1)} %bitcast.109, f32[1,2048]{1,0:T(1,128)S(1)} %bitcast.112, ...), custom_call_target="tpu_custom_call" | custom-call | bytes 100000000 | tf_op jit(solution)/shard_map/pallas_call | solution.py:650
  231.0 8.3 %multiply_convert_fusion.1 = (bf16[1024,1024]{1,0:T(8,128)(2,1)S(1)}, f32[1024,1024]{1,0:T(8,128)S(1)}) fusion(f32[1024]{0:T(1024)S(1)} %dynamic_slice.11, bf16[1024,2048]{1,0:T(8,128)(2,1)} %bitcast.151, bf16[2048,1024]{1,0:T(8,128)(2,1)} %get-tuple-element.43), kind=kOutput, calls=%fused_computation.10 | convolution fusion | flops 4301258752 | bytes 14684160 | tf_op jit(solution)/shard_map/dot_general | solution.py:708
  239.4 6.4 %convert_reduce_fusion = (f32[1024]{0:T(1024)S(1)}, bf16[1024,1024]{1,0:T(8,128)(2,1)S(1)}) fusion(f32[1024,1024]{1,0:T(8,128)S(1)} %get-tuple-element.73, f32[1024]{0:T(1024)S(1)} %dynamic_slice.11, bf16[1024,2048]{1,0:T(8,128)(2,1)S(1)} %bitcast.149, bf16[1024,2048]{1,0:T(8,128)(2,1)S(1)} %copy-done.29), kind=kOutput, calls=%fused_computation.7 | convolution fusion | flops 4308597760 | bytes 14688256 | tf_op jit(solution)/shard_map/td,fd->tf/dot_general | solution.py:711
  245.8 6.2 %convolution_convert_fusion.3.up = bf16[2048,1024]{1,0:T(8,128)(2,1)} fusion(bf16[1024,2048]{1,0:T(8,128)(2,1)S(1)} %bitcast.152, bf16[1024,1024]{1,0:T(8,128)(2,1)S(1)} %get-tuple-element.81), kind=kOutput, calls=%fused_computation.19 | convolution fusion | flops 4297064448 | bytes 10485760 | tf_op jit(solution)/shard_map/ta,tb->ab/dot_general | solution.py:714
  252.0 6.1 %convolution_convert_fusion.5 = bf16[1024,2048]{1,0:T(8,128)(2,1)} fusion(bf16[1024,1024]{1,0:T(8,128)(2,1)S(1)} %get-tuple-element.81, bf16[2048,1024]{1,0:T(8,128)(2,1)S(1)} %copy-done.30), kind=kOutput, calls=%fused_computation.21 | convolution fusion | flops 4297064448 | bytes 10485760 | tf_op jit(solution)/shard_map/td,fd->tf/dot_general | solution.py:711
  258.2 6.1 %convolution_convert_fusion.2 = bf16[1024,2048]{1,0:T(8,128)(2,1)} fusion(bf16[1024,1024]{1,0:T(8,128)(2,1)S(1)} %get-tuple-element.72, bf16[1024,2048]{1,0:T(8,128)(2,1)S(1)} %copy-done.29), kind=kOutput, calls=%fused_computation.18 | convolution fusion | flops 4297064448 | bytes 10485760 | tf_op jit(solution)/shard_map/dot_general | solution.py:708
  264.3 6.3 %convolution_convert_fusion.4.down = bf16[1024,2048]{1,0:T(8,128)(2,1)} fusion(bf16[1024,1024]{1,0:T(8,128)(2,1)S(1)} %get-tuple-element.72, bf16[1024,2048]{1,0:T(8,128)(2,1)S(1)} %bitcast.150), kind=kOutput, calls=%fused_computation.20 | convolution fusion | flops 4297064448 | bytes 10485760 | tf_op jit(solution)/shard_map/ta,tb->ab/dot_general | solution.py:714
  270.5 118.3 %shard_map.316 = (f32[128,2048]{1,0:T(8,128)S(1)}, bf16[2,4,128,2048]{3,2,1,0:T(8,128)(2,1)}, f32[8,2048]{1,0:T(8,128)S(1)}, f32[2048,256]{1,0:T(8,128)S(1)}, f32[256,2048]{1,0:T(8,128)}) custom-call(bf16[2,4,128,2048]{3,2,1,0:T(8,128)(2,1)} %bitcast.116, f32[128,2048]{1,0:T(8,128)S(1)} %get-tuple-element.44.resid, f32[128,2048]{1,0:T(8,128)S(1)} %copy-done.1, ...), custom_call_target="tpu_custom_call" | custom-call | bytes 100000000 | tf_op jit(solution)/shard_map/pallas_call | solution.py:650
  388.9 4.6 convolution_convert_fusion.8
  393.6 2.3 convolution_convert_fusion.7.out
  396.4 3.3 convert_reduce_fusion.1
  406.5 7.6 %convolution_convert_fusion.6.qkv = bf16[2048,768]{1,0:T(8,128)(2,1)} fusion(bf16[1024,2048]{1,0:T(8,128)(2,1)} %bitcast.148, bf16[1024,768]{1,0:T(8,128)(2,1)S(1)} %bitcast_dynamic-update-slice_fusion), kind=kOutput, calls=%fused_computation.23 | convolution fusion | flops 3222798336 | bytes 8912896 | tf_op jit(solution)/shard_map/ta,tb->ab/dot_general | solution.py:714
  414.1 5.0 convolution_convert_fusion.1
  420.6 102.9 %shard_map.317 = (f32[128,2048]{1,0:T(8,128)S(1)}, f32[128,2048]{1,0:T(8,128)S(1)}, f32[8,2048]{1,0:T(8,128)S(1)}, f32[512,256]{1,0:T(8,128)S(1)}, f32[256,512]{...) custom-call(bf16[2,4,128,2048]{3,2,1,0:T(8,128)(2,1)} %bitcast.115, ...), custom_call_target="tpu_custom_call" | custom-call | bytes 100000000 | tf_op jit(solution)/shard_map/pallas_call | solution.py:650
  (130 shorter events, 38.8 us)
Async XLA Ops:
  0.7 9.9 %copy-start = (f32[128,2048]{1,0:T(8,128)S(1)}, f32[128,2048]{1,0:T(8,128)}, u32[]{:S(2)}) copy-start(f32[128,2048]{1,0:T(8,128)} %x.5) | copy-start | bytes 3145732
  0.7 9.9 %copy-start.23 = (f32[2048]{0:T(1024)S(1)}, f32[2048]{0:T(1024)}, u32[]{:S(2)}) copy-start(f32[2048]{0:T(1024)} %param.31) | copy-start | bytes 24580
  0.7 104.0 %collective-permute-start.1 = (s32[512]{0:T(512)}, s32[512]{0:T(512)S(1)}, u32[]{:S(2)}, u32[]{:S(2)}) collective-permute-start(s32[512]{0:T(512)} %param.21), channel_id=1, source_target_pairs={{0,8},{4,12},{8,0},{12,4},{16,24},{20,28},{24,16},{28,20},{1,9},{5... | collective-permute-start | bytes 6152 | tf_op jit(solution)/shard_map/ppermute | solution.py:695
  3.8 101.0 %collective-permute-start = (s32[512]{0:T(512)}, s32[512]{0:T(512)S(1)}, u32[]{:S(2)}, u32[]{:S(2)}) collective-permute-start(s32[512]{0:T(512)} %param.22), channel_id=1, source_target_pairs={{0,8},{4,12},{8,0},{12,4},{16,24},{20,28},{24,16},{28,20},{1,9},{5... | collective-permute-start | bytes 6152 | tf_op jit(solution)/shard_map/ppermute | solution.py:695
  5.4 6.3 %copy-start.1 = (f32[128,2048]{1,0:T(8,128)S(1)}, f32[128,2048]{1,0:T(8,128)}, u32[]{:S(2)}) copy-start(f32[128,2048]{1,0:T(8,128)} %grad.3) | copy-start | bytes 3145732
  5.4 6.3 %copy-start.11 = (f32[2048]{0:T(1024)S(1)}, f32[2048]{0:T(1024)}, u32[]{:S(2)}) copy-start(f32[2048]{0:T(1024)} %param.23) | copy-start | bytes 24580
  5.4 6.3 %copy-start.13 = (f32[2048]{0:T(1024)S(1)}, f32[2048]{0:T(1024)}, u32[]{:S(2)}) copy-start(f32[2048]{0:T(1024)} %param.24) | copy-start | bytes 24580
  81.4 6.5 %copy-start.9 = (bf16[256,2048]{1,0:T(8,128)(2,1)}, bf16[256,2048]{1,0:T(8,128)(2,1)S(1)}, u32[]{:S(2)}) copy-start(bf16[256,2048]{1,0:T(8,128)(2,1)S(1)} %get-tuple-element.40) | copy-start | bytes 3145732
  93.1 11.6 %copy-start.26 = (f32[2048]{0:T(1024)S(1)}, f32[2048]{0:T(1024)}, u32[]{:S(2)}) copy-start(f32[2048]{0:T(1024)} %param.35) | copy-start | bytes 24580
  93.1 11.7 %copy-start.25 = (s32[512]{0:T(512)S(1)}, s32[512]{0:T(512)}, u32[]{:S(2)}) copy-start(s32[512]{0:T(512)} %param.21) | copy-start | bytes 6148
  93.1 11.7 %copy-start.27 = (s32[512]{0:T(512)S(1)}, s32[512]{0:T(512)}, u32[]{:S(2)}) copy-start(s32[512]{0:T(512)} %param.22) | copy-start | bytes 6148
  113.6 4.8 copy-start.5
  113.6 4.8 copy-start.12
  113.6 4.8 copy-start.14
  231.0 39.5 %copy-start.3 = (f32[128,2048]{1,0:T(8,128)}, f32[128,2048]{1,0:T(8,128)S(1)}, u32[]{:S(2)}) copy-start(f32[128,2048]{1,0:T(8,128)S(1)} %get-tuple-element.44.resid) | copy-start | bytes 3145732
  231.0 8.4 %copy-start.28 = (bf16[2,4,128,2048]{3,2,1,0:T(8,128)(2,1)S(1)}, bf16[2,4,128,2048]{3,2,1,0:T(8,128)(2,1)}, u32[]{:S(2)}) copy-start(bf16[2,4,128,2048]{3,2,1,0:T(8,128)(2,1)} %get-tuple-element.39) | copy-start | bytes 12582916
  231.0 8.4 %copy-start.29 = (bf16[1024,2048]{1,0:T(8,128)(2,1)S(1)}, bf16[1024,2048]{1,0:T(8,128)(2,1)}, u32[]{:S(2)}) copy-start(bf16[1024,2048]{1,0:T(8,128)(2,1)} %get-tuple-element.41) | copy-start | bytes 12582916
  239.4 6.4 %copy-start.31 = (bf16[2,4,128,2048]{3,2,1,0:T(8,128)(2,1)S(1)}, bf16[2,4,128,2048]{3,2,1,0:T(8,128)(2,1)}, u32[]{:S(2)}) copy-start(bf16[2,4,128,2048]{3,2,1,0:T(8,128)(2,1)} %get-tuple-element.42) | copy-start | bytes 12582916
  245.8 6.3 %copy-start.30 = (bf16[2048,1024]{1,0:T(8,128)(2,1)S(1)}, bf16[2048,1024]{1,0:T(8,128)(2,1)}, u32[]{:S(2)}) copy-start(bf16[2048,1024]{1,0:T(8,128)(2,1)} %get-tuple-element.43) | copy-start | bytes 12582916
  270.5 118.3 %copy-start.10 = (bf16[256,2048]{1,0:T(8,128)(2,1)S(1)}, bf16[256,2048]{1,0:T(8,128)(2,1)}, u32[]{:S(2)}) copy-start(bf16[256,2048]{1,0:T(8,128)(2,1)} %copy-done.9) | copy-start | bytes 3145732
  406.5 7.6 %copy-start.33 = (bf16[2048,768]{1,0:T(8,128)(2,1)S(1)}, bf16[2048,768]{1,0:T(8,128)(2,1)}, u32[]{:S(2)}) copy-start(bf16[2048,768]{1,0:T(8,128)(2,1)} %get-tuple-element.38) | copy-start | bytes 9437188
  414.1 5.1 copy-start.4
  414.1 5.1 copy-start.24
  524.7 5.1 copy-start.22
  (12 other events, 45.1 us)

commit v4 on v3

--- a/solution.py
+++ b/solution.py
@@ -19,49 +19,6 @@
     cumulative = 0.5 * (1.0 + lax.erf(pre_act * 0.7071067811865476))
     density = jnp.exp(-0.5 * pre_act * pre_act) * 0.3989422804014327
     return cumulative, cumulative + pre_act * density
-
-
-def heads_of(rows):
-    return rows.reshape(-1, GROUP, rows.shape[1] // HEAD_DIM, HEAD_DIM)
-
-
-def scores_of(query_heads, key_heads, segment, places):
-    scores = jnp.einsum(
-        "gqhd,gkhd->ghqk", query_heads, key_heads, preferred_element_type=F32
-    ) * (HEAD_DIM**-0.5)
-    allowed = (places[:, None, :] <= places[:, :, None]) & (
-        (segment[:, None, :] == segment[:, :, None]) | (segment[:, None, :] == 0)
-    )
-    return jnp.where(allowed[:, None], scores, NEGATIVE)
-
-
-def attend(queries, keys, values, segment, places):
-    scores = scores_of(heads_of(queries), heads_of(keys), segment, places)
-    row_max = jnp.max(scores, axis=3, keepdims=True)
-    exp_terms = jnp.exp(scores - row_max)
-    exp_total = jnp.sum(exp_terms, axis=3, keepdims=True)
-    probs = (exp_terms / exp_total).astype(LOW)
-    mixed = jnp.einsum("ghqk,gkhd->gqhd", probs, heads_of(values), preferred_element_type=F32)
-    return mixed.astype(LOW).reshape(queries.shape), row_max + jnp.log(exp_total)
-
-
-def attend_back(queries, keys, values, grad_att, segment, places, log_totals):
-    scale_factor = HEAD_DIM**-0.5
-    query_heads, key_heads, value_heads, grad_heads = map(heads_of, (queries, keys, values, grad_att))
-    probs = jnp.exp(scores_of(query_heads, key_heads, segment, places) - log_totals)
-    grad_probs = jnp.einsum("gqhd,gkhd->ghqk", grad_heads, value_heads, preferred_element_type=F32)
-    row_delta = jnp.sum(probs * grad_probs, axis=3, keepdims=True)
-    grad_scores = (probs * (grad_probs - row_delta)).astype(LOW)
-    grad_query = jnp.einsum("ghqk,gkhd->gqhd", grad_scores, key_heads, preferred_element_type=F32)
-    grad_key = jnp.einsum("ghqk,gqhd->gkhd", grad_scores, query_heads, preferred_element_type=F32)
-    grad_value = jnp.einsum(
-        "ghqk,gqhd->gkhd", probs.astype(LOW), grad_heads, preferred_element_type=F32
-    )
-    return (
-        (grad_query * scale_factor).astype(LOW).reshape(queries.shape),
-        (grad_key * scale_factor).astype(LOW).reshape(queries.shape),
-        grad_value.astype(LOW).reshape(queries.shape),
-    )
 
 
 NC = 4
@@ -313,18 +270,18 @@
         self.y_copy(0, p, self.piece(me.side, p), self.at(me.d, p)).start()
         self.local(p).start()
 
-    def forward(self, p):
+    def forward(self, p, first=1, last=None):
         me = self.me
 
-        @pl.loop(1, me.lines)
+        @pl.loop(first, me.lines if last is None else last)
         def _(k):
             slot = self.at(2 * me.behind(k) + me.lane, p)
             self.z_copy(k, p, slot, slot, me.y).wait_recv()
             self.y_copy(k, p, slot, slot).start()
 
-    def finish(self):
+    def finish(self, *which):
         me = self.me
-        for p in range(NW):
+        for p in which:
 
             @pl.loop(0, me.lines)
             def _(k):
@@ -486,12 +443,113 @@
         return taken
 
 
-def head_kernel(dp_total, x, gain, shift, grad, qkv, out, whole, whole_grad, qkv_whole, out_whole, own, own_grad, *scratch):
+NN, NT, TN = ((1,), (0,)), ((1,), (1,)), ((0,), (0,))
+
+
+def dot(left, right, dims):
+    return lax.dot_general(left, right, (dims, ((), ())), preferred_element_type=F32)
+
+
+def column_halves(halves, *weights):
+    width = weights[0].shape[1] // 2
+    for n, weight in enumerate(weights):
+        for half in range(2):
+            halves[half, :, n * width : (n + 1) * width] = weight[:, half * width : (half + 1) * width].astype(LOW)
+
+
+def row_halves(halves, weight):
+    rows = weight.shape[0] // 2
+    for half in range(2):
+        halves[half] = weight[half * rows : (half + 1) * rows].astype(LOW)
+
+
+def turned_halves(halves, weight):
+    rows = weight.shape[0] // 2
+    for half in range(2):
+        halves[half] = weight[half * rows : (half + 1) * rows].T.astype(LOW)
+
+
+def fill_mask(mask, infos, turned):
+    @pl.loop(0, 2)
+    def _(side):
+        across = infos[side].astype(F32)
+        down = across.T
+        seg_row, pos_row, seg_col, pos_col = down[:, 0:1], down[:, 1:2], across[0:1], across[1:2]
+        if turned:
+            seg_q, pos_q, seg_k, pos_k = seg_col, pos_col, seg_row, pos_row
+        else:
+            seg_q, pos_q, seg_k, pos_k = seg_row, pos_row, seg_col, pos_col
+        allowed = (pos_k <= pos_q) & ((seg_k == seg_q) | (seg_k == 0.0))
+        mask[side] = jnp.where(allowed, 0.0, NEGATIVE).astype(LOW)
+
+
+def heads_of(width):
+    return [slice(n * HEAD_DIM, (n + 1) * HEAD_DIM) for n in range(width // HEAD_DIM)]
+
+
+def attend(queries, keys, values, mask, attended, between):
+    group = mask.shape[1]
+    part = group // 2
+    for side in range(2):
+        for head in heads_of(queries.shape[1]):
+            all_rows = pl.ds(side * group, group)
+
+            @pl.loop(0, 2)
+            def _(r):
+                at = pl.ds(side * group + r * part, part)
+                scores = dot(queries[at, head], keys[all_rows, head], NT) * (HEAD_DIM**-0.5)
+                scores = scores + mask[side, pl.ds(r * part, part)].astype(F32)
+                terms = jnp.exp(scores - jnp.max(scores, axis=1, keepdims=True))
+                probs = (terms / jnp.sum(terms, axis=1, keepdims=True)).astype(LOW)
+                attended[at, head] = dot(probs, values[all_rows, head], NN).astype(LOW)
+
+            between()
+
+
+def attend_back(queries, keys, values, grads, mask, grad_qkv, between):
+    group, width = mask.shape[1], queries.shape[1]
+    part = group // 2
+    scale = HEAD_DIM**-0.5
+    for side in range(2):
+        for n, head in enumerate(heads_of(width)):
+            rows = pl.ds(side * group, group)
+            grad_key, grad_value = 0.0, 0.0
+            for r in range(2):
+                at = pl.ds(side * group + r * part, part)
+                scores = dot(keys[rows, head], queries[at, head], NT) * scale
+                scores = scores + mask[side, :, r * part : (r + 1) * part].astype(F32)
+                terms = jnp.exp(scores - jnp.max(scores, axis=0, keepdims=True))
+                probs = terms / jnp.sum(terms, axis=0, keepdims=True)
+                grad_probs = dot(values[rows, head], grads[at, head], NT)
+                delta = jnp.sum(probs * grad_probs, axis=0, keepdims=True)
+                grad_scores = (probs * (grad_probs - delta)).astype(LOW)
+                grad_value = grad_value + dot(probs.astype(LOW), grads[at, head], NN)
+                grad_key = grad_key + dot(grad_scores, queries[at, head], NN)
+                grad_query = dot(grad_scores, keys[rows, head], TN)
+                grad_qkv[at, n * HEAD_DIM : (n + 1) * HEAD_DIM] = (grad_query * scale).astype(LOW)
+            for m, value in ((1, grad_key * scale), (2, grad_value)):
+                grad_qkv[rows, m * width + n * HEAD_DIM : m * width + (n + 1) * HEAD_DIM] = value.astype(LOW)
+            between()
+
+
+def column_blocks_of(width, size=256):
+    return lambda n: pl.ds(pl.multiple_of(n * size, size), size)
+
+
+def head_kernel(
+    dp_total, x, gain, shift, grad, query, key, value, out, up, query_bias, value_bias, info,
+    whole_out, whole_grad, qkv_out, o_out, up_out, parts, queries, keys, values, attended, infos,
+    own, own_grad, whole, qkv_half, out_half, up_half, qkv_whole, o_whole, mask, *scratch,
+):
     me = Place(dp_total)
     at, cut = pieces(x.shape[0]), Cut(scratch)
     gather, gather_grad = Gather(me, own, whole, *cut.take(3)), Gather(me, own_grad, whole_grad, *cut.take(3))
-    first, second = WeightGather(me, qkv, qkv_whole, *cut.take(5)), WeightGather(me, out, out_whole, *cut.take(5))
+    first, second = WeightGather(me, qkv_half, qkv_whole, *cut.take(5)), WeightGather(me, out_half, o_whole, *cut.take(5))
+    third = WeightGather(me, up_half, up_out, *cut.take(5))
+    (save,) = cut.take(1)
     me.greet()
+    info_copy = remote(info, infos.at[1], save.at[0], save.at[1], me.z)
+    info_copy.start()
 
     @pl.loop(0, NC)
     def _(j):
@@ -499,82 +557,134 @@
         own[at(j)] = (unit_rows * gain[...] + shift[...]).astype(LOW)
         gather.start(j)
 
+    column_halves(qkv_half, query, key, value)
     for p in range(NW):
         first.start(p)
+    turned_halves(out_half, out)
+    for p in range(NW):
+        second.start(p)
+    column_halves(up_half, up)
 
     @pl.loop(0, NC)
     def _(j):
         own_grad[at(j)] = grad[at(j)].astype(LOW)
 
+    info_copy.wait()
+    infos[0] = info[...]
+    fill_mask(mask, infos, False)
     gather.relay()
-    for p in range(NW):
-        second.start(p)
     first.forward(0)
     gather.finish()
+    third.start(0)
+    first.forward(1)
 
     @pl.loop(0, NC)
     def _(j):
         gather_grad.start(j)
 
-    for p in range(1, NW):
-        first.forward(p)
-    for p in range(NW):
-        second.forward(p)
+    save_whole = pltpu.make_async_copy(whole, whole_out, save.at[2])
+    save_whole.start()
+    second.forward(0)
+    second.forward(1)
+    first.finish(0, 1)
+    save_qkv = pltpu.make_async_copy(qkv_whole, qkv_out, save.at[3])
+    save_qkv.start()
+    group = mask.shape[1]
+    width = queries.shape[1]
+
+    @pl.loop(0, 2)
+    def _(side):
+        rows = pl.ds(pl.multiple_of(side * group, group), group)
+        tokens = whole[side].reshape(group, -1)
+        for n, (result, bias) in enumerate(((queries, query_bias), (keys, None), (values, value_bias))):
+            total = dot(tokens, qkv_whole[:, n * width : (n + 1) * width], NN)
+            result[rows] = (total if bias is None else total + bias[...]).astype(LOW)
+
     gather_grad.relay()
+    steps = iter(((1, 2), (2, 3), (3, None)) if me.lines == 4 else ((1, None),))
+
+    def between():
+        span = next(steps, None)
+        if span:
+            third.forward(0, *span)
+
+    attend(queries, keys, values, mask, attended, between)
+    second.finish(0, 1)
+    save_o = pltpu.make_async_copy(o_whole, o_out, save.at[4])
+    save_o.start()
+    block = column_blocks_of(x.shape[1])
+
+    @pl.loop(0, x.shape[1] // 256)
+    def _(n):
+        total = dot(attended[...], o_whole[pl.ds(pl.multiple_of(n * 256, 256), 256)], NT)
+        parts[:, :, :, block(n)] = total.astype(LOW).reshape(*parts.shape[:3], 256)
+
     gather_grad.finish()
-    first.finish()
-    second.finish()
-
-
-def middle_kernel(dp_total, parts, base, gain, shift, up, down, resid, whole, up_whole, down_whole, own, *scratch):
+    third.finish(0)
+    for copy in (save_whole, save_qkv, save_o):
+        copy.wait()
+
+
+def middle_kernel(
+    dp_total, parts, x, out_bias, gain, shift, up, down, up_part,
+    resid, whole, up_whole, down_whole, own, up_half, down_half, *scratch,
+):
     me = Place(dp_total)
-    at, cut = pieces(base.shape[0]), Cut(scratch)
+    at, cut = pieces(x.shape[0]), Cut(scratch)
     scatter, gather = Scatter(me, parts, *cut.take(8)), Gather(me, own, whole, *cut.take(3))
-    first, second = WeightGather(me, up, up_whole, *cut.take(5)), WeightGather(me, down, down_whole, *cut.take(5))
+    first, second = WeightGather(me, up_half, up_whole, *cut.take(5)), WeightGather(me, down_half, down_whole, *cut.take(5))
     me.greet()
     scatter.start()
-    first.start(0)
+    column_halves(up_half, up)
+    first.start(1)
     scatter.spread()
     scatter.turn()
-    first.forward(0)
+    row_halves(down_half, down)
+    first.forward(1)
 
     @pl.loop(0, NC)
     def _(j):
-        rows = base[at(j)] + scatter.result(j)
+        rows = x[at(j)] + scatter.result(j) + out_bias[...]
         resid[at(j)] = rows
         unit_rows, _ = unit_of(rows)
         own[at(j)] = (unit_rows * gain[...] + shift[...]).astype(LOW)
         gather.start(j)
 
-    for p in range(1, NW):
-        first.start(p)
     for p in range(NW):
         second.start(p)
     gather.relay()
-    for p in range(1, NW):
-        first.forward(p)
     gather.finish()
     for p in range(NW):
         second.forward(p)
     scatter.finish()
-    first.finish()
-    second.finish()
+    first.finish(1)
+    second.finish(0, 1)
 
 
 def turn_kernel(
-    dp_total, parts, resid, grad, gain, down, up, grad_resid, whole, sums, down_done, up_done, own, *scratch
+    dp_total, parts, lowered, resid, grad, gain, down_bias, down, whole2, grad_pre, o_whole,
+    queries, keys, values, attended, infos,
+    grad_resid, output, sums, down_done, up_done, grad_qkv, grad_out,
+    own, whole, mask, grad_att, grad_up, *scratch,
 ):
     me = Place(dp_total)
     at, cut = pieces(resid.shape[0]), Cut(scratch)
-    scatter, gather = Scatter(me, parts, *cut.take(8)), Gather(me, own, whole, *cut.take(3))
-    first, second = WeightScatter(me, down, *cut.take(8)), WeightScatter(me, up, *cut.take(8))
+    scatter, other = Scatter(me, parts, *cut.take(8)), Scatter(me, lowered, *cut.take(8))
+    gather = Gather(me, own, whole, *cut.take(3))
+    first, second = WeightScatter(me, down, *cut.take(8)), WeightScatter(me, grad_up, *cut.take(8))
     lines = me.lines
+    block = column_blocks_of(resid.shape[1])
     me.greet()
     scatter.start()
     first.start()
-    second.start()
     scatter.spread()
     scatter.turn()
+
+    @pl.loop(0, grad_up.shape[0] // 256)
+    def _(n):
+        grad_up[pl.ds(pl.multiple_of(n * 256, 256), 256)] = dot(whole2[:, block(n)], grad_pre[...], TN).astype(LOW)
+
+    second.start()
     first.spread(1, lines // 2)
     sums[...] = jnp.zeros_like(sums)
 
@@ -591,33 +701,71 @@
         sums[2:3] += jnp.sum(rows, axis=0, keepdims=True)
         sums[3:4] += jnp.sum(grad[at(j)], axis=0, keepdims=True)
 
+    fill_mask(mask, infos, True)
     first.spread(lines // 2, lines)
     gather.relay()
     gather.finish()
+    other.start()
+    other.spread()
+    mixed = whole[...].reshape(-1, whole.shape[3])
+    grad_att[...] = dot(mixed, o_whole[...], NN).astype(LOW)
+    steps = iter(((1, 2), (2, 3), (3, 4)) if lines == 4 else ((1, lines),))
+
+    def between():
+        span = next(steps, None)
+        if span:
+            second.spread(*span)
+
+    attend_back(queries, keys, values, grad_att, mask, grad_qkv, between)
+    sums[4:5, : grad_qkv.shape[1]] = jnp.sum(grad_qkv[...].astype(F32), axis=0, keepdims=True)
+    other.turn()
+
+    @pl.loop(0, resid.shape[1] // 256)
+    def _(n):
+        columns = whole[:, :, :, block(n)].reshape(-1, 256)
+        grad_out[:, block(n)] = dot(attended[...], columns, TN).astype(LOW)
+
+    first.finish(store_rows(down_done))
+
+    @pl.loop(0, NC)
+    def _(j):
+        output[at(j)] = resid[at(j)] + other.result(j) + down_bias[...]
+
     scatter.finish()
-    second.spread(1, lines)
-    first.finish(store_rows(down_done))
+    other.finish()
     second.finish(store_columns(up_done))
 
 
 def tail_kernel(
-    dp_total, parts, lowered, x, gain, grad_resid, base, early, out, qkv,
-    grad_inputs, output, sums, out_done, query_done, key_done, value_done, *scratch,
+    dp_total, x, gain, grad_resid, early, out, whole, grad_qkv, qkv_whole,
+    grad_inputs, sums, out_done, query_done, key_done, value_done,
+    qkv, parts, *scratch,
 ):
     me = Place(dp_total)
     at, cut = pieces(x.shape[0]), Cut(scratch)
-    scatter, other = Scatter(me, parts, *cut.take(8)), Scatter(me, lowered, *cut.take(8))
+    scatter = Scatter(me, parts, *cut.take(8))
     first, second = WeightScatter(me, out, *cut.take(8)), WeightScatter(me, qkv, *cut.take(8))
     vectors = SumAll(me, *cut.take(4))
+    block = column_blocks_of(x.shape[1])
     me.greet()
+    first.start()
+
+    @pl.loop(0, qkv.shape[0] // 256)
+    def _(n):
+        qkv[pl.ds(pl.multiple_of(n * 256, 256), 256)] = dot(whole[:, block(n)], grad_qkv[...], TN).astype(LOW)
+
+    second.start()
+
+    @pl.loop(0, x.shape[1] // 256)
+    def _(n):
+        total = dot(grad_qkv[...], qkv_whole[pl.ds(pl.multiple_of(n * 256, 256), 256)], NT)
+        parts[:, :, :, block(n)] = total.astype(LOW).reshape(*parts.shape[:3], 256)
+
     scatter.start()
-    second.start()
-    first.start()
     scatter.spread()
+    first.spread(1, me.lines)
     scatter.turn()
     vectors.held[0] = early[...]
-    other.start()
-    second.spread(1, me.lines)
 
     @pl.loop(0, NC)
     def _(j):
@@ -627,34 +775,27 @@
         vectors.held[0, 0:1] += jnp.sum(e * unit_rows, axis=0, keepdims=True)
         vectors.held[0, 1:2] += jnp.sum(e, axis=0, keepdims=True)
 
+    second.spread(1, me.lines)
     sums[...] = vectors.run(6)
     scatter.finish()
-    other.spread()
-    other.turn()
-    first.spread(1, me.lines)
-
-    @pl.loop(0, NC)
-    def _(j):
-        output[at(j)] = base[at(j)] + other.result(j)
-
-    other.finish()
+    first.finish(store_rows(out_done))
     second.finish(store_columns(query_done, key_done, value_done))
-    first.finish(store_rows(out_done))
 
 
 VMEM = pl.BlockSpec(memory_space=pltpu.VMEM)
 ANY = pl.BlockSpec(memory_space=pl.ANY)
 
 
-def call(kernel, number, ins, in_specs, outs, out_specs, scratch):
+def call(kernel, number, ins, in_specs, outs, out_specs, scratch, aliases=None):
     return pl.pallas_call(
         functools.partial(kernel, lax.axis_size("dp")),
         out_shape=outs,
         in_specs=in_specs,
         out_specs=out_specs,
         scratch_shapes=scratch,
+        input_output_aliases=aliases or {},
         compiler_params=pltpu.CompilerParams(
-            collective_id=number, has_side_effects=True, vmem_limit_bytes=48 << 20
+            collective_id=number, has_side_effects=True, vmem_limit_bytes=60 << 20
         ),
         cost_estimate=pl.CostEstimate(flops=0, bytes_accessed=100_000_000, transcendentals=0),
     )(*ins)
@@ -691,18 +832,8 @@
     place = lax.axis_index("dp")
     side = (place >> 1) & 1
 
-    def hop(rows, mask):
-        return lax.ppermute(rows, "dp", [(i, i ^ mask) for i in range(dp_total)])
-
     def own_half(vector):
         return lax.dynamic_slice_in_dim(vector, side * (vector.shape[0] // 2), vector.shape[0] // 2, 0)
-
-    def column_halves(*weights):
-        cut = [w.astype(LOW).reshape(w.shape[0], 2, -1) for w in weights]
-        return jnp.concatenate(cut, 2).transpose(1, 0, 2)
-
-    def row_halves(weight):
-        return weight.astype(LOW).reshape(2, -1, weight.shape[1])
 
     def mm(left, right):
         return jnp.dot(left, right, preferred_element_type=F32)
@@ -719,103 +850,105 @@
     own = pltpu.VMEM((rows, width), LOW)
     token_scratch = Scatter.scratch(rows, width)
 
-    def whole_rows(halves):
-        return like(dp_total * halves.shape[1], halves.shape[2], dtype=LOW)
-
-    def whole_columns(halves):
-        _, high, wide = halves.shape
-        return like(*((dp_total, high, wide) if wide % 128 else (high, dp_total * wide)), dtype=LOW)
+    slab = lambda *shape: pltpu.VMEM(shape, LOW)
+    head_width, hidden = query_weight.shape[1] // 2, up_weight.shape[1] // 2
+    high, wide = up_weight.shape[0], down_weight.shape[1]
+    tokens = 2 * tensor_total * rows
 
     def side_by_side(whole):
         return whole if whole.ndim == 2 else whole.transpose(1, 0, 2).reshape(whole.shape[1], -1)
 
     def column_blocks(partial):
-        wide = partial.shape[1] // dp_total
         return partial.reshape(-1, dp_total, wide).transpose(1, 0, 2) if wide % 128 else partial
 
-    segment = jnp.stack([seg_ids, hop(seg_ids, 2)]).reshape(-1, GROUP)
-    places = jnp.stack([positions, hop(positions, 2)]).reshape(-1, GROUP)
-    qkv_halves = column_halves(query_weight, key_weight, value_weight)
-    out_halves, up_halves, down_halves = row_halves(out_weight), column_halves(up_weight), row_halves(down_weight)
-
-    whole1, grad_whole, qkv_full, o_full = call(
+    info = jnp.pad(jnp.stack([seg_ids, positions]), ((0, 6), (0, 0)))
+    heads = like(tokens, head_width, dtype=LOW)
+
+    whole1, grad_whole, qkv_full, o_full, up_part, parts, queries, keys, values, attended, infos = call(
         head_kernel, 1,
-        (inputs, row(norm1_gain), row(norm1_bias), grad_output, qkv_halves, out_halves), [VMEM] * 6,
-        (group, group, whole_rows(qkv_halves), whole_columns(out_halves)), (ANY,) * 4,
-        [own, own] + Gather.SEMS * 2 + WeightGather.sems(lines) * 2,
+        (
+            inputs, row(norm1_gain), row(norm1_bias), grad_output, query_weight, key_weight, value_weight, out_weight,
+            up_weight, row(own_half(query_bias)), row(own_half(value_bias)), info,
+        ),
+        [VMEM] * 12,
+        (
+            group, group, like(width, 3 * head_width, dtype=LOW), like(width, head_width, dtype=LOW),
+            like(width, hidden, dtype=LOW), group, heads, heads, heads, heads, like(2, *info.shape, dtype=jnp.int32),
+        ),
+        (ANY,) * 5 + (VMEM,) * 6,
+        [
+            own, own, slab(*group.shape), slab(2, high, 3 * head_width), slab(2, wide, head_width),
+            slab(2, high, hidden), slab(width, 3 * head_width), slab(width, head_width), slab(2, GROUP, GROUP),
+        ]
+        + Gather.SEMS * 2 + WeightGather.sems(lines) * 3 + [grid_of(5)],
     )
-    whole1, grad_whole, o_full = whole1.reshape(-1, width), grad_whole.reshape(-1, width), side_by_side(o_full)
-    halves = query_bias.shape[0] // 2
-    qkv = mm(whole1, qkv_full)
-    queries = (qkv[:, :halves] + own_half(query_bias)).astype(LOW)
-    keys = qkv[:, halves : 2 * halves].astype(LOW)
-    values = (qkv[:, 2 * halves :] + own_half(value_bias)).astype(LOW)
-    attended, log_totals = attend(queries, keys, values, segment, places)
-
-    def as_group(partial):
-        return partial.astype(LOW).reshape(group.shape)
-
     resid, whole2, up_full, down_full = call(
         middle_kernel, 2,
-        (as_group(mm(attended, o_full)), inputs + out_bias, row(norm2_gain), row(norm2_bias), up_halves, down_halves),
-        [ANY] + [VMEM] * 5,
-        (like(rows, width), group, whole_rows(up_halves), whole_columns(down_halves)), (VMEM, ANY, ANY, ANY),
-        [own] + token_scratch + Gather.SEMS + WeightGather.sems(lines) * 2,
+        (parts, inputs, row(out_bias), row(norm2_gain), row(norm2_bias), up_weight, down_weight, up_part),
+        [ANY] + [VMEM] * 6 + [ANY],
+        (
+            like(rows, width), group, like(width, hidden, dtype=LOW),
+            like(*((dp_total, hidden, wide) if wide % 128 else (hidden, width)), dtype=LOW),
+        ),
+        (VMEM, ANY, ANY, ANY),
+        [own, slab(2, high, hidden), slab(2, hidden, wide)]
+        + token_scratch + Gather.SEMS + WeightGather.sems(lines) * 2,
+        {7: 2},
     )
+    grad_whole = grad_whole.reshape(-1, width)
     whole2, down_full = whole2.reshape(-1, width), side_by_side(down_full)
     pre_act = mm(whole2, up_full) + own_half(up_bias)
     cumulative, slope = gelu_parts(pre_act)
     activated = (pre_act * cumulative).astype(LOW)
     grad_down = column_blocks(mm_tn(activated, grad_whole).astype(LOW))
-    lowered = as_group(mm(activated, down_full))
+    lowered = mm(activated, down_full).astype(LOW).reshape(group.shape)
     grad_pre = (mm_nt(grad_whole, down_full) * slope).astype(LOW)
-    grad_up = mm_tn(whole2, grad_pre).astype(LOW)
-
-    grad_resid, grad_mixed, sums2, down_done, up_done = call(
+    grad_parts = mm_nt(grad_pre, up_full).astype(LOW).reshape(group.shape)
+
+    grad_resid, layer_output, sums2, down_done, up_done, grad_qkv, grad_out = call(
         turn_kernel, 3,
-        (as_group(mm_nt(grad_pre, up_full)), resid, grad_output, row(norm2_gain), grad_down, grad_up),
-        [ANY] + [VMEM] * 3 + [ANY] * 2,
-        (like(rows, width), group, like(8, width), like(*down_weight.shape), like(*up_weight.shape)),
-        (VMEM, ANY, VMEM, VMEM, VMEM),
-        [own] + token_scratch + Gather.SEMS
-        + WeightScatter.scratch(lines, *down_halves.shape[1:]) + WeightScatter.scratch(lines, *up_halves.shape[1:]),
+        (
+            grad_parts, lowered, resid, grad_output, row(norm2_gain), row(down_bias), grad_down, whole2, grad_pre, o_full,
+            queries, keys, values, attended, infos,
+        ),
+        [ANY] * 2 + [VMEM] * 4 + [ANY] + [VMEM] * 8,
+        (
+            like(rows, width), like(rows, width), like(8, width), like(*down_weight.shape), like(*up_weight.shape),
+            like(tokens, 3 * head_width, dtype=LOW), like(head_width, width, dtype=LOW),
+        ),
+        (VMEM,) * 7,
+        [own, slab(*group.shape), slab(2, GROUP, GROUP), slab(tokens, head_width), slab(width, hidden)]
+        + token_scratch * 2 + Gather.SEMS
+        + WeightScatter.scratch(lines, hidden, wide) + WeightScatter.scratch(lines, high, hidden),
     )
-    grad_mixed = grad_mixed.reshape(-1, width)
-    grad_out = column_blocks(mm_tn(attended, grad_mixed).astype(LOW))
-    grad_att = mm_nt(grad_mixed, o_full).astype(LOW)
-    grad_queries, grad_keys, grad_values = attend_back(
-        queries, keys, values, grad_att, segment, places, log_totals
-    )
-    grad_qkv = jnp.concatenate([grad_queries, grad_keys, grad_values], 1)
-    grad_qkv_w = mm_tn(whole1, grad_qkv).astype(LOW)
-
-    def column_sums(values):
-        half = jnp.sum(values.astype(F32), axis=0)
+
+    def spread(half):
         return jnp.where(side == jnp.arange(2)[:, None], half, 0.0).reshape(-1)
 
-    heads = jnp.concatenate([column_sums(grad_queries), column_sums(grad_values)])
+    def padded(vector):
+        return row(jnp.pad(vector, (0, width - vector.shape[0])))
+
+    biases = [spread(sums2[4, n * head_width : (n + 1) * head_width]) for n in (0, 2)]
     early = jnp.concatenate(
         [
             jnp.zeros((2, width), F32),
             sums2[:4],
-            row(jnp.pad(column_sums(grad_pre), (0, width - 2 * grad_pre.shape[1]))),
-            row(jnp.pad(heads, (0, width - heads.shape[0]))),
+            padded(spread(jnp.sum(grad_pre.astype(F32), axis=0))),
+            padded(jnp.concatenate(biases)),
         ]
     )
-    grad_inputs, layer_output, sums, out_done, query_done, key_done, value_done = call(
+    grad_inputs, sums, out_done, query_done, key_done, value_done = call(
         tail_kernel, 4,
         (
-            as_group(mm_nt(grad_qkv, qkv_full)), lowered, inputs, row(norm1_gain), grad_resid, resid + down_bias, early,
-            grad_out, grad_qkv_w,
+            inputs, row(norm1_gain), grad_resid, early, column_blocks(grad_out), whole1.reshape(-1, width), grad_qkv,
+            qkv_full,
         ),
-        [ANY] * 2 + [VMEM] * 5 + [ANY] * 2,
-        (
-            like(rows, width), like(rows, width), like(8, width), like(*out_weight.shape),
-            *[like(*query_weight.shape)] * 3,
-        ),
-        (VMEM,) * 7,
-        token_scratch * 2
-        + WeightScatter.scratch(lines, *out_halves.shape[1:]) + WeightScatter.scratch(lines, *qkv_halves.shape[1:])
+        [VMEM] * 4 + [ANY] + [VMEM] * 3,
+        (like(rows, width), like(8, width), like(*out_weight.shape), *[like(*query_weight.shape)] * 3),
+        (VMEM,) * 6,
+        [slab(width, 3 * head_width), slab(*group.shape)]
+        + token_scratch
+        + WeightScatter.scratch(lines, head_width, wide) + WeightScatter.scratch(lines, high, 3 * head_width)
         + SumAll.scratch(dp_total, width),
     )
     return (
@@ -824,10 +957,10 @@
         sums[0],
         sums[1],
         query_done,
-        sums[7, : 2 * halves],
+        sums[7, : 2 * head_width],
         key_done,
         value_done,
-        sums[7, 2 * halves : 4 * halves],
+        sums[7, 2 * head_width : 4 * head_width],
         out_done,
         sums[4],
         sums[2],

time: 537 us -> 483 us (0.90)
  matrix products: 80.5 us -> 32.9 us
  Pallas kernels: 404 us -> 429 us
  local copies, waits for them, and re-layouts: 35 us -> 18 us
  other arithmetic: 8.98 us -> 1.58 us
    pallas_call x4, Pallas kernels: 404 us -> 429 us  [call(): pl.pallas_call(functools.partial(kernel, lax.axis_size('dp')), out_shape=...]
    dot_general x4 -> x1, matrix products: 22.4 us -> 6.24 us  [mm_tn(): return jnp.einsum('ta,tb->ab', left, right, preferred_element_type=F32)]
    reshape x11 -> x0, local copies, waits for them, and re-layouts: 12.1 us -> none  [the longest x7 10.4 us: heads_of(): return rows.reshape(-1, GROUP, rows.shape[1] // HEAD_DIM, HEAD_DIM)]
    dot_general x4 -> x2, matrix products: 25.7 us -> 14.2 us  [mm(): return jnp.dot(left, right, preferred_element_type=F32)]
    dot_general x6 -> x0, matrix products: 10.2 us -> none  [the longest x1 3.28 us: attend_back(): jnp.einsum('ghqk,gqhd->gkhd', probs.astype(LOW), grad_heads, preferred_el...]
    dot_general x4 -> x2, matrix products: 22.2 us -> 12.5 us  [mm_nt(): return jnp.einsum('td,fd->tf', left, right, preferred_element_type=F32)]
    unnamed x85 -> x33, local copies, waits for them, and re-layouts: 15 us -> 9.18 us
  transfers between devices with their start and end apart: 2 -> 0, of which waited for: 0 -> 0; matrix products, arithmetic and copies ran while one was open for 6% -> 0% of each run, Pallas kernels for 13% -> 0%
where the time goes in v4:
time: 483 us
  Pallas kernels  429 us (89%)
  matrix products  32.9 us (7%)
  local copies, waits for them, and re-layouts  18 us (4%)
    pallas_call x4, Pallas kernels, call(): pl.pallas_call(functools.partial(kernel, lax.axis_size('dp')), out_shape=...  429 us
    dot_general x2, matrix products, mm(): return jnp.dot(left, right, preferred_element_type=F32)  14.2 us
    dot_general x2, matrix products, mm_nt(): return jnp.einsum('td,fd->tf', left, right, preferred_element_type=F32)  12.5 us

profile of v4, /device:TPU:0, one launch (start us, length us, event | category | flops | bytes accessed | tf_op | source)
XLA Modules:
  0.0 482.5 jit_solution(14375356020294966760)
XLA Ops:
  1.4 1.3 dynamic_slice.9
  2.7 1.3 dynamic_slice.10
  5.3 106.9 %shard_map.314 = (bf16[2,4,128,2048]{3,2,1,0:T(8,128)(2,1)}, bf16[2,4,128,2048]{3,2,1,0:T(8,128)(2,1)}, bf16[2048,768]{1,0:T(8,128)(2,1)}, bf16[2048,256]{1,0:T(...) custom-call(f32[128,2048]{1,0:T(8,128)} %x.9, ...), custom_call_target="tpu_custom_call" | custom-call | bytes 100000000 | tf_op jit(solution)/shard_map/pallas_call | solution.py:790
  112.2 104.5 %shard_map.315 = (f32[128,2048]{1,0:T(8,128)}, bf16[2,4,128,2048]{3,2,1,0:T(8,128)(2,1)}, bf16[2048,1024]{1,0:T(8,128)(2,1)}, bf16[1024,2048]{1,0:T(8,128)(2,1)}) custom-call(bf16[2,4,128,2048]{3,2,1,0:T(8,128)(2,1)} %get-tuple-element.46.parts, f32[128,2048]{1,0:T(8,128)} %x.9, f32[1,2048]{1,0:T(1,128)} %bitcast.60, ...), custom_call_target="tpu_custom_call", output_to_operand_aliasing={{2}: (7, {})} | custom-call | bytes 100000000 | tf_op jit(solution)/shard_map/pallas_call | solution.py:790
  216.8 8.1 %multiply_convert_fusion = (bf16[1024,1024]{1,0:T(8,128)(2,1)S(1)}, f32[1024,1024]{1,0:T(8,128)S(1)}) fusion(f32[1024]{0:T(1024)S(1)} %dynamic_slice.11, bf16[1024,2048]{1,0:T(8,128)(2,1)} %bitcast.47, bf16[2048,1024]{1,0:T(8,128)(2,1)} %get-tuple-element.50), kind=kOutput, calls=%fused_computation.8 | convolution fusion | flops 4301258752 | bytes 14684160 | tf_op jit(solution)/shard_map/dot_general | solution.py:839
  224.9 6.1 %convert_reduce_fusion = (f32[1024]{0:T(1024)S(1)}, bf16[1024,1024]{1,0:T(8,128)(2,1)S(1)}) fusion(f32[1024,1024]{1,0:T(8,128)S(1)} %get-tuple-element.87, f32[1024]{0:T(1024)S(1)} %dynamic_slice.11, bf16[1024,2048]{1,0:T(8,128)(2,1)S(1)} %bitcast.79, bf16[1024,2048]{1,0:T(8,128)(2,1)S(1)} %copy-done.10), kind=kOutput, calls=%fused_computation.7 | convolution fusion | flops 4308597760 | bytes 14688256 | tf_op jit(solution)/shard_map/td,fd->tf/dot_general | solution.py:842
  231.1 6.4 %convolution_convert_fusion.2 = bf16[1024,2048]{1,0:T(8,128)(2,1)} fusion(bf16[1024,1024]{1,0:T(8,128)(2,1)S(1)} %get-tuple-element.89.grad_pre, bf16[2048,1024]{1,0:T(8,128)(2,1)S(1)} %copy-done), kind=kOutput, calls=%fused_computation.12 | convolution fusion | flops 4297064448 | bytes 10485760 | tf_op jit(solution)/shard_map/td,fd->tf/dot_general | solution.py:842
  237.4 6.1 %convolution_convert_fusion.1 = bf16[1024,2048]{1,0:T(8,128)(2,1)} fusion(bf16[1024,1024]{1,0:T(8,128)(2,1)S(1)} %get-tuple-element.86, bf16[1024,2048]{1,0:T(8,128)(2,1)S(1)} %copy-done.10), kind=kOutput, calls=%fused_computation.11 | convolution fusion | flops 4297064448 | bytes 10485760 | tf_op jit(solution)/shard_map/dot_general | solution.py:839
  243.5 6.2 %convolution_convert_fusion.down = bf16[1024,2048]{1,0:T(8,128)(2,1)} fusion(bf16[1024,1024]{1,0:T(8,128)(2,1)S(1)} %get-tuple-element.86, bf16[1024,2048]{1,0:T(8,128)(2,1)S(1)} %bitcast.80), kind=kOutput, calls=%fused_computation.10 | convolution fusion | flops 4297064448 | bytes 10485760 | tf_op jit(solution)/shard_map/ta,tb->ab/dot_general | solution.py:845
  249.8 127.9 %shard_map.316 = (f32[128,2048]{1,0:T(8,128)}, f32[128,2048]{1,0:T(8,128)}, f32[8,2048]{1,0:T(8,128)}, f32[2048,256]{1,0:T(8,128)}, f32[256,2048]{1,0:T(8,128)},...) custom-call(bf16[2,4,128,2048]{3,2,1,0:T(8,128)(2,1)} %bitcast.49, bf16[2,4,128,2048]{3,2,1,0:T(8,128)(2,1)} %bitcast.50, ...), custom_call_target="tpu_custom_call" | custom-call | bytes 100000000 | tf_op jit(solution)/shard_map/pallas_call | solution.py:790
  377.6 0.7 fusion.8
  378.5 0.8 slice.36
  379.4 0.7 pad_maximum_fusion.early
  380.1 89.9 %shard_map.317 = (f32[128,2048]{1,0:T(8,128)}, f32[8,2048]{1,0:T(8,128)}, f32[512,256]{1,0:T(8,128)}, f32[256,512]{1,0:T(8,128)}, f32[256,512]{1,0:T(8,128)}, /*index=5*/f32[256,512]{1,0:T(8,128)}) custom-call(f32[128,2048]{1,0:T(8,128)} %x.9, f32[1,2048]{1,0:T(1,128)} %bitcast.57, f32[128,2048]{1,0:T(8,128)} %get-tuple-element.59.grad_resid, ...), custom_call_target="tpu_custom_call" | custom-call | bytes 100000000 | tf_op jit(solution)/shard_map/pallas_call | solution.py:790
  470.1 2.0 fusion.6
  472.1 1.3 fusion.7
  473.4 1.0 copy.49
  474.4 2.3 copy.50
  476.7 0.8 copy.51
  477.5 0.8 copy.52
  478.3 0.8 copy.53
  479.1 0.8 copy.54
  479.9 1.3 copy.55
  481.2 1.3 copy.56
  (34 shorter events, 2.2 us)
Async XLA Ops:
  216.8 8.1 %copy-start.9 = (bf16[2,4,128,2048]{3,2,1,0:T(8,128)(2,1)S(1)}, bf16[2,4,128,2048]{3,2,1,0:T(8,128)(2,1)}, u32[]{:S(2)}) copy-start(bf16[2,4,128,2048]{3,2,1,0:T(8,128)(2,1)} %get-tuple-element.45) | copy-start | bytes 12582916
  216.8 8.1 %copy-start.10 = (bf16[1024,2048]{1,0:T(8,128)(2,1)S(1)}, bf16[1024,2048]{1,0:T(8,128)(2,1)}, u32[]{:S(2)}) copy-start(bf16[1024,2048]{1,0:T(8,128)(2,1)} %get-tuple-element.48) | copy-start | bytes 12582916
  224.9 6.1 %copy-start = (bf16[2048,1024]{1,0:T(8,128)(2,1)S(1)}, bf16[2048,1024]{1,0:T(8,128)(2,1)}, u32[]{:S(2)}) copy-start(bf16[2048,1024]{1,0:T(8,128)(2,1)} %get-tuple-element.50) | copy-start | bytes 12582916
  231.0 6.4 %copy-start.1 = (bf16[1024,1024]{1,0:T(8,128)(2,1)}, bf16[1024,1024]{1,0:T(8,128)(2,1)S(1)}, u32[]{:S(2)}) copy-start(bf16[1024,1024]{1,0:T(8,128)(2,1)S(1)} %get-tuple-element.89.grad_pre) | copy-start | bytes 6291460
  380.1 93.3 %copy-start.4 = (f32[128,2048]{1,0:T(8,128)S(1)}, f32[128,2048]{1,0:T(8,128)}, u32[]{:S(2)}) copy-start(f32[128,2048]{1,0:T(8,128)} %get-tuple-element.107) | copy-start | bytes 3145732
  470.0 6.7 %copy-start.8 = (f32[256,512]{1,0:T(8,128)S(1)}, f32[256,512]{1,0:T(8,128)}, u32[]{:S(2)}) copy-start(f32[256,512]{1,0:T(8,128)} %get-tuple-element.111) | copy-start | bytes 1572868
  470.0 7.5 %copy-start.7 = (f32[256,512]{1,0:T(8,128)S(1)}, f32[256,512]{1,0:T(8,128)}, u32[]{:S(2)}) copy-start(f32[256,512]{1,0:T(8,128)} %get-tuple-element.113) | copy-start | bytes 1572868
  470.0 8.3 %copy-start.6 = (f32[256,512]{1,0:T(8,128)S(1)}, f32[256,512]{1,0:T(8,128)}, u32[]{:S(2)}) copy-start(f32[256,512]{1,0:T(8,128)} %get-tuple-element.114) | copy-start | bytes 1572868
  470.0 9.0 %copy-start.5 = (f32[512,256]{1,0:T(8,128)S(1)}, f32[512,256]{1,0:T(8,128)}, u32[]{:S(2)}) copy-start(f32[512,256]{1,0:T(8,128)} %get-tuple-element.116) | copy-start | bytes 1572868
  473.4 6.5 %copy-start.3 = (f32[256,2048]{1,0:T(8,128)S(1)}, f32[256,2048]{1,0:T(8,128)}, u32[]{:S(2)}) copy-start(f32[256,2048]{1,0:T(8,128)} %get-tuple-element.120) | copy-start | bytes 6291460
  476.7 4.5 copy-start.2

commit v5 on v4

--- a/solution.py
+++ b/solution.py
@@ -23,6 +23,7 @@
 
 NC = 4
 NW = 2
+NF = 4
 MESH = pl.DeviceIdType.MESH
 
 
@@ -140,15 +141,20 @@
     SEMS = [grid_of(4, NC), grid_of(4, NC), grid_of(4, NC), grid_of(3, NC), grid_of(3, NC)]
 
     @staticmethod
-    def scratch(rows, width):
-        return [pltpu.VMEM((n, rows, width), LOW) for n in (4, 4, 3)] + Scatter.SEMS
-
-    def __init__(self, me, parts, held, came, hops, load, send, recv, hop_send, hop_recv):
+    def scratch(rows, width, loaded=True):
+        if loaded:
+            return [pltpu.VMEM((n, rows, width), LOW) for n in (4, 4, 3)] + Scatter.SEMS
+        return [pltpu.VMEM((n, rows, width), LOW) for n in (4, 3)] + Scatter.SEMS[1:]
+
+    def __init__(self, me, parts, *scratch):
         self.me, self.parts = me, parts
-        self.held, self.came, self.hops = held, came, hops
-        self.load, self.send, self.recv = load, send, recv
-        self.hop_send, self.hop_recv = hop_send, hop_recv
-        self.rows = held.shape[1] // NC
+        self.held, self.load = None, None
+        if len(scratch) == 8:
+            self.held, self.came, self.hops, self.load, *scratch = scratch
+        else:
+            self.came, self.hops, *scratch = scratch
+        self.send, self.recv, self.hop_send, self.hop_recv = scratch
+        self.rows = self.came.shape[1] // NC
         self.pairs = [
             (0, me.t, me.t_core),
             (0, me.t_x, me.t_far),
@@ -169,6 +175,10 @@
             self.me.core,
         )
 
+    def slot(self, i, j):
+        side, mine, _ = self.pairs[i]
+        return self.parts.at[side, mine, self.span(j)] if self.held is None else self.held.at[i, self.span(j)]
+
     def load_copy(self, i, j):
         side, mine, _ = self.pairs[i]
         return pltpu.make_async_copy(
@@ -186,12 +196,14 @@
             @pl.loop(0, NC)
             def _(j):
                 self.core_copy(i, j).start()
-                self.load_copy(i, j).start()
+                if self.load is not None:
+                    self.load_copy(i, j).start()
 
     def joined(self, i, j):
-        self.load_copy(i, j).wait()
+        if self.load is not None:
+            self.load_copy(i, j).wait()
         self.core_copy(i, j).wait_recv()
-        return self.held[i, self.span(j)].astype(F32) + self.came[i, self.span(j)].astype(F32)
+        return self.slot(i, j)[...].astype(F32) + self.came[i, self.span(j)].astype(F32)
 
     def arrived(self, kind, j):
         self.hop(kind, j, self.hops.at[kind, self.span(j)], self.me.x).wait_recv()
@@ -202,15 +214,15 @@
 
             @pl.loop(0, NC)
             def _(j):
-                self.held[i, self.span(j)] = self.joined(i, j).astype(LOW)
-                self.hop(kind, j, self.held.at[i, self.span(j)], self.me.x).start()
+                self.slot(i, j)[...] = self.joined(i, j).astype(LOW)
+                self.hop(kind, j, self.slot(i, j), self.me.x).start()
 
     def turn(self):
         @pl.loop(0, NC)
         def _(j):
             total = self.joined(2, j) + self.arrived(0, j)
-            self.held[2, self.span(j)] = total.astype(LOW)
-            self.hop(2, j, self.held.at[2, self.span(j)], self.me.z).start()
+            self.slot(2, j)[...] = total.astype(LOW)
+            self.hop(2, j, self.slot(2, j), self.me.z).start()
 
     def result(self, j):
         return self.joined(0, j) + self.arrived(1, j) + self.arrived(2, j)
@@ -235,14 +247,15 @@
 
 class WeightGather:
     @staticmethod
-    def sems(lines):
-        return [grid_of(lines, NW), grid_of(lines, NW), grid_of(lines, NW), grid_of(lines, NW), grid_of(NW)]
+    def sems(lines, parts):
+        return [grid_of(lines, parts)] * 4 + [grid_of(parts)]
 
     def __init__(self, me, halves, whole, z_send, z_recv, y_send, y_recv, keep):
         self.me, self.halves, self.whole = me, halves, whole
         self.z_send, self.z_recv, self.y_send, self.y_recv, self.keep = z_send, z_recv, y_send, y_recv, keep
         _, self.rows, self.width = halves.shape
-        self.count = self.rows // NW
+        self.parts = keep.shape[0]
+        self.count = self.rows // self.parts
 
     def at(self, owner, p):
         return block_at(self.whole, owner, self.rows, self.width, p * self.count, self.count)
@@ -270,18 +283,18 @@
         self.y_copy(0, p, self.piece(me.side, p), self.at(me.d, p)).start()
         self.local(p).start()
 
-    def forward(self, p, first=1, last=None):
+    def forward(self, p):
         me = self.me
 
-        @pl.loop(first, me.lines if last is None else last)
+        @pl.loop(1, me.lines)
         def _(k):
             slot = self.at(2 * me.behind(k) + me.lane, p)
             self.z_copy(k, p, slot, slot, me.y).wait_recv()
             self.y_copy(k, p, slot, slot).start()
 
-    def finish(self, *which):
+    def finish(self):
         me = self.me
-        for p in which:
+        for p in range(self.parts):
 
             @pl.loop(0, me.lines)
             def _(k):
@@ -536,26 +549,44 @@
     return lambda n: pl.ds(pl.multiple_of(n * size, size), size)
 
 
-def head_kernel(
-    dp_total, x, gain, shift, grad, query, key, value, out, up, query_bias, value_bias, info,
-    whole_out, whole_grad, qkv_out, o_out, up_out, parts, queries, keys, values, attended, infos,
-    own, own_grad, whole, qkv_half, out_half, up_half, qkv_whole, o_whole, mask, *scratch,
+def half_of(ref, side):
+    width = ref.shape[1] // 2
+    return ref[:, pl.ds(pl.multiple_of(side * width, width), width)]
+
+
+def front_kernel(
+    dp_total, x, gain1, shift1, grad, query, key, value, out, up, down, query_bias, value_bias, seg, pos,
+    out_bias, gain2, shift2, up_bias,
+    whole1_out, whole2_out, grad_out, qkv_out, o_out, up_out, down_whole, active_out, slope_out, grad_down_out,
+    queries, keys, values, attended, infos, resid,
+    own1, own2, own_grad, whole1, whole2, whole_grad, qkv_half, out_half, up_half, down_half,
+    qkv_whole, o_whole, up_whole, mask, parts, active, slope, grad_down, *scratch,
 ):
     me = Place(dp_total)
-    at, cut = pieces(x.shape[0]), Cut(scratch)
-    gather, gather_grad = Gather(me, own, whole, *cut.take(3)), Gather(me, own_grad, whole_grad, *cut.take(3))
+    at, cut, block = pieces(x.shape[0]), Cut(scratch), column_blocks_of(x.shape[1])
+    gather1, gather2 = Gather(me, own1, whole1, *cut.take(3)), Gather(me, own2, whole2, *cut.take(3))
+    gather_grad = Gather(me, own_grad, whole_grad, *cut.take(3))
     first, second = WeightGather(me, qkv_half, qkv_whole, *cut.take(5)), WeightGather(me, out_half, o_whole, *cut.take(5))
-    third = WeightGather(me, up_half, up_out, *cut.take(5))
+    third, fourth = WeightGather(me, up_half, up_whole, *cut.take(5)), WeightGather(me, down_half, down_whole, *cut.take(5))
+    scatter = Scatter(me, parts, *cut.take(6))
     (save,) = cut.take(1)
+    saved = []
+
+    def store(source, target):
+        saved.append(pltpu.make_async_copy(source, target, save.at[2 + len(saved)]))
+        saved[-1].start()
+
+    infos[0] = jnp.zeros(infos.shape[1:], jnp.int32)
+    infos[0, 0:1], infos[0, 1:2] = seg[...], pos[...]
     me.greet()
-    info_copy = remote(info, infos.at[1], save.at[0], save.at[1], me.z)
+    info_copy = remote(infos.at[0], infos.at[1], save.at[0], save.at[1], me.z)
     info_copy.start()
 
     @pl.loop(0, NC)
     def _(j):
         unit_rows, _ = unit_of(x[at(j)])
-        own[at(j)] = (unit_rows * gain[...] + shift[...]).astype(LOW)
-        gather.start(j)
+        own1[at(j)] = (unit_rows * gain1[...] + shift1[...]).astype(LOW)
+        gather1.start(j)
 
     column_halves(qkv_half, query, key, value)
     for p in range(NW):
@@ -564,101 +595,122 @@
     for p in range(NW):
         second.start(p)
     column_halves(up_half, up)
+    third.start(0)
+    third.start(1)
+    row_halves(down_half, down)
 
     @pl.loop(0, NC)
     def _(j):
         own_grad[at(j)] = grad[at(j)].astype(LOW)
 
     info_copy.wait()
-    infos[0] = info[...]
     fill_mask(mask, infos, False)
-    gather.relay()
+    gather1.relay()
     first.forward(0)
-    gather.finish()
-    third.start(0)
-    first.forward(1)
 
     @pl.loop(0, NC)
     def _(j):
         gather_grad.start(j)
 
-    save_whole = pltpu.make_async_copy(whole, whole_out, save.at[2])
-    save_whole.start()
-    second.forward(0)
-    second.forward(1)
-    first.finish(0, 1)
-    save_qkv = pltpu.make_async_copy(qkv_whole, qkv_out, save.at[3])
-    save_qkv.start()
+    gather1.finish()
+    store(whole1, whole1_out)
+    first.forward(1)
+    first.finish()
+    store(qkv_whole, qkv_out)
     group = mask.shape[1]
     width = queries.shape[1]
 
     @pl.loop(0, 2)
     def _(side):
         rows = pl.ds(pl.multiple_of(side * group, group), group)
-        tokens = whole[side].reshape(group, -1)
+        tokens = whole1[side].reshape(group, -1)
         for n, (result, bias) in enumerate(((queries, query_bias), (keys, None), (values, value_bias))):
             total = dot(tokens, qkv_whole[:, n * width : (n + 1) * width], NN)
-            result[rows] = (total if bias is None else total + bias[...]).astype(LOW)
-
-    gather_grad.relay()
-    steps = iter(((1, 2), (2, 3), (3, None)) if me.lines == 4 else ((1, None),))
+            result[rows] = (total if bias is None else total + half_of(bias, me.side)).astype(LOW)
+
+    for p in range(NW):
+        second.forward(p)
+    steps = iter((None, None, lambda: third.forward(0), lambda: third.start(2)))
 
     def between():
-        span = next(steps, None)
-        if span:
-            third.forward(0, *span)
+        step = next(steps, None)
+        if step:
+            step()
 
     attend(queries, keys, values, mask, attended, between)
-    second.finish(0, 1)
-    save_o = pltpu.make_async_copy(o_whole, o_out, save.at[4])
-    save_o.start()
-    block = column_blocks_of(x.shape[1])
+    second.finish()
+    store(o_whole, o_out)
 
     @pl.loop(0, x.shape[1] // 256)
     def _(n):
         total = dot(attended[...], o_whole[pl.ds(pl.multiple_of(n * 256, 256), 256)], NT)
         parts[:, :, :, block(n)] = total.astype(LOW).reshape(*parts.shape[:3], 256)
 
-    gather_grad.finish()
-    third.finish(0)
-    for copy in (save_whole, save_qkv, save_o):
-        copy.wait()
-
-
-def middle_kernel(
-    dp_total, parts, x, out_bias, gain, shift, up, down, up_part,
-    resid, whole, up_whole, down_whole, own, up_half, down_half, *scratch,
-):
-    me = Place(dp_total)
-    at, cut = pieces(x.shape[0]), Cut(scratch)
-    scatter, gather = Scatter(me, parts, *cut.take(8)), Gather(me, own, whole, *cut.take(3))
-    first, second = WeightGather(me, up_half, up_whole, *cut.take(5)), WeightGather(me, down_half, down_whole, *cut.take(5))
-    me.greet()
     scatter.start()
-    column_halves(up_half, up)
-    first.start(1)
+    third.forward(1)
     scatter.spread()
     scatter.turn()
-    row_halves(down_half, down)
-    first.forward(1)
+    third.start(3)
+    third.forward(2)
 
     @pl.loop(0, NC)
     def _(j):
         rows = x[at(j)] + scatter.result(j) + out_bias[...]
         resid[at(j)] = rows
         unit_rows, _ = unit_of(rows)
-        own[at(j)] = (unit_rows * gain[...] + shift[...]).astype(LOW)
-        gather.start(j)
-
-    for p in range(NW):
-        second.start(p)
-    gather.relay()
-    gather.finish()
-    for p in range(NW):
-        second.forward(p)
+        own2[at(j)] = (unit_rows * gain2[...] + shift2[...]).astype(LOW)
+        gather2.start(j)
+
+    fourth.start(0)
+    fourth.start(1)
+    third.forward(3)
+    gather2.relay()
+    fourth.start(2)
+    fourth.start(3)
+    gather_grad.relay()
+    fourth.forward(0)
+    gather2.finish()
+    store(whole2, whole2_out)
+    third.finish()
+    store(up_whole, up_out)
+
+    def activate(first_block, last_block):
+        @pl.loop(first_block, last_block)
+        def _(n):
+            bias = up_bias[:, pl.ds(pl.multiple_of(me.side * active.shape[1] + n * 256, 256), 256)]
+
+            @pl.loop(0, 2)
+            def _(side):
+                rows = pl.ds(pl.multiple_of(side * group, group), group)
+                pre_act = dot(whole2[side].reshape(group, -1), up_whole[:, block(n)], NN) + bias
+                cumulative, rise = gelu_parts(pre_act)
+                active[rows, block(n)] = (pre_act * cumulative).astype(LOW)
+                slope[rows, block(n)] = rise.astype(LOW)
+
+    hidden_blocks = active.shape[1] // 256
+    activate(0, hidden_blocks // 2)
+    fourth.forward(1)
+    activate(hidden_blocks // 2, hidden_blocks)
+    store(active, active_out)
+    store(slope, slope_out)
+    gather_grad.finish()
+    store(whole_grad, grad_out)
+
+    def product(first_block, last_block):
+        @pl.loop(first_block, last_block)
+        def _(n):
+            total = dot(active[:, block(n)], whole_grad[...].reshape(active.shape[0], -1), TN)
+            grad_down[pl.ds(pl.multiple_of(n * 256, 256), 256)] = total.astype(LOW)
+
+    product(0, hidden_blocks // 2)
+    fourth.forward(2)
+    product(hidden_blocks // 2, hidden_blocks)
+    store(grad_down, grad_down_out)
+    fourth.forward(3)
     scatter.finish()
-    first.finish(1)
-    second.finish(0, 1)
+    fourth.finish()
+    for copy in saved:
+        copy.wait()
 
 
 def turn_kernel(
@@ -832,17 +884,11 @@
     place = lax.axis_index("dp")
     side = (place >> 1) & 1
 
-    def own_half(vector):
-        return lax.dynamic_slice_in_dim(vector, side * (vector.shape[0] // 2), vector.shape[0] // 2, 0)
-
     def mm(left, right):
         return jnp.dot(left, right, preferred_element_type=F32)
 
     def mm_nt(left, right):
         return jnp.einsum("td,fd->tf", left, right, preferred_element_type=F32)
-
-    def mm_tn(left, right):
-        return jnp.einsum("ta,tb->ab", left, right, preferred_element_type=F32)
 
     rows, width = inputs.shape
     row = lambda vector: vector.reshape(1, -1)
@@ -861,49 +907,42 @@
     def column_blocks(partial):
         return partial.reshape(-1, dp_total, wide).transpose(1, 0, 2) if wide % 128 else partial
 
-    info = jnp.pad(jnp.stack([seg_ids, positions]), ((0, 6), (0, 0)))
     heads = like(tokens, head_width, dtype=LOW)
-
-    whole1, grad_whole, qkv_full, o_full, up_part, parts, queries, keys, values, attended, infos = call(
-        head_kernel, 1,
+    units = like(tokens, hidden, dtype=LOW)
+
+    (
+        whole1, whole2, grad_whole, qkv_full, o_full, up_full, down_full, activated, slope, grad_down,
+        queries, keys, values, attended, infos, resid,
+    ) = call(
+        front_kernel, 1,
         (
             inputs, row(norm1_gain), row(norm1_bias), grad_output, query_weight, key_weight, value_weight, out_weight,
-            up_weight, row(own_half(query_bias)), row(own_half(value_bias)), info,
+            up_weight, down_weight, row(query_bias), row(value_bias), row(seg_ids), row(positions),
+            row(out_bias), row(norm2_gain), row(norm2_bias), row(up_bias),
         ),
-        [VMEM] * 12,
+        [VMEM] * 18,
         (
-            group, group, like(width, 3 * head_width, dtype=LOW), like(width, head_width, dtype=LOW),
-            like(width, hidden, dtype=LOW), group, heads, heads, heads, heads, like(2, *info.shape, dtype=jnp.int32),
+            group, group, group, like(width, 3 * head_width, dtype=LOW), like(width, head_width, dtype=LOW),
+            like(width, hidden, dtype=LOW), like(*((dp_total, hidden, wide) if wide % 128 else (hidden, width)), dtype=LOW),
+            units, units, like(hidden, width, dtype=LOW),
+            heads, heads, heads, heads, like(2, 8, GROUP, dtype=jnp.int32), like(rows, width),
         ),
-        (ANY,) * 5 + (VMEM,) * 6,
+        (ANY,) * 10 + (VMEM,) * 6,
         [
-            own, own, slab(*group.shape), slab(2, high, 3 * head_width), slab(2, wide, head_width),
-            slab(2, high, hidden), slab(width, 3 * head_width), slab(width, head_width), slab(2, GROUP, GROUP),
+            own, own, own, *[slab(*group.shape)] * 3,
+            slab(2, high, 3 * head_width), slab(2, wide, head_width), slab(2, high, hidden), slab(2, hidden, wide),
+            slab(width, 3 * head_width), slab(width, head_width), slab(width, hidden), slab(2, GROUP, GROUP),
+            slab(*group.shape), slab(tokens, hidden), slab(tokens, hidden), slab(hidden, width),
         ]
-        + Gather.SEMS * 2 + WeightGather.sems(lines) * 3 + [grid_of(5)],
+        + Gather.SEMS * 3
+        + WeightGather.sems(lines, NW) * 2 + WeightGather.sems(lines, NF) * 2
+        + Scatter.scratch(rows, width, False) + [grid_of(12)],
     )
-    resid, whole2, up_full, down_full = call(
-        middle_kernel, 2,
-        (parts, inputs, row(out_bias), row(norm2_gain), row(norm2_bias), up_weight, down_weight, up_part),
-        [ANY] + [VMEM] * 6 + [ANY],
-        (
-            like(rows, width), group, like(width, hidden, dtype=LOW),
-            like(*((dp_total, hidden, wide) if wide % 128 else (hidden, width)), dtype=LOW),
-        ),
-        (VMEM, ANY, ANY, ANY),
-        [own, slab(2, high, hidden), slab(2, hidden, wide)]
-        + token_scratch + Gather.SEMS + WeightGather.sems(lines) * 2,
-        {7: 2},
-    )
-    grad_whole = grad_whole.reshape(-1, width)
-    whole2, down_full = whole2.reshape(-1, width), side_by_side(down_full)
-    pre_act = mm(whole2, up_full) + own_half(up_bias)
-    cumulative, slope = gelu_parts(pre_act)
-    activated = (pre_act * cumulative).astype(LOW)
-    grad_down = column_blocks(mm_tn(activated, grad_whole).astype(LOW))
+    grad_whole, whole2 = grad_whole.reshape(-1, width), whole2.reshape(-1, width)
+    down_full, grad_down = side_by_side(down_full), column_blocks(grad_down)
+    grad_pre = (mm_nt(grad_whole, down_full) * slope.astype(F32)).astype(LOW)
+    grad_parts = mm_nt(grad_pre, up_full).astype(LOW).reshape(group.shape)
     lowered = mm(activated, down_full).astype(LOW).reshape(group.shape)
-    grad_pre = (mm_nt(grad_whole, down_full) * slope).astype(LOW)
-    grad_parts = mm_nt(grad_pre, up_full).astype(LOW).reshape(group.shape)
 
     grad_resid, layer_output, sums2, down_done, up_done, grad_qkv, grad_out = call(
         turn_kernel, 3,

time: 483 us -> 439 us (0.909)
  Pallas kernels: 429 us -> 402 us
  matrix products: 32.9 us -> 21 us
    pallas_call x4 -> x3, Pallas kernels: 429 us -> 402 us  [call(): pl.pallas_call(functools.partial(kernel, lax.axis_size('dp')), out_shape=...]
    dot_general x2 -> x1, matrix products: 14.2 us -> 6.05 us  [mm(): return jnp.dot(left, right, preferred_element_type=F32)]
    dot_general x1 -> x0, matrix products: 6.24 us -> none  [mm_tn(): return jnp.einsum('ta,tb->ab', left, right, preferred_element_type=F32)]
where the time goes in v5:
time: 439 us
  Pallas kernels  402 us (92%)
  matrix products  21 us (5%)
  local copies, waits for them, and re-layouts  13.9 us (3%)
    pallas_call x3, Pallas kernels, call(): pl.pallas_call(functools.partial(kernel, lax.axis_size('dp')), out_shape=...  402 us
    dot_general x2, matrix products, mm_nt(): return jnp.einsum('td,fd->tf', left, right, preferred_element_type=F32)  14.9 us
    unnamed x33, local copies, waits for them, and re-layouts  9.18 us

profile of v5, /device:TPU:0, one launch (start us, length us, event | category | flops | bytes accessed | tf_op | source)
XLA Modules:
  0.0 438.7 jit_solution(5993205615776622796)
XLA Ops:
  0.7 182.7 %shard_map.314 = (bf16[2,4,128,2048]{3,2,1,0:T(8,128)(2,1)}, bf16[2,4,128,2048]{3,2,1,0:T(8,128)(2,1)}, bf16[2,4,128,2048]{3,2,1,0:T(8,128)(2,1)}, bf16[2048,768...) custom-call(f32[128,2048]{1,0:T(8,128)} %x.5, ...), custom_call_target="tpu_custom_call" | custom-call | bytes 100000000 | tf_op jit(solution)/shard_map/pallas_call | solution.py:842
  183.4 0.0 copy-start.9
  183.4 8.7 %convert_reduce_fusion = (f32[1024]{0:T(1024)S(1)}, bf16[1024,1024]{1,0:T(8,128)(2,1)S(1)}) fusion(bf16[1024,1024]{1,0:T(8,128)(2,1)} %get-tuple-element.48, bf16[1024,2048]{1,0:T(8,128)(2,1)} %bitcast.76, bf16[1024,2048]{1,0:T(8,128)(2,1)} %get-tuple-element.47), kind=kOutput, calls=%fused_computation | convolution fusion | flops 4300209152 | bytes 12587008 | tf_op jit(solution)/shard_map/td,fd->tf/dot_general | solution.py:891
  192.1 0.0 copy-start
  192.2 6.2 %convolution_convert_fusion.1 = bf16[1024,2048]{1,0:T(8,128)(2,1)} fusion(bf16[1024,1024]{1,0:T(8,128)(2,1)S(1)} %get-tuple-element.89.grad_pre, bf16[2048,1024]{1,0:T(8,128)(2,1)S(1)} %copy-done.9), kind=kOutput, calls=%fused_computation.3 | convolution fusion | flops 4297064448 | bytes 10485760 | tf_op jit(solution)/shard_map/td,fd->tf/dot_general | solution.py:891
  198.3 6.1 %convolution_convert_fusion = bf16[1024,2048]{1,0:T(8,128)(2,1)} fusion(bf16[1024,1024]{1,0:T(8,128)(2,1)S(1)} %copy-done.10, bf16[1024,2048]{1,0:T(8,128)(2,1)S(1)} %copy-done.8), kind=kOutput, calls=%fused_computation.2 | convolution fusion | flops 4297064448 | bytes 10485760 | tf_op jit(solution)/shard_map/dot_general | solution.py:888
  204.4 128.7 %shard_map.315 = (f32[128,2048]{1,0:T(8,128)}, f32[128,2048]{1,0:T(8,128)}, f32[8,2048]{1,0:T(8,128)}, f32[2048,256]{1,0:T(8,128)}, f32[256,2048]{1,0:T(8,128)},...) custom-call(bf16[2,4,128,2048]{3,2,1,0:T(8,128)(2,1)} %bitcast.45, bf16[2,4,128,2048]{3,2,1,0:T(8,128)(2,1)} %bitcast.46, ...), custom_call_target="tpu_custom_call" | custom-call | bytes 100000000 | tf_op jit(solution)/shard_map/pallas_call | solution.py:842
  333.1 0.7 fusion.2
  333.8 0.1 select_bitcast_fusion.2
  333.9 0.8 slice.36
  334.8 0.1 select_bitcast_fusion
  334.9 0.7 pad_maximum_fusion.early
  335.6 90.8 %shard_map.316 = (f32[128,2048]{1,0:T(8,128)}, f32[8,2048]{1,0:T(8,128)}, f32[512,256]{1,0:T(8,128)}, f32[256,512]{1,0:T(8,128)}, f32[256,512]{1,0:T(8,128)}, /*index=5*/f32[256,512]{1,0:T(8,128)}) custom-call(f32[128,2048]{1,0:T(8,128)} %x.5, f32[1,2048]{1,0:T(1,128)} %bitcast.53, f32[128,2048]{1,0:T(8,128)} %get-tuple-element.61.grad_resid, ...), custom_call_target="tpu_custom_call" | custom-call | bytes 100000000 | tf_op jit(solution)/shard_map/pallas_call | solution.py:842
  426.4 1.8 fusion
  428.3 1.3 fusion.1
  429.6 1.0 copy.47
  430.6 2.3 copy.48
  432.9 0.8 copy.49
  433.7 0.8 copy.50
  434.5 0.0 copy-done.5
  434.5 0.8 copy.51
  435.3 0.8 copy.52
  436.1 1.3 copy.53
  437.4 1.3 copy.54
  (26 shorter events, 0.1 us)
Async XLA Ops:
  183.4 8.8 %copy-start.9 = (bf16[2048,1024]{1,0:T(8,128)(2,1)S(1)}, bf16[2048,1024]{1,0:T(8,128)(2,1)}, u32[]{:S(2)}) copy-start(bf16[2048,1024]{1,0:T(8,128)(2,1)} %get-tuple-element.49) | copy-start | bytes 12582916
  192.1 6.2 %copy-start = (bf16[1024,1024]{1,0:T(8,128)(2,1)}, bf16[1024,1024]{1,0:T(8,128)(2,1)S(1)}, u32[]{:S(2)}) copy-start(bf16[1024,1024]{1,0:T(8,128)(2,1)S(1)} %get-tuple-element.89.grad_pre) | copy-start | bytes 6291460
  192.1 6.2 %copy-start.8 = (bf16[1024,2048]{1,0:T(8,128)(2,1)S(1)}, bf16[1024,2048]{1,0:T(8,128)(2,1)}, u32[]{:S(2)}) copy-start(bf16[1024,2048]{1,0:T(8,128)(2,1)} %get-tuple-element.47) | copy-start | bytes 12582916
  192.1 6.2 %copy-start.10 = (bf16[1024,1024]{1,0:T(8,128)(2,1)S(1)}, bf16[1024,1024]{1,0:T(8,128)(2,1)}, u32[]{:S(2)}) copy-start(bf16[1024,1024]{1,0:T(8,128)(2,1)} %get-tuple-element.50) | copy-start | bytes 6291460
  335.6 94.0 %copy-start.3 = (f32[128,2048]{1,0:T(8,128)S(1)}, f32[128,2048]{1,0:T(8,128)}, u32[]{:S(2)}) copy-start(f32[128,2048]{1,0:T(8,128)} %get-tuple-element.107) | copy-start | bytes 3145732
  426.4 6.5 %copy-start.7 = (f32[256,512]{1,0:T(8,128)S(1)}, f32[256,512]{1,0:T(8,128)}, u32[]{:S(2)}) copy-start(f32[256,512]{1,0:T(8,128)} %get-tuple-element.111) | copy-start | bytes 1572868
  426.4 7.3 %copy-start.6 = (f32[256,512]{1,0:T(8,128)S(1)}, f32[256,512]{1,0:T(8,128)}, u32[]{:S(2)}) copy-start(f32[256,512]{1,0:T(8,128)} %get-tuple-element.113) | copy-start | bytes 1572868
  426.4 8.1 %copy-start.5 = (f32[256,512]{1,0:T(8,128)S(1)}, f32[256,512]{1,0:T(8,128)}, u32[]{:S(2)}) copy-start(f32[256,512]{1,0:T(8,128)} %get-tuple-element.114) | copy-start | bytes 1572868
  426.4 8.9 %copy-start.4 = (f32[512,256]{1,0:T(8,128)S(1)}, f32[512,256]{1,0:T(8,128)}, u32[]{:S(2)}) copy-start(f32[512,256]{1,0:T(8,128)} %get-tuple-element.116) | copy-start | bytes 1572868
  429.6 6.5 %copy-start.2 = (f32[256,2048]{1,0:T(8,128)S(1)}, f32[256,2048]{1,0:T(8,128)}, u32[]{:S(2)}) copy-start(f32[256,2048]{1,0:T(8,128)} %get-tuple-element.120) | copy-start | bytes 6291460
  432.9 4.5 %copy-start.1 = (f32[2048,256]{1,0:T(8,128)S(1)}, f32[2048,256]{1,0:T(8,128)}, u32[]{:S(2)}) copy-start(f32[2048,256]{1,0:T(8,128)} %get-tuple-element.122) | copy-start | bytes 6291460

commit v6 on v5

--- a/solution.py
+++ b/solution.py
@@ -311,93 +311,83 @@
 
 class WeightScatter:
     @staticmethod
-    def scratch(lines, rows, width):
-        return [pltpu.VMEM((lines, rows, width), LOW)] * 3 + [grid_of(lines)] * 5
-
-    def __init__(self, me, parts, held, came, hops, load, y_send, y_recv, z_send, z_recv):
-        self.me, self.parts, self.held, self.came, self.hops = me, parts, held, came, hops
-        self.load, self.y_send, self.y_recv, self.z_send, self.z_recv = load, y_send, y_recv, z_send, z_recv
-        _, self.rows, self.width = held.shape
+    def scratch(lines, rows, width, loaded=False):
+        blocks = [pltpu.VMEM((lines, rows, width), LOW)] * (2 if loaded else 1)
+        return blocks + [grid_of(lines)] * (5 if loaded else 4) + [grid_of(1)]
+
+    def __init__(self, me, parts, hops, *scratch):
+        self.me, self.parts, self.hops = me, parts, hops
+        self.held, self.load = None, None
+        if len(scratch) == 8:
+            self.held, self.came, self.load, *scratch = scratch
+        else:
+            self.came, *scratch = scratch
+        self.y_send, self.y_recv, self.z_send, self.z_recv, self.keep = scratch
+        _, self.rows, self.width = self.came.shape
         self.step = 32
 
+    def theirs(self, k):
+        return block_at(self.parts, 2 * self.me.ahead(k) + 1 - self.me.lane, self.rows, self.width)
+
+    def mine(self, k):
+        return block_at(self.parts, 2 * self.me.ahead(k) + self.me.lane, self.rows, self.width)
+
+    def slot(self, k):
+        return self.mine(k) if self.held is None else self.held.at[k]
+
     def y_copy(self, k):
-        src = block_at(self.parts, 2 * self.me.ahead(k) + 1 - self.me.lane, self.rows, self.width)
-        return remote(src, self.came.at[k], self.y_send.at[k], self.y_recv.at[k], self.me.y)
+        return remote(self.theirs(k), self.came.at[k], self.y_send.at[k], self.y_recv.at[k], self.me.y)
 
     def load_copy(self, k):
-        src = block_at(self.parts, 2 * self.me.ahead(k) + self.me.lane, self.rows, self.width)
-        return pltpu.make_async_copy(src, self.held.at[k], self.load.at[k])
+        return pltpu.make_async_copy(self.mine(k), self.held.at[k], self.load.at[k])
 
     def z_copy(self, k, peer):
-        return remote(self.held.at[k], self.hops.at[k], self.z_send.at[k], self.z_recv.at[k], peer)
+        return remote(self.slot(k), self.hops.at[k], self.z_send.at[k], self.z_recv.at[k], peer)
+
+    def keep_copy(self):
+        return pltpu.make_async_copy(self.slot(0), self.hops.at[0], self.keep.at[0])
 
     def start(self):
         @pl.loop(1, self.me.lines + 1)
         def _(n):
             k = lax.rem(n, self.me.lines)
             self.y_copy(k).start()
-            self.load_copy(k).start()
-
-    def joined(self, k, at):
-        return self.held[k, at].astype(F32) + self.came[k, at].astype(F32)
+            if self.load is not None:
+                self.load_copy(k).start()
+
+    def join(self, k):
+        if self.load is not None:
+            self.load_copy(k).wait()
+        self.y_copy(k).wait_recv()
+        slot = self.slot(k)
+
+        @pl.loop(0, self.rows, step=self.step)
+        def _(row):
+            at = pl.ds(pl.multiple_of(row, self.step), self.step)
+            slot[at] = (slot[at].astype(F32) + self.came[k, at].astype(F32)).astype(LOW)
 
     def spread(self, first, last):
         @pl.loop(first, last)
         def _(k):
-            self.load_copy(k).wait()
-            self.y_copy(k).wait_recv()
-
-            @pl.loop(0, self.rows, step=self.step)
-            def _(row):
-                at = pl.ds(row, self.step)
-                self.held[k, at] = self.joined(k, at).astype(LOW)
-
+            self.join(k)
             self.z_copy(k, self.me.mate(self.me.ahead(k))).start()
 
-    def finish(self, store):
+    def own(self):
+        self.join(0)
+        self.keep_copy().start()
+
+    def finish(self):
         me = self.me
-        self.load_copy(0).wait()
-        self.y_copy(0).wait_recv()
 
         @pl.loop(1, me.lines)
         def _(k):
-            self.z_copy(k, me.y).wait_recv()
-
-        @pl.loop(0, self.rows, step=self.step)
-        def _(row):
-            at = pl.ds(row, self.step)
-            same, other = self.joined(0, at), self.hops[1, at].astype(F32)
-            for k in range(2, me.lines):
-                if k % 2:
-                    other = other + self.hops[k, at].astype(F32)
-                else:
-                    same = same + self.hops[k, at].astype(F32)
-            store(me.side, at, same)
-            store(1 - me.side, at, other)
+            self.z_copy(k, me.y).wait()
 
         @pl.loop(0, me.lines)
         def _(k):
             self.y_copy(k).wait_send()
 
-        @pl.loop(1, me.lines)
-        def _(k):
-            self.z_copy(k, me.y).wait_send()
-
-
-def store_columns(*outs):
-    def store(half, at, value):
-        width = outs[0].shape[1] // 2
-        for n, out in enumerate(outs):
-            out[at, pl.ds(pl.multiple_of(half * width, width), width)] = value[:, n * width : (n + 1) * width]
-
-    return store
-
-
-def store_rows(out):
-    def store(half, at, value):
-        out[pl.ds(pl.multiple_of(half * (out.shape[0] // 2) + at.start, at.size), at.size)] = value
-
-    return store
+        self.keep_copy().wait()
 
 
 class SumAll:
@@ -409,22 +399,22 @@
     def __init__(self, me, held, came, send, recv):
         self.me, self.held, self.came, self.send, self.recv = me, held, came, send, recv
 
-    def run(self, shared):
-        me, peers, mask = self.me, [], 1
+    def run(self, first, last, shared):
+        me, mask = self.me, 1
+        peers = [me.core, me.x]
         while mask < 2 * me.lines:
             peers.append((me.d + mask - 2 * mask * lax.rem(lax.div(me.d, mask), 2), me.t))
             mask *= 2
-        dp_steps = len(peers)
-        for n, peer in enumerate(peers + [me.core, me.x]):
-            copy = remote(self.held.at[n], self.came.at[n], self.send.at[n], self.recv.at[n], peer)
+        for n in range(len(peers))[first:last]:
+            copy = remote(self.held.at[n], self.came.at[n], self.send.at[n], self.recv.at[n], peers[n])
             copy.start()
             copy.wait()
             total = self.held[n] + self.came[n]
-            if n >= dp_steps:
+            if n < 2:
                 row = lax.broadcasted_iota(jnp.int32, total.shape, 0)
                 total = jnp.where(row < shared, total, self.held[n])
             self.held[n + 1] = total
-        return self.held[dp_steps + 2]
+        return self.held[len(peers)]
 
 
 def unit_of(rows):
@@ -713,45 +703,69 @@
         copy.wait()
 
 
-def turn_kernel(
-    dp_total, parts, lowered, resid, grad, gain, down_bias, down, whole2, grad_pre, o_whole,
-    queries, keys, values, attended, infos,
-    grad_resid, output, sums, down_done, up_done, grad_qkv, grad_out,
-    own, whole, mask, grad_att, grad_up, *scratch,
+def back_kernel(
+    dp_total, grad_parts, lowered, down, whole2, whole1, grad_pre_in, resid, grad, gain2, down_bias, o_whole,
+    queries, keys, values, attended, infos, x, gain1, qkv_whole,
+    down_hops, up_hops, out_hops, qkv_hops, output, grad_inputs, sums,
+    own, tokens, whole, mask, grad_att, grad_up, shared, grad_out, qkv, *scratch,
 ):
     me = Place(dp_total)
-    at, cut = pieces(resid.shape[0]), Cut(scratch)
-    scatter, other = Scatter(me, parts, *cut.take(8)), Scatter(me, lowered, *cut.take(8))
-    gather = Gather(me, own, whole, *cut.take(3))
-    first, second = WeightScatter(me, down, *cut.take(8)), WeightScatter(me, grad_up, *cut.take(8))
-    lines = me.lines
-    block = column_blocks_of(resid.shape[1])
+    at, cut, block = pieces(x.shape[0]), Cut(scratch), column_blocks_of(x.shape[1])
+    scatter, other = Scatter(me, grad_parts, *cut.take(8)), Scatter(me, lowered, *cut.take(8))
+    last, gather = Scatter(me, whole, *cut.take(6)), Gather(me, own, whole, *cut.take(3))
+    first = WeightScatter(me, down, down_hops, *cut.take(8))
+    second = WeightScatter(me, grad_up, up_hops, *cut.take(6))
+    third = WeightScatter(me, grad_out, out_hops, *cut.take(6))
+    fourth = WeightScatter(me, qkv, qkv_hops, *cut.take(6))
+    vectors = SumAll(me, *cut.take(4))
+    (load,) = cut.take(1)
+    start = vectors.held.at[0]
+    lines, hidden, head_width = me.lines, grad_up.shape[1], queries.shape[1]
+    grad_pre, grad_qkv = shared.at[:, :hidden], shared.at[:, : 3 * head_width]
     me.greet()
+    load2 = pltpu.make_async_copy(whole2, tokens, load.at[0])
+    load1 = pltpu.make_async_copy(whole1, tokens, load.at[1])
+    load3 = pltpu.make_async_copy(grad_pre_in, grad_pre, load.at[2])
+    load2.start()
+    load3.start()
     scatter.start()
     first.start()
     scatter.spread()
+    load2.wait()
+    load3.wait()
+    row_blocks = grad_up.shape[0] // 256
+
+    def up_product(first_block, last_block):
+        @pl.loop(first_block, last_block)
+        def _(n):
+            total = dot(tokens[:, block(n)], grad_pre[...], TN)
+            grad_up[pl.ds(pl.multiple_of(n * 256, 256), 256)] = total.astype(LOW)
+
+    up_product(0, row_blocks // 2)
     scatter.turn()
-
-    @pl.loop(0, grad_up.shape[0] // 256)
+    up_product(row_blocks // 2, row_blocks)
+    second.start()
+    load1.start()
+    first.spread(1, lines // 2)
+    start[...] = jnp.zeros_like(start)
+
+    @pl.loop(0, hidden // 256)
     def _(n):
-        grad_up[pl.ds(pl.multiple_of(n * 256, 256), 256)] = dot(whole2[:, block(n)], grad_pre[...], TN).astype(LOW)
-
-    second.start()
-    first.spread(1, lines // 2)
-    sums[...] = jnp.zeros_like(sums)
+        columns = pl.ds(pl.multiple_of(me.side * hidden + n * 256, 256), 256)
+        start[6:7, columns] = jnp.sum(grad_pre[:, block(n)].astype(F32), axis=0, keepdims=True)
 
     @pl.loop(0, NC)
     def _(j):
         unit_rows, inverse = unit_of(resid[at(j)])
         e = scatter.result(j)
-        rows = grad[at(j)] + back_of(e, unit_rows, inverse, gain[...])
-        grad_resid[at(j)] = rows
+        rows = grad[at(j)] + back_of(e, unit_rows, inverse, gain2[...])
+        grad_inputs[at(j)] = rows
         own[at(j)] = rows.astype(LOW)
         gather.start(j)
-        sums[0:1] += jnp.sum(e * unit_rows, axis=0, keepdims=True)
-        sums[1:2] += jnp.sum(e, axis=0, keepdims=True)
-        sums[2:3] += jnp.sum(rows, axis=0, keepdims=True)
-        sums[3:4] += jnp.sum(grad[at(j)], axis=0, keepdims=True)
+        start[2:3] += jnp.sum(e * unit_rows, axis=0, keepdims=True)
+        start[3:4] += jnp.sum(e, axis=0, keepdims=True)
+        start[4:5] += jnp.sum(rows, axis=0, keepdims=True)
+        start[5:6] += jnp.sum(grad[at(j)], axis=0, keepdims=True)
 
     fill_mask(mask, infos, True)
     first.spread(lines // 2, lines)
@@ -761,93 +775,125 @@
     other.spread()
     mixed = whole[...].reshape(-1, whole.shape[3])
     grad_att[...] = dot(mixed, o_whole[...], NN).astype(LOW)
-    steps = iter(((1, 2), (2, 3), (3, 4)) if lines == 4 else ((1, lines),))
+    steps = iter((None, lambda: second.spread(1, lines // 2), None, lambda: first.own()))
 
     def between():
-        span = next(steps, None)
-        if span:
-            second.spread(*span)
+        step = next(steps, None)
+        if step:
+            step()
 
     attend_back(queries, keys, values, grad_att, mask, grad_qkv, between)
-    sums[4:5, : grad_qkv.shape[1]] = jnp.sum(grad_qkv[...].astype(F32), axis=0, keepdims=True)
-    other.turn()
-
-    @pl.loop(0, resid.shape[1] // 256)
+
+    for n in (0, 2):
+        total = jnp.sum(grad_qkv[:, n * head_width : (n + 1) * head_width].astype(F32), axis=0, keepdims=True)
+        start[7:8, pl.ds(pl.multiple_of((n + me.side) * head_width, head_width), head_width)] = total
+
+    wide = third.width
+
+    @pl.loop(0, x.shape[1] // 256)
     def _(n):
         columns = whole[:, :, :, block(n)].reshape(-1, 256)
-        grad_out[:, block(n)] = dot(attended[...], columns, TN).astype(LOW)
-
-    first.finish(store_rows(down_done))
+        total = dot(attended[...], columns, TN).astype(LOW)
+        if wide % 128:
+            for i in range(256 // wide):
+                grad_out[n * (256 // wide) + i] = total[:, i * wide : (i + 1) * wide]
+        else:
+            grad_out[:, block(n)] = total
+
+    second.spread(lines // 2, lines - 1)
+    third.start()
+    load1.wait()
+
+    @pl.loop(0, qkv.shape[0] // 256)
+    def _(n):
+        qkv[pl.ds(pl.multiple_of(n * 256, 256), 256)] = dot(tokens[:, block(n)], grad_qkv[...], TN).astype(LOW)
+
+    fourth.start()
+    other.turn()
+
+    @pl.loop(0, x.shape[1] // 256)
+    def _(n):
+        total = dot(grad_qkv[...], qkv_whole[pl.ds(pl.multiple_of(n * 256, 256), 256)], NT)
+        whole[:, :, :, block(n)] = total.astype(LOW).reshape(*whole.shape[:3], 256)
+
+    last.start()
+    second.spread(lines - 1, lines)
+    last.spread()
+    last.turn()
+    second.own()
 
     @pl.loop(0, NC)
     def _(j):
         output[at(j)] = resid[at(j)] + other.result(j) + down_bias[...]
 
-    scatter.finish()
-    other.finish()
-    second.finish(store_columns(up_done))
-
-
-def tail_kernel(
-    dp_total, x, gain, grad_resid, early, out, whole, grad_qkv, qkv_whole,
-    grad_inputs, sums, out_done, query_done, key_done, value_done,
-    qkv, parts, *scratch,
-):
-    me = Place(dp_total)
-    at, cut = pieces(x.shape[0]), Cut(scratch)
-    scatter = Scatter(me, parts, *cut.take(8))
-    first, second = WeightScatter(me, out, *cut.take(8)), WeightScatter(me, qkv, *cut.take(8))
-    vectors = SumAll(me, *cut.take(4))
-    block = column_blocks_of(x.shape[1])
-    me.greet()
-    first.start()
-
-    @pl.loop(0, qkv.shape[0] // 256)
-    def _(n):
-        qkv[pl.ds(pl.multiple_of(n * 256, 256), 256)] = dot(whole[:, block(n)], grad_qkv[...], TN).astype(LOW)
-
-    second.start()
-
-    @pl.loop(0, x.shape[1] // 256)
-    def _(n):
-        total = dot(grad_qkv[...], qkv_whole[pl.ds(pl.multiple_of(n * 256, 256), 256)], NT)
-        parts[:, :, :, block(n)] = total.astype(LOW).reshape(*parts.shape[:3], 256)
-
-    scatter.start()
-    scatter.spread()
-    first.spread(1, me.lines)
-    scatter.turn()
-    vectors.held[0] = early[...]
+    third.spread(1, lines)
+    third.own()
 
     @pl.loop(0, NC)
     def _(j):
         unit_rows, inverse = unit_of(x[at(j)])
-        e = scatter.result(j)
-        grad_inputs[at(j)] = grad_resid[at(j)] + back_of(e, unit_rows, inverse, gain[...])
-        vectors.held[0, 0:1] += jnp.sum(e * unit_rows, axis=0, keepdims=True)
-        vectors.held[0, 1:2] += jnp.sum(e, axis=0, keepdims=True)
-
-    second.spread(1, me.lines)
-    sums[...] = vectors.run(6)
-    scatter.finish()
-    first.finish(store_rows(out_done))
-    second.finish(store_columns(query_done, key_done, value_done))
+        e = last.result(j)
+        grad_inputs[at(j)] += back_of(e, unit_rows, inverse, gain1[...])
+        start[0:1] += jnp.sum(e * unit_rows, axis=0, keepdims=True)
+        start[1:2] += jnp.sum(e, axis=0, keepdims=True)
+
+    vectors.run(0, 2, 6)
+    fourth.spread(1, lines)
+    fourth.own()
+    sums[...] = vectors.run(2, None, 6)
+    for part in (scatter, other, last, first, second, third, fourth):
+        part.finish()
+
+
+def final_kernel(
+    lines, down_hops, up_hops, out_hops, qkv_hops, rows_in, grads_in, sums,
+    output, grad_inputs, down, up, out, query, key, value, *vectors,
+):
+    side = lax.rem(lax.div(lax.axis_index("dp"), 2), 2)
+
+    def half_sums(hops):
+        same, opposite = hops[0].astype(F32), hops[1].astype(F32)
+        for k in range(2, lines):
+            if k % 2:
+                opposite = opposite + hops[k].astype(F32)
+            else:
+                same = same + hops[k].astype(F32)
+        return (side, same), (1 - side, opposite)
+
+    for half, total in half_sums(down_hops):
+        down[half] = total
+    for half, total in half_sums(out_hops):
+        out[half] = total
+    for half, total in half_sums(up_hops):
+        width = total.shape[1]
+        up[:, pl.ds(pl.multiple_of(half * width, width), width)] = total
+    for half, total in half_sums(qkv_hops):
+        width = total.shape[1] // 3
+        for n, ref in enumerate((query, key, value)):
+            ref[:, pl.ds(pl.multiple_of(half * width, width), width)] = total[:, n * width : (n + 1) * width]
+    output[...], grad_inputs[...] = rows_in[...], grads_in[...]
+    first = 0
+    for n, ref in enumerate(vectors):
+        if n < 7:
+            ref[...] = sums[n : n + 1, : ref.shape[1]]
+        else:
+            ref[...] = sums[7:8, first : first + ref.shape[1]]
+            first += ref.shape[1]
 
 
 VMEM = pl.BlockSpec(memory_space=pltpu.VMEM)
 ANY = pl.BlockSpec(memory_space=pl.ANY)
 
 
-def call(kernel, number, ins, in_specs, outs, out_specs, scratch, aliases=None):
+def call(kernel, number, ins, in_specs, outs, out_specs, scratch, limit=60):
     return pl.pallas_call(
         functools.partial(kernel, lax.axis_size("dp")),
         out_shape=outs,
         in_specs=in_specs,
         out_specs=out_specs,
         scratch_shapes=scratch,
-        input_output_aliases=aliases or {},
         compiler_params=pltpu.CompilerParams(
-            collective_id=number, has_side_effects=True, vmem_limit_bytes=60 << 20
+            collective_id=number, has_side_effects=True, vmem_limit_bytes=limit << 20
         ),
         cost_estimate=pl.CostEstimate(flops=0, bytes_accessed=100_000_000, transcendentals=0),
     )(*ins)
@@ -944,69 +990,74 @@
     grad_parts = mm_nt(grad_pre, up_full).astype(LOW).reshape(group.shape)
     lowered = mm(activated, down_full).astype(LOW).reshape(group.shape)
 
-    grad_resid, layer_output, sums2, down_done, up_done, grad_qkv, grad_out = call(
-        turn_kernel, 3,
+    hops = [
+        like(lines, *shape, dtype=LOW)
+        for shape in ((hidden, wide), (high, hidden), (head_width, wide), (high, 3 * head_width))
+    ]
+    *hops, layer_output, grad_inputs, sums = call(
+        back_kernel, 2,
         (
-            grad_parts, lowered, resid, grad_output, row(norm2_gain), row(down_bias), grad_down, whole2, grad_pre, o_full,
-            queries, keys, values, attended, infos,
+            grad_parts, lowered, grad_down, whole2, whole1.reshape(-1, width), grad_pre, resid, grad_output,
+            row(norm2_gain), row(down_bias), o_full, queries, keys, values, attended, infos, inputs, row(norm1_gain), qkv_full,
         ),
-        [ANY] * 2 + [VMEM] * 4 + [ANY] + [VMEM] * 8,
-        (
-            like(rows, width), like(rows, width), like(8, width), like(*down_weight.shape), like(*up_weight.shape),
-            like(tokens, 3 * head_width, dtype=LOW), like(head_width, width, dtype=LOW),
+        [ANY] * 6 + [VMEM] * 13,
+        (*hops, like(rows, width), like(rows, width), like(8, width)),
+        (ANY,) * 4 + (VMEM,) * 3,
+        [
+            own, slab(tokens, width), slab(*group.shape), slab(2, GROUP, GROUP), slab(tokens, head_width),
+            slab(width, hidden), slab(tokens, max(hidden, 3 * head_width)),
+            slab(*((dp_total, head_width, wide) if wide % 128 else (head_width, width))), slab(width, 3 * head_width),
+        ]
+        + Scatter.scratch(rows, width) * 2 + Scatter.scratch(rows, width, False) + Gather.SEMS
+        + WeightScatter.scratch(lines, hidden, wide, True) + WeightScatter.scratch(lines, high, hidden)
+        + WeightScatter.scratch(lines, head_width, wide) + WeightScatter.scratch(lines, high, 3 * head_width)
+        + SumAll.scratch(dp_total, width) + [grid_of(3)],
+        63,
+    )
+    cuts = 4
+
+    def cut_at(dim, *shape):
+        block = tuple(n // cuts if i == dim else n for i, n in enumerate(shape))
+        return pl.BlockSpec(block, lambda g: tuple(g if i == dim else 0 for i in range(len(shape))))
+
+    up_total, bias_total = up_bias.shape[0], query_bias.shape[0]
+    lengths = [width] * 6 + [up_total, bias_total, bias_total]
+    results = pl.pallas_call(
+        functools.partial(final_kernel, lines),
+        grid=(cuts,),
+        out_shape=(
+            like(rows, width), like(rows, width), like(2, hidden, wide), like(high, 2 * hidden), like(2, head_width, wide),
+            *[like(high, 2 * head_width)] * 3, *[like(1, n) for n in lengths],
         ),
-        (VMEM,) * 7,
-        [own, slab(*group.shape), slab(2, GROUP, GROUP), slab(tokens, head_width), slab(width, hidden)]
-        + token_scratch * 2 + Gather.SEMS
-        + WeightScatter.scratch(lines, hidden, wide) + WeightScatter.scratch(lines, high, hidden),
-    )
-
-    def spread(half):
-        return jnp.where(side == jnp.arange(2)[:, None], half, 0.0).reshape(-1)
-
-    def padded(vector):
-        return row(jnp.pad(vector, (0, width - vector.shape[0])))
-
-    biases = [spread(sums2[4, n * head_width : (n + 1) * head_width]) for n in (0, 2)]
-    early = jnp.concatenate(
-        [
-            jnp.zeros((2, width), F32),
-            sums2[:4],
-            padded(spread(jnp.sum(grad_pre.astype(F32), axis=0))),
-            padded(jnp.concatenate(biases)),
-        ]
-    )
-    grad_inputs, sums, out_done, query_done, key_done, value_done = call(
-        tail_kernel, 4,
-        (
-            inputs, row(norm1_gain), grad_resid, early, column_blocks(grad_out), whole1.reshape(-1, width), grad_qkv,
-            qkv_full,
+        in_specs=[
+            cut_at(1, lines, hidden, wide), cut_at(1, lines, high, hidden), cut_at(1, lines, head_width, wide),
+            cut_at(1, lines, high, 3 * head_width), cut_at(0, rows, width), cut_at(0, rows, width), cut_at(None, 8, width),
+        ],
+        out_specs=(
+            cut_at(0, rows, width), cut_at(0, rows, width), cut_at(1, 2, hidden, wide), cut_at(0, high, 2 * hidden),
+            cut_at(1, 2, head_width, wide), *[cut_at(0, high, 2 * head_width)] * 3, *[cut_at(None, 1, n) for n in lengths],
         ),
-        [VMEM] * 4 + [ANY] + [VMEM] * 3,
-        (like(rows, width), like(8, width), like(*out_weight.shape), *[like(*query_weight.shape)] * 3),
-        (VMEM,) * 6,
-        [slab(width, 3 * head_width), slab(*group.shape)]
-        + token_scratch
-        + WeightScatter.scratch(lines, head_width, wide) + WeightScatter.scratch(lines, high, 3 * head_width)
-        + SumAll.scratch(dp_total, width),
-    )
+        compiler_params=pltpu.CompilerParams(vmem_limit_bytes=63 << 20),
+    )(*hops, layer_output, grad_inputs, sums)
+    layer_output, grad_inputs, down_done, up_done, out_done, query_done, key_done, value_done = results[:8]
+    sums = [vector.reshape(-1) for vector in results[8:]]
     return (
         layer_output,
         grad_inputs,
         sums[0],
         sums[1],
         query_done,
-        sums[7, : 2 * head_width],
+        sums[7],
         key_done,
         value_done,
-        sums[7, 2 * head_width : 4 * head_width],
-        out_done,
+        sums[8],
+        out_done.reshape(-1, wide),
         sums[4],
         sums[2],
         sums[3],
         up_done,
-        sums[6, : up_bias.shape[0]],
-        down_done,
+        sums[6],
+        down_done.reshape(-1, wide),
         sums[5],
     )
 

time: 439 us -> 395 us (0.90)
  Pallas kernels: 402 us -> 373 us
  local copies, waits for them, and re-layouts: 13.9 us -> 0.02 us
    pallas_call x3 -> x2, Pallas kernels: 402 us -> 366 us  [call(): pl.pallas_call(functools.partial(kernel, lax.axis_size('dp')), out_shape=...]
    unnamed x33 -> x8, local copies, waits for them, and re-layouts: 9.18 us -> 0.02 us
    pallas_call x0 -> x1, Pallas kernels: none -> 6.97 us  [local(): pl.pallas_call(functools.partial(final_kernel, lines), grid=(cuts,), out_...]
    slice x4 -> x0, local copies, waits for them, and re-layouts: 4.71 us -> none  [the longest x1 1.82 us: local(): sums[5]]
where the time goes in v6:
time: 395 us
  Pallas kernels  373 us (94%)
  matrix products  20.9 us (5%)
    pallas_call x2, Pallas kernels, call(): pl.pallas_call(functools.partial(kernel, lax.axis_size('dp')), out_shape=...  366 us
    dot_general x2, matrix products, mm_nt(): return jnp.einsum('td,fd->tf', left, right, preferred_element_type=F32)  14.8 us

profile of v6, /device:TPU:0, one launch (start us, length us, event | category | flops | bytes accessed | tf_op | source)
XLA Modules:
  0.0 394.8 jit_solution(5796268597691568966)
XLA Ops:
  0.7 182.7 %shard_map.314 = (bf16[2,4,128,2048]{3,2,1,0:T(8,128)(2,1)}, bf16[2,4,128,2048]{3,2,1,0:T(8,128)(2,1)}, bf16[2,4,128,2048]{3,2,1,0:T(8,128)(2,1)}, bf16[2048,768...) custom-call(f32[128,2048]{1,0:T(8,128)} %x.3, ...), custom_call_target="tpu_custom_call" | custom-call | bytes 100000000 | tf_op jit(solution)/shard_map/pallas_call | solution.py:889
  183.3 0.0 copy-start.2
  183.4 0.0 copy-start.3
  183.4 8.7 %multiply_convert_fusion.grad_pre_in = bf16[1024,1024]{1,0:T(8,128)(2,1)S(1)} fusion(bf16[1024,1024]{1,0:T(8,128)(2,1)} %get-tuple-element.59, bf16[1024,2048]{1,0:T(8,128)(2,1)} %bitcast.50, bf16[1024,2048]{1,0:T(8,128)(2,1)} %get-tuple-element.58), kind=kOutput, calls=%fused_computation | convolution fusion | flops 4298113024 | bytes 12582912 | tf_op jit(solution)/shard_map/td,fd->tf/dot_general | solution.py:937
  192.1 0.0 copy-done.2
  192.1 0.0 copy-done.3
  192.1 0.0 copy-start
  192.1 0.0 copy-start.1
  192.1 6.1 %convolution_convert_fusion = bf16[1024,2048]{1,0:T(8,128)(2,1)} fusion(bf16[1024,1024]{1,0:T(8,128)(2,1)S(1)} %copy-done.3, bf16[1024,2048]{1,0:T(8,128)(2,1)S(1)} %copy-done.2), kind=kOutput, calls=%fused_computation.1 | convolution fusion | flops 4297064448 | bytes 10485760 | tf_op jit(solution)/shard_map/dot_general | solution.py:934
  198.2 0.0 copy-done
  198.2 0.0 copy-done.1
  198.2 6.1 %convolution_convert_fusion.1 = bf16[1024,2048]{1,0:T(8,128)(2,1)} fusion(bf16[1024,1024]{1,0:T(8,128)(2,1)S(1)} %multiply_convert_fusion.grad_pre_in, bf16[2048,1024]{1,0:T(8,128)(2,1)S(1)} %copy-done.1), kind=kOutput, calls=%fused_computation.2 | convolution fusion | flops 4297064448 | bytes 10485760 | tf_op jit(solution)/shard_map/td,fd->tf/dot_general | solution.py:937
  204.3 183.3 %shard_map.315 = (bf16[4,1024,256]{2,1,0:T(8,128)(2,1)}, bf16[4,256,1024]{2,1,0:T(8,128)(2,1)}, bf16[4,256,256]{2,1,0:T(8,128)(2,1)}, bf16[4,256,768]{2,1,0:T(8,...) custom-call(bf16[2,4,128,2048]{3,2,1,0:T(8,128)(2,1)} %bitcast.36, ...), custom_call_target="tpu_custom_call" | custom-call | bytes 100000000 | tf_op jit(solution)/shard_map/pallas_call | solution.py:889
  387.6 7.0 %shard_map.316 = (f32[128,2048]{1,0:T(8,128)}, f32[128,2048]{1,0:T(8,128)}, f32[2,1024,256]{2,1,0:T(8,128)}, f32[256,2048]{1,0:T(8,128)}, f32[2,256,256]{2,1,0:T...) custom-call(bf16[4,1024,256]{2,1,0:T(8,128)(2,1)} %get-tuple-element, ...), custom_call_target="tpu_custom_call" | custom-call | tf_op jit(solution)/shard_map/pallas_call | solution.py:1025
Async XLA Ops:
  183.3 8.7 %copy-start.2 = (bf16[1024,2048]{1,0:T(8,128)(2,1)S(1)}, bf16[1024,2048]{1,0:T(8,128)(2,1)}, u32[]{:S(2)}) copy-start(bf16[1024,2048]{1,0:T(8,128)(2,1)} %get-tuple-element.58) | copy-start | bytes 12582916
  183.4 8.7 %copy-start.3 = (bf16[1024,1024]{1,0:T(8,128)(2,1)S(1)}, bf16[1024,1024]{1,0:T(8,128)(2,1)}, u32[]{:S(2)}) copy-start(bf16[1024,1024]{1,0:T(8,128)(2,1)} %get-tuple-element.61) | copy-start | bytes 6291460
  192.1 6.1 %copy-start = (bf16[1024,1024]{1,0:T(8,128)(2,1)}, bf16[1024,1024]{1,0:T(8,128)(2,1)S(1)}, u32[]{:S(2)}) copy-start(bf16[1024,1024]{1,0:T(8,128)(2,1)S(1)} %multiply_convert_fusion.grad_pre_in) | copy-start | bytes 6291460
  192.1 6.1 %copy-start.1 = (bf16[2048,1024]{1,0:T(8,128)(2,1)S(1)}, bf16[2048,1024]{1,0:T(8,128)(2,1)}, u32[]{:S(2)}) copy-start(bf16[2048,1024]{1,0:T(8,128)(2,1)} %get-tuple-element.60) | copy-start | bytes 12582916

commit v7 on v6

--- a/solution.py
+++ b/solution.py
@@ -165,10 +165,20 @@
     def span(self, j):
         return pl.ds(j * self.rows, self.rows)
 
+    def part(self, side, t, j):
+        if len(self.parts.shape) == 4:
+            return self.parts.at[side, t, self.span(j)]
+        return self.parts.at[pl.ds(pl.multiple_of(((4 * side + t) * NC + j) * self.rows, self.rows), self.rows)]
+
+    def pair_rows(self, i):
+        side, mine, _ = self.pairs[i]
+        count = 2 * NC * self.rows
+        return pl.ds(pl.multiple_of((2 * side + lax.div(mine, 2)) * count, count), count)
+
     def core_copy(self, i, j):
         side, _, theirs = self.pairs[i]
         return remote(
-            self.parts.at[side, theirs, self.span(j)],
+            self.part(side, theirs, j),
             self.came.at[i, self.span(j)],
             self.send.at[i, j],
             self.recv.at[i, j],
@@ -177,12 +187,12 @@
 
     def slot(self, i, j):
         side, mine, _ = self.pairs[i]
-        return self.parts.at[side, mine, self.span(j)] if self.held is None else self.held.at[i, self.span(j)]
+        return self.part(side, mine, j) if self.held is None else self.held.at[i, self.span(j)]
 
     def load_copy(self, i, j):
         side, mine, _ = self.pairs[i]
         return pltpu.make_async_copy(
-            self.parts.at[side, mine, self.span(j)], self.held.at[i, self.span(j)], self.load.at[i, j]
+            self.part(side, mine, j), self.held.at[i, self.span(j)], self.load.at[i, j]
         )
 
     def hop(self, kind, j, src, peer):
@@ -190,8 +200,8 @@
             src, self.hops.at[kind, self.span(j)], self.hop_send.at[kind, j], self.hop_recv.at[kind, j], peer
         )
 
-    def start(self):
-        for i in (3, 1, 2, 0):
+    def start(self, blocks=(3, 1, 2, 0)):
+        for i in blocks:
 
             @pl.loop(0, NC)
             def _(j):
@@ -209,8 +219,8 @@
         self.hop(kind, j, self.hops.at[kind, self.span(j)], self.me.x).wait_recv()
         return self.hops[kind, self.span(j)].astype(F32)
 
-    def spread(self):
-        for kind, i in ((0, 3), (1, 1)):
+    def spread(self, hops=((0, 3), (1, 1))):
+        for kind, i in hops:
 
             @pl.loop(0, NC)
             def _(j):
@@ -292,21 +302,24 @@
             self.z_copy(k, p, slot, slot, me.y).wait_recv()
             self.y_copy(k, p, slot, slot).start()
 
+    def arrive(self, p):
+        me = self.me
+
+        @pl.loop(0, me.lines)
+        def _(k):
+            slot = self.at(2 * me.behind(k) + 1 - me.lane, p)
+            self.y_copy(k, p, slot, slot).wait()
+
+        @pl.loop(1, me.lines)
+        def _(k):
+            slot = self.at(me.d, p)
+            self.z_copy(k, p, slot, slot, me.y).wait_send()
+
+        self.local(p).wait()
+
     def finish(self):
-        me = self.me
         for p in range(self.parts):
-
-            @pl.loop(0, me.lines)
-            def _(k):
-                slot = self.at(2 * me.behind(k) + 1 - me.lane, p)
-                self.y_copy(k, p, slot, slot).wait()
-
-            @pl.loop(1, me.lines)
-            def _(k):
-                slot = self.at(me.d, p)
-                self.z_copy(k, p, slot, slot, me.y).wait_send()
-
-            self.local(p).wait()
+            self.arrive(p)
 
 
 class WeightScatter:
@@ -547,10 +560,10 @@
 def front_kernel(
     dp_total, x, gain1, shift1, grad, query, key, value, out, up, down, query_bias, value_bias, seg, pos,
     out_bias, gain2, shift2, up_bias,
-    whole1_out, whole2_out, grad_out, qkv_out, o_out, up_out, down_whole, active_out, slope_out, grad_down_out,
+    whole1_out, whole2_out, qkv_out, o_out, up_out, down_out, active_out, grad_pre_out, grad_down_out,
     queries, keys, values, attended, infos, resid,
     own1, own2, own_grad, whole1, whole2, whole_grad, qkv_half, out_half, up_half, down_half,
-    qkv_whole, o_whole, up_whole, mask, parts, active, slope, grad_down, *scratch,
+    qkv_whole, o_whole, up_whole, down_whole, mask, parts, active, slope, grad_down, *scratch,
 ):
     me = Place(dp_total)
     at, cut, block = pieces(x.shape[0]), Cut(scratch), column_blocks_of(x.shape[1])
@@ -682,70 +695,97 @@
     fourth.forward(1)
     activate(hidden_blocks // 2, hidden_blocks)
     store(active, active_out)
-    store(slope, slope_out)
     gather_grad.finish()
-    store(whole_grad, grad_out)
-
-    def product(first_block, last_block):
-        @pl.loop(first_block, last_block)
-        def _(n):
-            total = dot(active[:, block(n)], whole_grad[...].reshape(active.shape[0], -1), TN)
-            grad_down[pl.ds(pl.multiple_of(n * 256, 256), 256)] = total.astype(LOW)
-
-    product(0, hidden_blocks // 2)
     fourth.forward(2)
-    product(hidden_blocks // 2, hidden_blocks)
+
+    @pl.loop(0, hidden_blocks)
+    def _(n):
+        total = dot(active[:, block(n)], whole_grad[...].reshape(active.shape[0], -1), TN)
+        grad_down[pl.ds(pl.multiple_of(n * 256, 256), 256)] = total.astype(LOW)
+
     store(grad_down, grad_down_out)
+
+    def lower(p):
+        fourth.arrive(p)
+        units = pl.ds(p * fourth.count, fourth.count)
+        if len(down_whole.shape) == 2:
+            store(down_whole.at[units], down_out.at[units])
+            total = dot(whole_grad[...].reshape(slope.shape[0], -1), down_whole[units], NT)
+        else:
+            store(down_whole.at[:, units], down_out.at[:, units])
+            owners = 128 // fourth.width
+
+            def add(n, total):
+                columns = pl.ds(pl.multiple_of(n * 128, 128), 128)
+                weights = jnp.concatenate([down_whole[n * owners + i, units] for i in range(owners)], axis=1)
+                return total + dot(whole_grad[:, :, :, columns].reshape(slope.shape[0], -1), weights, NT)
+
+            total = lax.fori_loop(
+                0, down_whole.shape[0] // owners, add, jnp.zeros((slope.shape[0], fourth.count), F32)
+            )
+        slope[:, units] = (total * slope[:, units].astype(F32)).astype(LOW)
+        store(slope.at[:, units], grad_pre_out.at[:, units])
+
+    lower(0)
+    lower(1)
     fourth.forward(3)
+    lower(2)
+    lower(3)
     scatter.finish()
-    fourth.finish()
     for copy in saved:
         copy.wait()
 
 
 def back_kernel(
-    dp_total, grad_parts, lowered, down, whole2, whole1, grad_pre_in, resid, grad, gain2, down_bias, o_whole,
+    dp_total, down, whole2, whole1, grad_pre_in, active, up_whole, down_whole, resid, grad, gain2, down_bias, o_whole,
     queries, keys, values, attended, infos, x, gain1, qkv_whole,
-    down_hops, up_hops, out_hops, qkv_hops, output, grad_inputs, sums,
+    down_hops, up_hops, out_hops, qkv_hops, lowered, output, grad_inputs, sums,
     own, tokens, whole, mask, grad_att, grad_up, shared, grad_out, qkv, *scratch,
 ):
     me = Place(dp_total)
     at, cut, block = pieces(x.shape[0]), Cut(scratch), column_blocks_of(x.shape[1])
-    scatter, other = Scatter(me, grad_parts, *cut.take(8)), Scatter(me, lowered, *cut.take(8))
+    scatter, other = Scatter(me, tokens, *cut.take(6)), Scatter(me, lowered, *cut.take(8))
     last, gather = Scatter(me, whole, *cut.take(6)), Gather(me, own, whole, *cut.take(3))
     first = WeightScatter(me, down, down_hops, *cut.take(8))
     second = WeightScatter(me, grad_up, up_hops, *cut.take(6))
     third = WeightScatter(me, grad_out, out_hops, *cut.take(6))
     fourth = WeightScatter(me, qkv, qkv_hops, *cut.take(6))
     vectors = SumAll(me, *cut.take(4))
-    (load,) = cut.take(1)
+    load, tiles = cut.take(2)
     start = vectors.held.at[0]
     lines, hidden, head_width = me.lines, grad_up.shape[1], queries.shape[1]
     grad_pre, grad_qkv = shared.at[:, :hidden], shared.at[:, : 3 * head_width]
+    load1, load2, load3, load4 = (
+        pltpu.make_async_copy(source, target, load.at[n])
+        for n, (source, target) in enumerate(
+            ((whole1, tokens), (whole2, tokens), (grad_pre_in, grad_pre), (up_whole, grad_up))
+        )
+    )
+    load3.start()
+    load4.start()
     me.greet()
-    load2 = pltpu.make_async_copy(whole2, tokens, load.at[0])
-    load1 = pltpu.make_async_copy(whole1, tokens, load.at[1])
-    load3 = pltpu.make_async_copy(grad_pre_in, grad_pre, load.at[2])
-    load2.start()
-    load3.start()
-    scatter.start()
     first.start()
-    scatter.spread()
-    load2.wait()
     load3.wait()
-    row_blocks = grad_up.shape[0] // 256
-
-    def up_product(first_block, last_block):
-        @pl.loop(first_block, last_block)
+    load4.wait()
+
+    def norm_parts(i):
+        rows = scatter.pair_rows(i)
+
+        @pl.loop(0, x.shape[1] // 256)
         def _(n):
-            total = dot(tokens[:, block(n)], grad_pre[...], TN)
-            grad_up[pl.ds(pl.multiple_of(n * 256, 256), 256)] = total.astype(LOW)
-
-    up_product(0, row_blocks // 2)
+            weights = grad_up[pl.ds(pl.multiple_of(n * 256, 256), 256)]
+            tokens[rows, block(n)] = dot(grad_pre[rows], weights, NT).astype(LOW)
+
+        scatter.start((i,))
+
+    norm_parts(3)
+    norm_parts(1)
+    scatter.spread(((0, 3),))
+    norm_parts(2)
+    scatter.spread(((1, 1),))
+    norm_parts(0)
+
     scatter.turn()
-    up_product(row_blocks // 2, row_blocks)
-    second.start()
-    load1.start()
     first.spread(1, lines // 2)
     start[...] = jnp.zeros_like(start)
 
@@ -767,12 +807,22 @@
         start[4:5] += jnp.sum(rows, axis=0, keepdims=True)
         start[5:6] += jnp.sum(grad[at(j)], axis=0, keepdims=True)
 
+    scatter.finish()
+    load2.start()
     fill_mask(mask, infos, True)
-    first.spread(lines // 2, lines)
+    first.spread(lines // 2, lines - 1)
+    load2.wait()
+
+    @pl.loop(0, grad_up.shape[0] // 256)
+    def _(n):
+        total = dot(tokens[:, block(n)], grad_pre[...], TN)
+        grad_up[pl.ds(pl.multiple_of(n * 256, 256), 256)] = total.astype(LOW)
+
+    second.start()
+    load1.start()
+    first.spread(lines - 1, lines)
     gather.relay()
     gather.finish()
-    other.start()
-    other.spread()
     mixed = whole[...].reshape(-1, whole.shape[3])
     grad_att[...] = dot(mixed, o_whole[...], NN).astype(LOW)
     steps = iter((None, lambda: second.spread(1, lines // 2), None, lambda: first.own()))
@@ -788,6 +838,14 @@
         total = jnp.sum(grad_qkv[:, n * head_width : (n + 1) * head_width].astype(F32), axis=0, keepdims=True)
         start[7:8, pl.ds(pl.multiple_of((n + me.side) * head_width, head_width), head_width)] = total
 
+    load1.wait()
+
+    @pl.loop(0, qkv.shape[0] // 256)
+    def _(n):
+        qkv[pl.ds(pl.multiple_of(n * 256, 256), 256)] = dot(tokens[:, block(n)], grad_qkv[...], TN).astype(LOW)
+
+    fourth.start()
+    second.spread(lines // 2, lines - 1)
     wide = third.width
 
     @pl.loop(0, x.shape[1] // 256)
@@ -800,16 +858,7 @@
         else:
             grad_out[:, block(n)] = total
 
-    second.spread(lines // 2, lines - 1)
     third.start()
-    load1.wait()
-
-    @pl.loop(0, qkv.shape[0] // 256)
-    def _(n):
-        qkv[pl.ds(pl.multiple_of(n * 256, 256), 256)] = dot(tokens[:, block(n)], grad_qkv[...], TN).astype(LOW)
-
-    fourth.start()
-    other.turn()
 
     @pl.loop(0, x.shape[1] // 256)
     def _(n):
@@ -819,15 +868,54 @@
     last.start()
     second.spread(lines - 1, lines)
     last.spread()
+
+    held = tokens.at[:, :hidden]
+    load_active = pltpu.make_async_copy(active, held, tiles.at[0])
+    load_active.start()
+
+    def tile_at(b):
+        return tokens.at[:hidden, hidden + b * 256 : hidden + (b + 1) * 256]
+
+    def result_at(b):
+        return tokens.at[:, hidden + (2 + b) * 256 : hidden + (3 + b) * 256]
+
+    def load_tile(n, b):
+        return pltpu.make_async_copy(down_whole.at[:, block(n)], tile_at(b), tiles.at[1 + b])
+
+    def save_tile(n, b):
+        return pltpu.make_async_copy(result_at(b), lowered.at[:, block(n)], tiles.at[3 + b])
+
+    load_tile(0, 0).start()
+    load_tile(1, 1).start()
+    load_active.wait()
+    tile_total = x.shape[1] // 256
+
+    @pl.loop(0, tile_total // 2)
+    def _(m):
+        for b in range(2):
+            n = 2 * m + b
+            load_tile(n, b).wait()
+
+            @pl.when(m > 0)
+            def _():
+                save_tile(n, b).wait()
+
+            result_at(b)[...] = dot(held[...], tile_at(b)[...], NN).astype(LOW)
+            save_tile(n, b).start()
+
+            @pl.when(m < tile_total // 2 - 1)
+            def _():
+                load_tile(n + 2, b).start()
+
+    for b in range(2):
+        save_tile(tile_total - 2 + b, b).wait()
+    other.start()
     last.turn()
     second.own()
-
-    @pl.loop(0, NC)
-    def _(j):
-        output[at(j)] = resid[at(j)] + other.result(j) + down_bias[...]
-
-    third.spread(1, lines)
-    third.own()
+    other.spread()
+    fourth.spread(1, lines // 2)
+    other.turn()
+    fourth.spread(lines // 2, lines - 1)
 
     @pl.loop(0, NC)
     def _(j):
@@ -838,10 +926,17 @@
         start[1:2] += jnp.sum(e, axis=0, keepdims=True)
 
     vectors.run(0, 2, 6)
-    fourth.spread(1, lines)
+    fourth.spread(lines - 1, lines)
     fourth.own()
+    third.spread(1, lines)
+    third.own()
+
+    @pl.loop(0, NC)
+    def _(j):
+        output[at(j)] = resid[at(j)] + other.result(j) + down_bias[...]
+
     sums[...] = vectors.run(2, None, 6)
-    for part in (scatter, other, last, first, second, third, fourth):
+    for part in (other, last, first, second, third, fourth):
         part.finish()
 
 
@@ -930,12 +1025,6 @@
     place = lax.axis_index("dp")
     side = (place >> 1) & 1
 
-    def mm(left, right):
-        return jnp.dot(left, right, preferred_element_type=F32)
-
-    def mm_nt(left, right):
-        return jnp.einsum("td,fd->tf", left, right, preferred_element_type=F32)
-
     rows, width = inputs.shape
     row = lambda vector: vector.reshape(1, -1)
     group = like(2, tensor_total, rows, width, dtype=LOW)
@@ -953,11 +1042,12 @@
     def column_blocks(partial):
         return partial.reshape(-1, dp_total, wide).transpose(1, 0, 2) if wide % 128 else partial
 
+    down_shape = (dp_total, hidden, wide) if wide % 128 else (hidden, width)
     heads = like(tokens, head_width, dtype=LOW)
     units = like(tokens, hidden, dtype=LOW)
 
     (
-        whole1, whole2, grad_whole, qkv_full, o_full, up_full, down_full, activated, slope, grad_down,
+        whole1, whole2, qkv_full, o_full, up_full, down_full, activated, grad_pre, grad_down,
         queries, keys, values, attended, infos, resid,
     ) = call(
         front_kernel, 1,
@@ -968,50 +1058,47 @@
         ),
         [VMEM] * 18,
         (
-            group, group, group, like(width, 3 * head_width, dtype=LOW), like(width, head_width, dtype=LOW),
-            like(width, hidden, dtype=LOW), like(*((dp_total, hidden, wide) if wide % 128 else (hidden, width)), dtype=LOW),
+            group, group, like(width, 3 * head_width, dtype=LOW), like(width, head_width, dtype=LOW),
+            like(width, hidden, dtype=LOW), like(*down_shape, dtype=LOW),
             units, units, like(hidden, width, dtype=LOW),
             heads, heads, heads, heads, like(2, 8, GROUP, dtype=jnp.int32), like(rows, width),
         ),
-        (ANY,) * 10 + (VMEM,) * 6,
+        (ANY,) * 9 + (VMEM,) * 6,
         [
             own, own, own, *[slab(*group.shape)] * 3,
             slab(2, high, 3 * head_width), slab(2, wide, head_width), slab(2, high, hidden), slab(2, hidden, wide),
-            slab(width, 3 * head_width), slab(width, head_width), slab(width, hidden), slab(2, GROUP, GROUP),
-            slab(*group.shape), slab(tokens, hidden), slab(tokens, hidden), slab(hidden, width),
+            slab(width, 3 * head_width), slab(width, head_width), slab(width, hidden), slab(*down_shape),
+            slab(2, GROUP, GROUP), slab(*group.shape), slab(tokens, hidden), slab(tokens, hidden), slab(hidden, width),
         ]
         + Gather.SEMS * 3
         + WeightGather.sems(lines, NW) * 2 + WeightGather.sems(lines, NF) * 2
-        + Scatter.scratch(rows, width, False) + [grid_of(12)],
+        + Scatter.scratch(rows, width, False) + [grid_of(9 + 2 * NF)],
+        63,
     )
-    grad_whole, whole2 = grad_whole.reshape(-1, width), whole2.reshape(-1, width)
     down_full, grad_down = side_by_side(down_full), column_blocks(grad_down)
-    grad_pre = (mm_nt(grad_whole, down_full) * slope.astype(F32)).astype(LOW)
-    grad_parts = mm_nt(grad_pre, up_full).astype(LOW).reshape(group.shape)
-    lowered = mm(activated, down_full).astype(LOW).reshape(group.shape)
-
     hops = [
         like(lines, *shape, dtype=LOW)
         for shape in ((hidden, wide), (high, hidden), (head_width, wide), (high, 3 * head_width))
     ]
-    *hops, layer_output, grad_inputs, sums = call(
+    *hops, _, layer_output, grad_inputs, sums = call(
         back_kernel, 2,
         (
-            grad_parts, lowered, grad_down, whole2, whole1.reshape(-1, width), grad_pre, resid, grad_output,
-            row(norm2_gain), row(down_bias), o_full, queries, keys, values, attended, infos, inputs, row(norm1_gain), qkv_full,
+            grad_down, whole2.reshape(-1, width), whole1.reshape(-1, width), grad_pre, activated, up_full, down_full,
+            resid, grad_output, row(norm2_gain), row(down_bias), o_full, queries, keys, values, attended, infos, inputs, row(norm1_gain), qkv_full,
         ),
-        [ANY] * 6 + [VMEM] * 13,
-        (*hops, like(rows, width), like(rows, width), like(8, width)),
-        (ANY,) * 4 + (VMEM,) * 3,
+        [ANY] * 7 + [VMEM] * 13,
+        (*hops, like(tokens, width, dtype=LOW), like(rows, width), like(rows, width), like(8, width)),
+        (ANY,) * 5 + (VMEM,) * 3,
         [
             own, slab(tokens, width), slab(*group.shape), slab(2, GROUP, GROUP), slab(tokens, head_width),
             slab(width, hidden), slab(tokens, max(hidden, 3 * head_width)),
             slab(*((dp_total, head_width, wide) if wide % 128 else (head_width, width))), slab(width, 3 * head_width),
         ]
-        + Scatter.scratch(rows, width) * 2 + Scatter.scratch(rows, width, False) + Gather.SEMS
+        + Scatter.scratch(rows, width, False) + Scatter.scratch(rows, width) + Scatter.scratch(rows, width, False)
+        + Gather.SEMS
         + WeightScatter.scratch(lines, hidden, wide, True) + WeightScatter.scratch(lines, high, hidden)
         + WeightScatter.scratch(lines, head_width, wide) + WeightScatter.scratch(lines, high, 3 * head_width)
-        + SumAll.scratch(dp_total, width) + [grid_of(3)],
+        + SumAll.scratch(dp_total, width) + [grid_of(4), grid_of(5)],
         63,
     )
     cuts = 4

time: 395 us -> 385 us (0.975)
  matrix products: 20.9 us -> 0 us
  Pallas kernels: 373 us -> 383 us
    dot_general x3 -> x0, matrix products: 20.9 us -> none  [the longest x2 14.8 us: mm_nt(): return jnp.einsum('td,fd->tf', left, right, preferred_element_type=F32)]
    pallas_call x2, Pallas kernels: 366 us -> 376 us  [call(): pl.pallas_call(functools.partial(kernel, lax.axis_size('dp')), out_shape=...]
where the time goes in v7:
time: 385 us; the launch traced here: 384 us
  Pallas kernels  383 us (99%)
    pallas_call x2, Pallas kernels, call(): pl.pallas_call(functools.partial(kernel, lax.axis_size('dp')), out_shape=...  376 us

profile of v7, /device:TPU:0, one launch (start us, length us, event | category | flops | bytes accessed | tf_op | source)
XLA Modules:
  0.0 384.2 jit_solution(6320657466670403356)
XLA Ops:
  0.7 185.6 %shard_map.314 = (bf16[2,4,128,2048]{3,2,1,0:T(8,128)(2,1)}, bf16[2,4,128,2048]{3,2,1,0:T(8,128)(2,1)}, bf16[2048,768]{1,0:T(8,128)(2,1)}, bf16[2048,256]{1,0:T(...) custom-call(f32[128,2048]{1,0:T(8,128)} %x.3, ...), custom_call_target="tpu_custom_call" | custom-call | bytes 100000000 | tf_op jit(solution)/shard_map/pallas_call | solution.py:984
  186.2 190.8 %shard_map.315 = (bf16[4,1024,256]{2,1,0:T(8,128)(2,1)}, bf16[4,256,1024]{2,1,0:T(8,128)(2,1)}, bf16[4,256,256]{2,1,0:T(8,128)(2,1)}, bf16[4,256,768]{2,1,0:T(8,...) custom-call(bf16[1024,2048]{1,0:T(8,128)(2,1)} %get-tuple-element.56.down, ...), custom_call_target="tpu_custom_call" | custom-call | bytes 100000000 | tf_op jit(solution)/shard_map/pallas_call | solution.py:984
  377.0 7.0 %shard_map.316 = (f32[128,2048]{1,0:T(8,128)}, f32[128,2048]{1,0:T(8,128)}, f32[2,1024,256]{2,1,0:T(8,128)}, f32[256,2048]{1,0:T(8,128)}, f32[2,256,256]{2,1,0:T...) custom-call(bf16[4,1024,256]{2,1,0:T(8,128)(2,1)} %get-tuple-element, ...), custom_call_target="tpu_custom_call" | custom-call | tf_op jit(solution)/shard_map/pallas_call | solution.py:1112

commit v8 on v7

--- a/solution.py
+++ b/solution.py
@@ -666,10 +666,10 @@
 
     fourth.start(0)
     fourth.start(1)
+    fourth.start(2)
+    fourth.start(3)
     third.forward(3)
     gather2.relay()
-    fourth.start(2)
-    fourth.start(3)
     gather_grad.relay()
     fourth.forward(0)
     gather2.finish()
@@ -914,7 +914,6 @@
     second.own()
     other.spread()
     fourth.spread(1, lines // 2)
-    other.turn()
     fourth.spread(lines // 2, lines - 1)
 
     @pl.loop(0, NC)
@@ -925,6 +924,7 @@
         start[0:1] += jnp.sum(e * unit_rows, axis=0, keepdims=True)
         start[1:2] += jnp.sum(e, axis=0, keepdims=True)
 
+    other.turn()
     vectors.run(0, 2, 6)
     fourth.spread(lines - 1, lines)
     fourth.own()

time: 385 us -> 388 us (level)
  Pallas kernels: 383 us -> 387 us
where the time goes in v8:
time: 388 us; the launch traced here: 387 us
  Pallas kernels  387 us (100%)
    pallas_call x2, Pallas kernels, call(): pl.pallas_call(functools.partial(kernel, lax.axis_size('dp')), out_shape=...  380 us

profile of v8, /device:TPU:0, one launch (start us, length us, event | category | flops | bytes accessed | tf_op | source)
XLA Modules:
  0.0 387.4 jit_solution(15853469196170189724)
XLA Ops:
  0.7 189.1 %shard_map.314 = (bf16[2,4,128,2048]{3,2,1,0:T(8,128)(2,1)}, bf16[2,4,128,2048]{3,2,1,0:T(8,128)(2,1)}, bf16[2048,768]{1,0:T(8,128)(2,1)}, bf16[2048,256]{1,0:T(...) custom-call(f32[128,2048]{1,0:T(8,128)} %x.3, ...), custom_call_target="tpu_custom_call" | custom-call | bytes 100000000 | tf_op jit(solution)/shard_map/pallas_call | solution.py:984
  189.8 190.4 %shard_map.315 = (bf16[4,1024,256]{2,1,0:T(8,128)(2,1)}, bf16[4,256,1024]{2,1,0:T(8,128)(2,1)}, bf16[4,256,256]{2,1,0:T(8,128)(2,1)}, bf16[4,256,768]{2,1,0:T(8,...) custom-call(bf16[1024,2048]{1,0:T(8,128)(2,1)} %get-tuple-element.56.down, ...), custom_call_target="tpu_custom_call" | custom-call | bytes 100000000 | tf_op jit(solution)/shard_map/pallas_call | solution.py:984
  380.2 7.0 %shard_map.316 = (f32[128,2048]{1,0:T(8,128)}, f32[128,2048]{1,0:T(8,128)}, f32[2,1024,256]{2,1,0:T(8,128)}, f32[256,2048]{1,0:T(8,128)}, f32[2,256,256]{2,1,0:T...) custom-call(bf16[4,1024,256]{2,1,0:T(8,128)(2,1)} %get-tuple-element, ...), custom_call_target="tpu_custom_call" | custom-call | tf_op jit(solution)/shard_map/pallas_call | solution.py:1112
